TPU v7x, 128 devices: a whole 4x4x4 slice. The times are simulated.
128 devices in a mesh: space: 8 (over y_lo, z), tm: 16 (over y_hi, x, core).
Axes of the slice: x: 4, y: 4 (y_hi: 2, y_lo: 2; y = y_hi * 2 + y_lo), z: 4, core: 2. Of those that a mesh axis runs over, the one named last changes fastest.
Arguments:
- coefficients: float32 [2048, 8192], P('tm', 'space'), may hold values from -6 to 6
- counts: int32 [2048, 8192], P('tm', 'space'), may hold values from 0 to 2
- coords: float32 [2, 8192], replicated, may hold values from 0 to 12
- pattern: int32 [64, 8], replicated, may hold values from 0 to 63, as said below
- temporal_taps: float32 [9], replicated, may hold values from 0.05 to 0.35
Outputs:
- newton_step: float32 [2048, 8192], P('tm', 'space')
- residual: float32 [2048, 8192], P('tm', 'space')
Inputs may be any that keep to these rules, and one draw needn't show every extreme that they name: `pattern`: each row lists 8 distinct block indices including the row's own index, and block j appears in row i exactly when block i appears in row j.
All inputs are finite; a program needn't handle non-finite values.
Results may differ from a plain program's by a relative error of at most 0.00016.
Values sent between devices are 32-bit elements; how exact they have to be, the bound alone decides.
A program may use at most 64 MiB of HBM per device.

v0:
```python
import functools

import jax
import jax.numpy as jnp
from jax import lax
from jax.experimental import pallas as pl
from jax.experimental.pallas import tpu as pltpu
from jax.sharding import PartitionSpec as P

BLOCK = 128
BW = 8
ITERS = 2


support = 0.25
amplitude = 0.2


def wendland(distance):
    scaled = distance / support
    remain = jnp.maximum(1.0 - scaled, 0.0)
    return amplitude * remain**4 * (1.0 + 4.0 * scaled)


def spatial_weights(coords, pattern):
    blocks = pattern.shape[0]
    located = coords.reshape(2, blocks, BLOCK)
    row_coords = located[:, :, None, None, :]
    col_coords = located[:, pattern][:, :, :, :, None]
    delta_x = row_coords[0] - col_coords[0]
    delta_y = row_coords[1] - col_coords[1]
    weight = wendland(jnp.sqrt(delta_x * delta_x + delta_y * delta_y))
    return weight.reshape(blocks, pattern.shape[1] * BLOCK, BLOCK)


def day_order_halo(field):
    spaces, times = lax.axis_size("space"), lax.axis_size("tm")
    place = [(rank % spaces) * times + rank // spaces for rank in range(spaces * times)]
    forward = [(place[i], place[i + 1]) for i in range(len(place) - 1)]
    backward = [(place[i + 1], place[i]) for i in range(len(place) - 1)]
    axes = ("space", "tm")
    low = lax.ppermute(field[field.shape[0] - BW :], axes, forward)
    high = lax.ppermute(field[:BW], axes, backward)
    return jnp.concatenate([low, field, high], axis=0)


def band_product(field, temporal_taps):
    length = field.shape[0]
    padded = day_order_halo(field)
    summed = temporal_taps[0] * field
    for offset in range(1, BW + 1):
        summed = summed + temporal_taps[offset] * (
            padded[BW - offset : BW - offset + length] + padded[BW + offset : BW + offset + length]
        )
    return summed


def block_product(field, weights, pattern):
    day_count = field.shape[0]
    blocks = pattern.shape[0]
    blocked = field.reshape(day_count, blocks, BLOCK)
    picked = blocked[:, pattern].reshape(day_count, blocks, pattern.shape[1] * BLOCK)
    out = jnp.einsum("rkc,drk->drc", weights, picked, precision=lax.Precision.HIGH)
    return out.reshape(day_count, blocks * BLOCK)


def to_days(field):
    n = lax.axis_size("space")
    k, days, cells = field.shape
    chunked = field.reshape(k, n, days // n, cells).transpose(1, 0, 2, 3)
    got = lax.all_to_all(chunked, "space", split_axis=0, concat_axis=0, tiled=True)
    return got.transpose(1, 2, 0, 3).reshape(k, days // n, n * cells)


def to_cells(field):
    n = lax.axis_size("space")
    k, days, cells = field.shape
    chunked = field.reshape(k, days, n, cells // n).transpose(2, 0, 1, 3)
    got = lax.all_to_all(chunked, "space", split_axis=0, concat_axis=0, tiled=True)
    return got.transpose(1, 0, 2, 3).reshape(k, n * days, cells // n)


def group_sum_kernel(axis, x_ref, o_ref, slots, send, recv):
    n = slots.shape[0]
    me = lax.axis_index(axis)

    def peer(index):
        return {axis: index}

    barrier = pltpu.get_barrier_semaphore()
    for k in range(1, n):
        pl.semaphore_signal(barrier, 1, device_id=peer(lax.rem(me + k, n)), device_id_type=pl.DeviceIdType.MESH)
    pl.semaphore_wait(barrier, n - 1)
    copies = []
    for k in range(1, n):
        target = lax.rem(me + k, n)
        copy = pltpu.make_async_remote_copy(
            src_ref=x_ref,
            dst_ref=slots.at[me],
            send_sem=send.at[target],
            recv_sem=recv.at[me],
            device_id=peer(target),
            device_id_type=pl.DeviceIdType.MESH,
        )
        copy.start()
        copies.append(copy)
    slots[me] = x_ref[...]
    for k in range(1, n):
        source = lax.rem(me - k + n, n)
        pltpu.make_async_remote_copy(
            src_ref=x_ref,
            dst_ref=slots.at[source],
            send_sem=send.at[source],
            recv_sem=recv.at[source],
            device_id=peer(source),
            device_id_type=pl.DeviceIdType.MESH,
        ).wait_recv()
    for copy in copies:
        copy.wait_send()
    acc = slots[0]
    for j in range(1, n):
        acc = acc + slots[j]
    o_ref[...] = acc


def group_sum(tile, axis, collective_id):
    n = lax.axis_size(axis)
    return pl.pallas_call(
        functools.partial(group_sum_kernel, axis),
        out_shape=jax.ShapeDtypeStruct(tile.shape, tile.dtype),
        in_specs=[pl.BlockSpec(memory_space=pltpu.VMEM)],
        out_specs=pl.BlockSpec(memory_space=pltpu.VMEM),
        scratch_shapes=[
            pltpu.VMEM((n,) + tile.shape, tile.dtype),
            pltpu.SemaphoreType.DMA((n,)),
            pltpu.SemaphoreType.DMA((n,)),
        ],
        compiler_params=pltpu.CompilerParams(collective_id=collective_id, has_side_effects=True),
    )(tile)


def total(values):
    tile = jnp.zeros((8, 128), jnp.float32) + jnp.stack(values + [values[0]] * (8 - len(values)))[:, None]
    tile = group_sum(group_sum(tile, "space", 0), "tm", 1)
    return [tile[i, 0] for i in range(len(values))]


def shards(coefficients, counts, coords, pattern, temporal_taps):
    weights = lax.optimization_barrier(spatial_weights(coords, pattern))

    def spread(field):
        return block_product(band_product(field, temporal_taps), weights, pattern)

    both = to_days(jnp.stack([coefficients, counts.astype(jnp.float32)]))
    coef, cnt = both[0], both[1]
    latent = spread(coef)
    intensity = jnp.exp(latent)
    gradient = coef + spread(intensity - cnt)
    residual = -gradient
    direction = residual
    newton_step = jnp.zeros_like(residual)
    norm_part = jnp.sum(residual * residual)
    norm_now = None
    for iteration in range(ITERS):
        image = spread(direction)
        weighted = intensity * image
        curv_part = jnp.sum(direction * direction) + jnp.sum(weighted * image)
        if norm_now is None:
            norm_now, curvature = total([norm_part, curv_part])
        else:
            (curvature,) = total([curv_part])
        curved = direction + spread(weighted)
        step_size = norm_now / curvature
        newton_step = newton_step + step_size * direction
        residual = residual - step_size * curved
        if iteration + 1 < ITERS:
            (norm_next,) = total([jnp.sum(residual * residual)])
            direction = residual + norm_next / norm_now * direction
            norm_now = norm_next
    out = to_cells(jnp.stack([newton_step, residual]))
    return (out[0], out[1])


def solution(mesh):
    placed = (P("tm", "space"), P("tm", "space"), P(), P(), P())
    return jax.shard_map(
        shards,
        mesh=mesh,
        in_specs=placed,
        out_specs=(P("tm", "space"), P("tm", "space")),
        check_vma=False,
    )
```

profile of v0, /device:TPU:0, one launch (start us, length us, event | category | flops | bytes accessed | tf_op | source)
XLA Modules:
  0.0 375.5 jit_solution(8830553530222770917)
XLA Ops:
  4.0 6.4 %all-to-all-start = ((f32[8,2,16,1024]{3,2,1,0:T(8,128)}), f32[8,2,16,1024]{3,2,1,0:T(8,128)S(1)}, u32[]{:S(2)}, u32[]{:S(2)}) async-start(f32[8,2,16,1024]{3,2,1,0:T(8,128)} %copy.48), calls=%async_computation | async-start | bytes 2097152 | tf_op jit(solution)/shard_map/all_to_all | solution.py:71
  10.7 2.1 gather_fusion.1
  12.8 1.4 slice_reduce_fusion.1
  14.3 26.8 %add_multiply_fusion = f32[64,1024,128]{2,1,0:T(8,128)} fusion(f32[64,1024]{1,0:T(8,128)S(1)} %get-tuple-element.43, f32[64,128]{1,0:T(8,128)S(1)} %bitcast.219, f32[64,1024]{1,0:T(8,128)S(1)} %get-tuple-element.44, f32[64,128]{1,0:T(8,128)S(1)} %bitcast.218), kind=kLoop, calls=%fused_computation.7 | loop fusion | flops 117440512 | bytes 34144256 | tf_op jit(solution)/shard_map/mul | solution.py:22
  42.6 3.9 %collective-permute-start = (f32[8,8192]{1,0:T(8,128)S(1)}, f32[8,8192]{1,0:T(8,128)S(1)}, u32[]{:S(2)}, u32[]{:S(2)}) collective-permute-start(f32[8,8192]{1,0:T(8,128)S(1)} %bitcast.216), channel_id=1, source_target_pairs={{0,16},{16,32},{32,48},{48,64},{64,80},{80,96},{96,112},{112,1},{1... | collective-permute-start | bytes 786440 | tf_op jit(solution)/shard_map/ppermute | solution.py:42
  47.4 1.3 collective-permute-start.1
  48.7 2.8 collective-permute-done
  51.6 4.9 %collective-permute-done.1 = f32[8,8192]{1,0:T(8,128)S(1)} collective-permute-done((f32[8,8192]{1,0:T(8,128)S(1)}, f32[8,8192]{1,0:T(8,128)S(1)}, u32[]{:S(2)}, u32[]{:S(2)}) %collective-permute-start.1) | collective-permute-done | bytes 262176 | tf_op jit(solution)/shard_map/ppermute | solution.py:43
  56.5 6.5 %copy_bitcast_fusion.7 = f32[16,64,128]{2,0,1:T(8,128)S(1)} fusion(f32[24,8192]{1,0:T(8,128)S(1)} %constant_dynamic-update-slice_fusion.2, f32[24,8192]{1,0:T(8,128)S(1)} %get-tuple-element.24, f32[16,8192]{1,0:T(8,128)S(1)} %bitcast.200, f32[]{:T(128)} %bitcast.12, f32[]{:T(128)} %bitcast.11, f32[]{:T(128)} %bitcast.10, f32[]{:T(128)} %bitcast.9, ...), kind=kLoop, calls=%fused_computation.375 | loop fusion | flops 3276800 | bytes 9437220 | tf_op jit(solution)/shard_map/reshape | solution.py:61
  63.0 3.2 gather_fusion
  66.2 15.0 %fusion.18 = f32[64,16,128]{2,1,0:T(8,128)S(1)} fusion(f32[64,1024,128]{2,1,0:T(8,128)} %add_multiply_fusion, f32[64,8,2,8,128]{4,3,2,1,0:T(8,128)} %bitcast.193), kind=kOutput, calls=%fused_computation.166 | convolution fusion | flops 805306368 | bytes 38273024 | tf_op jit(solution)/shard_map/rkc,drk->drc/dot_general | solution.py:63
  81.4 1.3 collective-permute-start.3
  82.7 4.7 %collective-permute-start.2 = (f32[8,8192]{1,0:T(8,128)S(1)}, f32[8,8192]{1,0:T(8,128)S(1)}, u32[]{:S(2)}, u32[]{:S(2)}) collective-permute-start(f32[8,8192]{1,0:T(8,128)S(1)} %get-tuple-element.22), channel_id=1, source_target_pairs={{0,16},{16,32},{32,48},{48,64},{64,80},{80,96},{96,112},{112,1},{1... | collective-permute-start | bytes 786440 | tf_op jit(solution)/shard_map/ppermute | solution.py:42
  87.4 4.8 %collective-permute-done.3 = f32[8,8192]{1,0:T(8,128)S(1)} collective-permute-done((f32[8,8192]{1,0:T(8,128)S(1)}, f32[8,8192]{1,0:T(8,128)S(1)}, u32[]{:S(2)}, u32[]{:S(2)}) %collective-permute-start.3) | collective-permute-done | bytes 262176 | tf_op jit(solution)/shard_map/ppermute | solution.py:43
  92.2 6.9 %copy_bitcast_fusion.6 = f32[16,64,128]{2,0,1:T(8,128)S(1)} fusion(f32[16,8192]{1,0:T(8,128)S(1)} %bitcast_subtract_fusion, f32[8,8192]{1,0:T(8,128)S(1)} %collective-permute-done.3, f32[8,8192]{1,0:T(8,128)S(1)} %collective-permute-done.2, f32[]{:T(128)} %bitcast.12, f32[]{:T(128)} %bitcast.11, f32[]{:T(128)} %bitcast.10, f32[]{:T(128)} %bitcast.9, ...), kind=kLoop, calls=%fused_computation.374 | loop fusion | flops 5373952 | bytes 1572900 | tf_op jit(solution)/shard_map/reshape | solution.py:61
  99.2 3.2 gather_fusion.2
  102.4 15.0 %fusion.12 = f32[64,16,128]{2,1,0:T(8,128)S(1)} fusion(f32[64,1024,128]{2,1,0:T(8,128)} %add_multiply_fusion, f32[64,8,2,8,128]{4,3,2,1,0:T(8,128)} %bitcast.194), kind=kOutput, calls=%fused_computation.20 | convolution fusion | flops 805306368 | bytes 38273024 | tf_op jit(solution)/shard_map/rkc,drk->drc/dot_general | solution.py:63
  119.6 5.2 %collective-permute-start.4 = (f32[8,8192]{1,0:T(8,128)}, f32[8,8192]{1,0:T(8,128)}, u32[]{:S(2)}, u32[]{:S(2)}) collective-permute-start(f32[8,8192]{1,0:T(8,128)} %get-tuple-element.20), channel_id=1, source_target_pairs={{0,16},{16,32},{32,48},{48,64},{64,80},{80,96},{96,112},{112,1},{1... | collective-permute-start | bytes 786440 | tf_op jit(solution)/shard_map/ppermute | solution.py:42
  126.8 1.6 collective-permute-done.4
  128.3 8.8 %copy_bitcast_fusion.5 = f32[16,64,128]{2,0,1:T(8,128)S(1)} fusion(f32[16,8192]{1,0:T(8,128)S(1)} %fusion.214, f32[8,8192]{1,0:T(8,128)S(1)} %collective-permute-done.5, f32[8,8192]{1,0:T(8,128)} %collective-permute-done.4, f32[]{:T(128)} %bitcast.12, f32[]{:T(128)} %bitcast.11, f32[]{:T(128)} %bitcast.10, f32[]{:T(128)} %bitcast.9, f32[]{:T(128)} %bitcast.8, ...), kind=kLoop, calls=%fused_computation.373 | loop fusion | flops 5373952 | bytes 1572900 | tf_op jit(solution)/shard_map/reshape | solution.py:61
  137.1 3.2 gather_fusion.3
  140.3 16.0 %fusion.24 = (f32[]{:T(128)}, f32[64,16,128]{2,1,0:T(8,128)S(1)}) fusion(f32[64,16,128]{2,1,0:T(8,128)S(1)} %fusion.18, f32[64,1024,128]{2,1,0:T(8,128)} %add_multiply_fusion, f32[64,8,2,8,128]{4,3,2,1,0:T(8,128)} %bitcast.190), kind=kOutput, calls=%fused_computation.174 | convolution fusion | flops 805699584 | bytes 38797316 | tf_op jit(solution)/shard_map/rkc,drk->drc/dot_general | solution.py:63
  158.6 5.9 %collective-permute-start.6 = (f32[8,8192]{1,0:T(8,128)}, f32[8,8192]{1,0:T(8,128)}, u32[]{:S(2)}, u32[]{:S(2)}) collective-permute-start(f32[8,8192]{1,0:T(8,128)} %get-tuple-element.18), channel_id=1, source_target_pairs={{0,16},{16,32},{32,48},{48,64},{64,80},{80,96},{96,112},{112,1},{1... | collective-permute-start | bytes 786440 | tf_op jit(solution)/shard_map/ppermute | solution.py:42
  164.5 1.9 multiply_reduce_fusion.2
  167.6 4.5 %stack.19 = f32[8]{0:T(128)S(1)} concatenate(f32[1]{0:T(128)} %bitcast.25, f32[1]{0:T(128)} %bitcast.29, f32[1]{0:T(128)} %bitcast.25, f32[1]{0:T(128)} %bitcast.25, f32[1]{0:T(128)} %bitcast.25, f32[1]{0:T(128)} %bitcast.25, f32[1]{0:T(128)} %bitcast.25, f32[1]{0:T(128)} %bitcast.25), dimensions={0} | concatenate | bytes 64 | tf_op jit(solution)/shard_map/stack | solution.py:143
  172.8 15.4 %shard_map.68.x_ref = f32[8,128]{1,0:T(8,128)} custom-call(f32[8,128]{1,0:T(8,128)} %add.423.x_ref), custom_call_target="tpu_custom_call" | custom-call | tf_op jit(solution)/shard_map/pallas_call | solution.py:128
  188.2 14.1 %shard_map.69 = f32[8,128]{1,0:T(8,128)} custom-call(f32[8,128]{1,0:T(8,128)} %shard_map.68.x_ref), custom_call_target="tpu_custom_call" | custom-call | tf_op jit(solution)/shard_map/pallas_call | solution.py:128
  202.3 1.3 fusion.250
  205.0 12.7 %copy_bitcast_fusion.4 = f32[16,64,128]{2,0,1:T(8,128)S(1)} fusion(f32[16,8192]{1,0:T(8,128)} %copy-done.1, f32[8,8192]{1,0:T(8,128)S(1)} %collective-permute-done.7, f32[8,8192]{1,0:T(8,128)} %collective-permute-done.6, f32[]{:T(128)} %bitcast.12, f32[]{:T(128)} %bitcast.11, f32[]{:T(128)} %bitcast.10, f32[]{:T(128)} %bitcast.9, f32[]{:T(128)} %bitcast.8, ...), kind=kLoop, calls=%fused_computation.372 | loop fusion | flops 5373952 | bytes 1572900 | tf_op jit(solution)/shard_map/reshape | solution.py:61
  217.7 3.2 gather_fusion.4
  220.9 15.0 %fusion.6 = f32[64,16,128]{2,1,0:T(8,128)S(1)} fusion(f32[64,1024,128]{2,1,0:T(8,128)} %add_multiply_fusion, f32[64,8,2,8,128]{4,3,2,1,0:T(8,128)} %bitcast.195), kind=kOutput, calls=%fused_computation.14 | convolution fusion | flops 805306368 | bytes 38273024 | tf_op jit(solution)/shard_map/rkc,drk->drc/dot_general | solution.py:63
  238.2 7.4 %shard_map.70.x_ref = f32[8,128]{1,0:T(8,128)} custom-call(f32[8,128]{1,0:T(8,128)} %add.441.x_ref), custom_call_target="tpu_custom_call" | custom-call | tf_op jit(solution)/shard_map/pallas_call | solution.py:128
  245.7 9.3 %shard_map.71 = f32[8,128]{1,0:T(8,128)} custom-call(f32[8,128]{1,0:T(8,128)} %shard_map.70.x_ref), custom_call_target="tpu_custom_call" | custom-call | tf_op jit(solution)/shard_map/pallas_call | solution.py:128
  257.6 1.3 collective-permute-start.9
  258.9 4.6 %collective-permute-start.8 = (f32[8,8192]{1,0:T(8,128)S(1)}, f32[8,8192]{1,0:T(8,128)S(1)}, u32[]{:S(2)}, u32[]{:S(2)}) collective-permute-start(f32[8,8192]{1,0:T(8,128)S(1)} %get-tuple-element.16), channel_id=1, source_target_pairs={{0,16},{16,32},{32,48},{48,64},{64,80},{80,96},{96,112},{112,1},{1... | collective-permute-start | bytes 786440 | tf_op jit(solution)/shard_map/ppermute | solution.py:42
  263.5 4.3 %collective-permute-done.9 = f32[8,8192]{1,0:T(8,128)S(1)} collective-permute-done((f32[8,8192]{1,0:T(8,128)S(1)}, f32[8,8192]{1,0:T(8,128)S(1)}, u32[]{:S(2)}, u32[]{:S(2)}) %collective-permute-start.9) | collective-permute-done | bytes 262176 | tf_op jit(solution)/shard_map/ppermute | solution.py:43
  267.9 2.1 collective-permute-done.8
  269.9 6.9 %copy_bitcast_fusion.3 = f32[16,64,128]{2,0,1:T(8,128)S(1)} fusion(f32[16,8192]{1,0:T(8,128)S(1)} %fusion.213, f32[8,8192]{1,0:T(8,128)S(1)} %collective-permute-done.9, f32[8,8192]{1,0:T(8,128)S(1)} %collective-permute-done.8, f32[]{:T(128)} %bitcast.12, f32[]{:T(128)} %bitcast.11, f32[]{:T(128)} %bitcast.10, f32[]{:T(128)} %bitcast.9, f32[]{:T(128)} %bitcast.8, ...), kind=kLoop, calls=%fused_computation.371 | loop fusion | flops 5373952 | bytes 1572900 | tf_op jit(solution)/shard_map/reshape | solution.py:61
  276.9 3.2 gather_fusion.5
  280.1 16.1 %fusion.25 = (f32[]{:T(128)}, f32[64,16,128]{2,1,0:T(8,128)S(1)}) fusion(f32[64,16,128]{2,1,0:T(8,128)S(1)} %fusion.18, f32[64,1024,128]{2,1,0:T(8,128)} %add_multiply_fusion, f32[64,8,2,8,128]{4,3,2,1,0:T(8,128)} %bitcast.191), kind=kOutput, calls=%fused_computation.175 | convolution fusion | flops 805699584 | bytes 38797316 | tf_op jit(solution)/shard_map/rkc,drk->drc/dot_general | solution.py:63
  296.2 1.3 collective-permute-start.11
  297.5 5.3 %collective-permute-start.10 = (f32[8,8192]{1,0:T(8,128)S(1)}, f32[8,8192]{1,0:T(8,128)S(1)}, u32[]{:S(2)}, u32[]{:S(2)}) collective-permute-start(f32[8,8192]{1,0:T(8,128)S(1)} %get-tuple-element.14), channel_id=1, source_target_pairs={{0,16},{16,32},{32,48},{48,64},{64,80},{80,96},{96,112},{112,1},{1... | collective-permute-start | bytes 786440 | tf_op jit(solution)/shard_map/ppermute | solution.py:42
  305.5 10.2 %shard_map.72.x_ref = f32[8,128]{1,0:T(8,128)} custom-call(f32[8,128]{1,0:T(8,128)} %add.462.x_ref), custom_call_target="tpu_custom_call" | custom-call | tf_op jit(solution)/shard_map/pallas_call | solution.py:128
  315.6 10.5 %shard_map.73 = f32[8,128]{1,0:T(8,128)} custom-call(f32[8,128]{1,0:T(8,128)} %shard_map.72.x_ref), custom_call_target="tpu_custom_call" | custom-call | tf_op jit(solution)/shard_map/pallas_call | solution.py:128
  328.7 6.9 %copy_bitcast_fusion.2 = f32[16,64,128]{2,0,1:T(8,128)S(1)} fusion(f32[16,8192]{1,0:T(8,128)S(1)} %bitcast_multiply_fusion, f32[8,8192]{1,0:T(8,128)S(1)} %collective-permute-done.11, f32[8,8192]{1,0:T(8,128)S(1)} %collective-permute-done.10, f32[]{:T(128)} %bitcast.12, f32[]{:T(128)} %bitcast.11, f32[]{:T(128)} %bitcast.10, f32[]{:T(128)} %bitcast.9, ...), kind=kLoop, calls=%fused_computation.370 | loop fusion | flops 5373952 | bytes 1572900 | tf_op jit(solution)/shard_map/reshape | solution.py:61
  335.7 3.2 gather_fusion.6
  338.8 15.0 %fusion.21 = f32[16,64,128]{2,0,1:T(8,128)S(1)} fusion(f32[64,1024,128]{2,1,0:T(8,128)} %add_multiply_fusion, f32[64,8,2,8,128]{4,3,2,1,0:T(8,128)} %bitcast.192), kind=kOutput, calls=%fused_computation.167 | convolution fusion | flops 805306368 | bytes 38273024 | tf_op jit(solution)/shard_map/rkc,drk->drc/dot_general | solution.py:63
  355.1 19.2 %all_to_all.10 = f32[8,2,16,1024]{3,2,1,0:T(8,128)S(1)} all-to-all(f32[8,2,16,1024]{3,2,1,0:T(8,128)S(1)} %copy.77), channel_id=1, replica_groups=mesh['space'=8,'tm'=16] {'space'}, dimensions={0} | all-to-all | bytes 2097152 | tf_op jit(solution)/shard_map/all_to_all | solution.py:79
  (65 shorter events, 21.8 us)
Async XLA Ops:
  0.6 9.8 %copy-start.3 = (s32[64,8]{0,1:T(8,128)S(1)}, s32[64,8]{0,1:T(8,128)}, u32[]{:S(2)}) copy-start(s32[64,8]{0,1:T(8,128)} %param.8) | copy-start | bytes 6148
  0.6 10.0 %copy-start = (f32[2,8192]{1,0:T(2,128)S(1)}, f32[2,8192]{1,0:T(2,128)}, u32[]{:S(2)}) copy-start(f32[2,8192]{1,0:T(2,128)} %param.7) | copy-start | bytes 196612
  4.0 37.8 %all-to-all-start = ((f32[8,2,16,1024]{3,2,1,0:T(8,128)}), f32[8,2,16,1024]{3,2,1,0:T(8,128)S(1)}, u32[]{:S(2)}, u32[]{:S(2)}) async-start(f32[8,2,16,1024]{3,2,1,0:T(8,128)} %copy.48), calls=%async_computation | async-start | bytes 2097152 | tf_op jit(solution)/shard_map/all_to_all | solution.py:71
  14.3 26.8 %copy-start.2 = (f32[9]{0:T(128)S(1)}, f32[9]{0:T(128)}, u32[]{:S(2)}) copy-start(f32[9]{0:T(128)} %param.9) | copy-start | bytes 112
  42.6 8.9 %collective-permute-start = (f32[8,8192]{1,0:T(8,128)S(1)}, f32[8,8192]{1,0:T(8,128)S(1)}, u32[]{:S(2)}, u32[]{:S(2)}) collective-permute-start(f32[8,8192]{1,0:T(8,128)S(1)} %bitcast.216), channel_id=1, source_target_pairs={{0,16},{16,32},{32,48},{48,64},{64,80},{80,96},{96,112},{112,1},{1... | collective-permute-start | bytes 786440 | tf_op jit(solution)/shard_map/ppermute | solution.py:42
  47.4 9.1 %collective-permute-start.1 = (f32[8,8192]{1,0:T(8,128)S(1)}, f32[8,8192]{1,0:T(8,128)S(1)}, u32[]{:S(2)}, u32[]{:S(2)}) collective-permute-start(f32[8,8192]{1,0:T(8,128)S(1)} %bitcast.217), channel_id=1, source_target_pairs={{16,0},{32,16},{48,32},{64,48},{80,64},{96,80},{112,96},{1,112},{1... | collective-permute-start | bytes 786440 | tf_op jit(solution)/shard_map/ppermute | solution.py:43
  81.4 10.9 %collective-permute-start.3 = (f32[8,8192]{1,0:T(8,128)S(1)}, f32[8,8192]{1,0:T(8,128)S(1)}, u32[]{:S(2)}, u32[]{:S(2)}) collective-permute-start(f32[8,8192]{1,0:T(8,128)S(1)} %get-tuple-element.23), channel_id=1, source_target_pairs={{16,0},{32,16},{48,32},{64,48},{80,64},{96,80},{112,96},{1,112},{1... | collective-permute-start | bytes 786440 | tf_op jit(solution)/shard_map/ppermute | solution.py:43
  82.7 9.6 %collective-permute-start.2 = (f32[8,8192]{1,0:T(8,128)S(1)}, f32[8,8192]{1,0:T(8,128)S(1)}, u32[]{:S(2)}, u32[]{:S(2)}) collective-permute-start(f32[8,8192]{1,0:T(8,128)S(1)} %get-tuple-element.22), channel_id=1, source_target_pairs={{0,16},{16,32},{32,48},{48,64},{64,80},{80,96},{96,112},{112,1},{1... | collective-permute-start | bytes 786440 | tf_op jit(solution)/shard_map/ppermute | solution.py:42
  118.3 8.5 %collective-permute-start.5 = (f32[8,8192]{1,0:T(8,128)}, f32[8,8192]{1,0:T(8,128)S(1)}, u32[]{:S(2)}, u32[]{:S(2)}) collective-permute-start(f32[8,8192]{1,0:T(8,128)} %get-tuple-element.21), channel_id=1, source_target_pairs={{16,0},{32,16},{48,32},{64,48},{80,64},{96,80},{112,96},{1,112},{1... | collective-permute-start | bytes 786440 | tf_op jit(solution)/shard_map/ppermute | solution.py:43
  119.6 8.7 %collective-permute-start.4 = (f32[8,8192]{1,0:T(8,128)}, f32[8,8192]{1,0:T(8,128)}, u32[]{:S(2)}, u32[]{:S(2)}) collective-permute-start(f32[8,8192]{1,0:T(8,128)} %get-tuple-element.20), channel_id=1, source_target_pairs={{0,16},{16,32},{32,48},{48,64},{64,80},{80,96},{96,112},{112,1},{1... | collective-permute-start | bytes 786440 | tf_op jit(solution)/shard_map/ppermute | solution.py:42
  156.4 48.6 %copy-start.1 = (f32[16,8192]{1,0:T(8,128)}, f32[16,8192]{1,0:T(8,128)S(1)}, u32[]{:S(2)}) copy-start(f32[16,8192]{1,0:T(8,128)S(1)} %bitcast_multiply_fusion.1) | copy-start | bytes 1572868
  157.3 47.7 %collective-permute-start.7 = (f32[8,8192]{1,0:T(8,128)}, f32[8,8192]{1,0:T(8,128)S(1)}, u32[]{:S(2)}, u32[]{:S(2)}) collective-permute-start(f32[8,8192]{1,0:T(8,128)} %get-tuple-element.19), channel_id=1, source_target_pairs={{16,0},{32,16},{48,32},{64,48},{80,64},{96,80},{112,96},{1,112},{1... | collective-permute-start | bytes 786440 | tf_op jit(solution)/shard_map/ppermute | solution.py:43
  158.6 46.4 %collective-permute-start.6 = (f32[8,8192]{1,0:T(8,128)}, f32[8,8192]{1,0:T(8,128)}, u32[]{:S(2)}, u32[]{:S(2)}) collective-permute-start(f32[8,8192]{1,0:T(8,128)} %get-tuple-element.18), channel_id=1, source_target_pairs={{0,16},{16,32},{32,48},{48,64},{64,80},{80,96},{96,112},{112,1},{1... | collective-permute-start | bytes 786440 | tf_op jit(solution)/shard_map/ppermute | solution.py:42
  257.6 10.2 %collective-permute-start.9 = (f32[8,8192]{1,0:T(8,128)S(1)}, f32[8,8192]{1,0:T(8,128)S(1)}, u32[]{:S(2)}, u32[]{:S(2)}) collective-permute-start(f32[8,8192]{1,0:T(8,128)S(1)} %get-tuple-element.17), channel_id=1, source_target_pairs={{16,0},{32,16},{48,32},{64,48},{80,64},{96,80},{112,96},{1,112},{1... | collective-permute-start | bytes 786440 | tf_op jit(solution)/shard_map/ppermute | solution.py:43
  258.9 11.0 %collective-permute-start.8 = (f32[8,8192]{1,0:T(8,128)S(1)}, f32[8,8192]{1,0:T(8,128)S(1)}, u32[]{:S(2)}, u32[]{:S(2)}) collective-permute-start(f32[8,8192]{1,0:T(8,128)S(1)} %get-tuple-element.16), channel_id=1, source_target_pairs={{0,16},{16,32},{32,48},{48,64},{64,80},{80,96},{96,112},{112,1},{1... | collective-permute-start | bytes 786440 | tf_op jit(solution)/shard_map/ppermute | solution.py:42
  296.2 32.5 %collective-permute-start.11 = (f32[8,8192]{1,0:T(8,128)S(1)}, f32[8,8192]{1,0:T(8,128)S(1)}, u32[]{:S(2)}, u32[]{:S(2)}) collective-permute-start(f32[8,8192]{1,0:T(8,128)S(1)} %get-tuple-element.15), channel_id=1, source_target_pairs={{16,0},{32,16},{48,32},{64,48},{80,64},{96,80},{112,96},{1,112},{1... | collective-permute-start | bytes 786440 | tf_op jit(solution)/shard_map/ppermute | solution.py:43
  297.5 31.2 %collective-permute-start.10 = (f32[8,8192]{1,0:T(8,128)S(1)}, f32[8,8192]{1,0:T(8,128)S(1)}, u32[]{:S(2)}, u32[]{:S(2)}) collective-permute-start(f32[8,8192]{1,0:T(8,128)S(1)} %get-tuple-element.14), channel_id=1, source_target_pairs={{0,16},{16,32},{32,48},{48,64},{64,80},{80,96},{96,112},{112,1},{1... | collective-permute-start | bytes 786440 | tf_op jit(solution)/shard_map/ppermute | solution.py:42
where the time goes:
time: 377 us; the launch traced here: 375 us
  matrix products  92.2 us (24%)
  other arithmetic  81.8 us (22%)
  Pallas kernels  67 us (18%)
  starting transfers between devices  43.9 us (12%)
  local copies, waits for them, and re-layouts  42.3 us (11%)
  waiting for transfers between devices  21.4 us (6%)
  blocking collectives  19.2 us (5%)
  between operations  7.68 us (2%)
    dot_general x6, matrix products, block_product(): jnp.einsum('rkc,drk->drc', weights, picked, precision=lax.Precision.HIGH)  92.2 us
    pallas_call x6, Pallas kernels, group_sum(): pl.pallas_call(functools.partial(group_sum_kernel, axis), out_shape=jax.S...  67 us
    reshape x6, other arithmetic, block_product(): blocked = field.reshape(day_count, blocks, BLOCK)  48.7 us
    ppermute x6, starting transfers between devices, day_order_halo(): low = lax.ppermute(field[field.shape[0] - BW:], axes, forward)  29.7 us
    mul x1, other arithmetic, wendland(): return amplitude * remain ** 4 * (1.0 + 4.0 * scaled)  26.8 us
    all_to_all x1, blocking collectives, to_cells(): lax.all_to_all(chunked, 'space', split_axis=0, concat_axis=0, tiled=True)  19.2 us
    gather x6, local copies, waits for them, and re-layouts, block_product(): blocked[:, pattern].reshape(day_count, blocks, pattern.shape[1] * BLOCK)  19.1 us
    ppermute x6, waiting for transfers between devices, day_order_halo(): high = lax.ppermute(field[:BW], axes, backward)  15 us
  transfers between devices with their start and end apart: 13, of which 7 were waited for; matrix products, arithmetic and copies ran while one was open for 12% of the time, Pallas kernels for 13%

commit v1 on v0

--- a/solution.py
+++ b/solution.py
@@ -9,7 +9,6 @@
 
 BLOCK = 128
 BW = 8
-ITERS = 2
 
 
 support = 0.25
@@ -44,9 +43,18 @@
     return jnp.concatenate([low, field, high], axis=0)
 
 
-def band_product(field, temporal_taps):
+def tm_halo(field):
+    count = lax.axis_size("tm")
+    forward = [(i, i + 1) for i in range(count - 1)]
+    backward = [(i + 1, i) for i in range(count - 1)]
+    low = lax.ppermute(field[field.shape[0] - BW :], "tm", forward)
+    high = lax.ppermute(field[:BW], "tm", backward)
+    return jnp.concatenate([low, field, high], axis=0)
+
+
+def band_product(field, temporal_taps, halo=None):
     length = field.shape[0]
-    padded = day_order_halo(field)
+    padded = (halo or day_order_halo)(field)
     summed = temporal_taps[0] * field
     for offset in range(1, BW + 1):
         summed = summed + temporal_taps[offset] * (
@@ -151,32 +159,31 @@
     def spread(field):
         return block_product(band_product(field, temporal_taps), weights, pattern)
 
-    both = to_days(jnp.stack([coefficients, counts.astype(jnp.float32)]))
-    coef, cnt = both[0], both[1]
-    latent = spread(coef)
+    banded = band_product(coefficients, temporal_taps, tm_halo)
+    moved = to_days(jnp.stack([coefficients, counts.astype(jnp.float32), banded]))
+    coef, cnt = moved[0], moved[1]
+    latent = block_product(moved[2], weights, pattern)
     intensity = jnp.exp(latent)
     gradient = coef + spread(intensity - cnt)
     residual = -gradient
     direction = residual
-    newton_step = jnp.zeros_like(residual)
-    norm_part = jnp.sum(residual * residual)
-    norm_now = None
-    for iteration in range(ITERS):
-        image = spread(direction)
-        weighted = intensity * image
-        curv_part = jnp.sum(direction * direction) + jnp.sum(weighted * image)
-        if norm_now is None:
-            norm_now, curvature = total([norm_part, curv_part])
-        else:
-            (curvature,) = total([curv_part])
-        curved = direction + spread(weighted)
-        step_size = norm_now / curvature
-        newton_step = newton_step + step_size * direction
-        residual = residual - step_size * curved
-        if iteration + 1 < ITERS:
-            (norm_next,) = total([jnp.sum(residual * residual)])
-            direction = residual + norm_next / norm_now * direction
-            norm_now = norm_next
+    image = spread(direction)
+    curved = direction + spread(intensity * image)
+    norm_now, curvature, curved_sq = total(
+        [jnp.sum(residual * residual), jnp.sum(direction * curved), jnp.sum(curved * curved)]
+    )
+    step_size = norm_now / curvature
+    newton_step = step_size * direction
+    residual = residual - step_size * curved
+    norm_next = step_size * step_size * curved_sq - norm_now
+    direction = residual + norm_next / norm_now * direction
+    norm_now = norm_next
+    image = spread(direction)
+    curved = direction + spread(intensity * image)
+    (curvature,) = total([jnp.sum(direction * curved)])
+    step_size = norm_now / curvature
+    newton_step = newton_step + step_size * direction
+    residual = residual - step_size * curved
     out = to_cells(jnp.stack([newton_step, residual]))
     return (out[0], out[1])
 

time: 377 us -> 373 us (0.989)
  Pallas kernels: 67 us -> 44 us
  waiting for transfers between devices: 21.4 us -> 40.2 us
  starting transfers between devices: 43.9 us -> 34.6 us
  local copies, waits for them, and re-layouts: 42.3 us -> 51.5 us
    pallas_call x6 -> x4, Pallas kernels: 67 us -> 44 us  [group_sum(): pl.pallas_call(functools.partial(group_sum_kernel, axis), out_shape=jax.S...]
    ppermute x6 -> x5, waiting for transfers between devices: 6.45 us -> 19 us  [day_order_halo(): low = lax.ppermute(field[field.shape[0] - BW:], axes, forward)]
    ppermute x6 -> x5, starting transfers between devices: 29.7 us -> 18 us  [day_order_halo(): low = lax.ppermute(field[field.shape[0] - BW:], axes, forward)]
    reshape x6 -> x5, other arithmetic: 48.7 us -> 40.8 us  [block_product(): blocked = field.reshape(day_count, blocks, BLOCK)]
    add x0 -> x1, other arithmetic: none -> 6.61 us  [band_product(): summed + temporal_taps[offset] * (padded[BW - offset:BW - offset + length...]
    ppermute x6 -> x5, waiting for transfers between devices: 15 us -> 21.2 us  [day_order_halo(): high = lax.ppermute(field[:BW], axes, backward)]
    ppermute x6 -> x5, starting transfers between devices: 7.73 us -> 7.12 us  [day_order_halo(): high = lax.ppermute(field[:BW], axes, backward)]
  transfers between devices with their start and end apart: 13 -> 13, of which waited for: 7 -> 10; matrix products, arithmetic and copies ran while one was open for 12% -> 10% of each run, Pallas kernels for 13% -> 0%
where the time goes in v1:
time: 373 us; the launch traced here: 371 us
  matrix products  93.2 us (25%)
  other arithmetic  82.2 us (22%)
  local copies, waits for them, and re-layouts  51.5 us (14%)
  Pallas kernels  44 us (12%)
  waiting for transfers between devices  40.2 us (11%)
  starting transfers between devices  34.6 us (9%)
  blocking collectives  20 us (5%)
  between operations  5.14 us (1%)
    dot_general x6, matrix products, block_product(): jnp.einsum('rkc,drk->drc', weights, picked, precision=lax.Precision.HIGH)  93.2 us
    pallas_call x4, Pallas kernels, group_sum(): pl.pallas_call(functools.partial(group_sum_kernel, axis), out_shape=jax.S...  44 us
    reshape x5, other arithmetic, block_product(): blocked = field.reshape(day_count, blocks, BLOCK)  40.8 us
    mul x1, other arithmetic, wendland(): return amplitude * remain ** 4 * (1.0 + 4.0 * scaled)  26.8 us
    ppermute x5, waiting for transfers between devices, day_order_halo(): high = lax.ppermute(field[:BW], axes, backward)  21.2 us
    all_to_all x1, blocking collectives, to_cells(): lax.all_to_all(chunked, 'space', split_axis=0, concat_axis=0, tiled=True)  20 us
    gather x6, local copies, waits for them, and re-layouts, block_product(): blocked[:, pattern].reshape(day_count, blocks, pattern.shape[1] * BLOCK)  19.2 us
    ppermute x5, waiting for transfers between devices, day_order_halo(): low = lax.ppermute(field[field.shape[0] - BW:], axes, forward)  19 us
  transfers between devices with their start and end apart: 13, of which 10 were waited for; matrix products, arithmetic and copies ran while one was open for 10% of the time, Pallas kernels for 0%

profile of v1, /device:TPU:0, one launch (start us, length us, event | category | flops | bytes accessed | tf_op | source)
XLA Modules:
  0.0 370.8 jit_solution(14566387961257694531)
XLA Ops:
  5.9 2.3 gather_fusion.1
  9.7 1.7 fusion.263
  12.7 6.6 %fusion.233 = f32[128,1024]{1,0:T(8,128)S(1)} fusion(f32[136,1024]{1,0:T(8,128)S(1)} %constant_dynamic-update-slice_fusion.2, f32[136,1024]{1,0:T(8,128)S(1)} %get-tuple-element.24, f32[128,1024]{1,0:T(8,128)S(1)} %copy-done.2, f32[]{:T(128)} %bitcast.10, f32[]{:T(128)} %bitcast.9, f32[]{:T(128)} %bitcast.8, f32[]{:T(128)} %bitcast.7, f32[]{:T(128)} %bitcast.6, ...), kind=kLoop, calls=%fused_computation.396 | loop fusion | flops 3276800 | bytes 9437220 | tf_op jit(solution)/shard_map/add | solution.py:60
  20.7 6.9 %all-to-all-start = ((f32[8,3,16,1024]{3,2,1,0:T(8,128)}), f32[8,3,16,1024]{3,2,1,0:T(8,128)}, u32[]{:S(2)}, u32[]{:S(2)}) async-start(f32[8,3,16,1024]{3,2,1,0:T(8,128)} %copy.53), calls=%async_computation | async-start | bytes 3145728 | tf_op jit(solution)/shard_map/all_to_all | solution.py:79
  27.6 26.8 %add_multiply_fusion = f32[64,1024,128]{2,1,0:T(8,128)} fusion(f32[64,1024]{1,0:T(8,128)S(1)} %get-tuple-element.44, f32[64,128]{1,0:T(8,128)S(1)} %bitcast.204, f32[64,1024]{1,0:T(8,128)S(1)} %get-tuple-element.45, f32[64,128]{1,0:T(8,128)S(1)} %bitcast.203), kind=kLoop, calls=%fused_computation.7 | loop fusion | flops 117440512 | bytes 34144256 | tf_op jit(solution)/shard_map/mul | solution.py:21
  54.4 2.3 copy.178
  58.1 3.2 gather_fusion
  61.6 15.1 %fusion.21 = f32[64,2,8,128]{3,2,1,0:T(8,128)S(1)} fusion(f32[64,1024,128]{2,1,0:T(8,128)} %add_multiply_fusion, f32[64,8,2,8,128]{4,3,2,1,0:T(8,128)} %bitcast.179), kind=kOutput, calls=%fused_computation.169 | convolution fusion | flops 805306368 | bytes 38273024 | tf_op jit(solution)/shard_map/rkc,drk->drc/dot_general | solution.py:71
  76.8 3.8 %collective-permute-start.2 = (f32[8,8192]{1,0:T(8,128)S(1)}, f32[8,8192]{1,0:T(8,128)S(1)}, u32[]{:S(2)}, u32[]{:S(2)}) collective-permute-start(f32[8,8192]{1,0:T(8,128)S(1)} %get-tuple-element.22), channel_id=1, source_target_pairs={{0,16},{16,32},{32,48},{48,64},{64,80},{80,96},{96,112},{112,1},{1... | collective-permute-start | bytes 786440 | tf_op jit(solution)/shard_map/ppermute | solution.py:41
  83.2 3.2 collective-permute-done.2
  86.4 4.7 %collective-permute-done.3 = f32[8,8192]{1,0:T(8,128)S(1)} collective-permute-done((f32[8,8192]{1,0:T(8,128)S(1)}, f32[8,8192]{1,0:T(8,128)S(1)}, u32[]{:S(2)}, u32[]{:S(2)}) %collective-permute-start.3) | collective-permute-done | bytes 262176 | tf_op jit(solution)/shard_map/ppermute | solution.py:42
  91.1 7.1 %copy_bitcast_fusion.6 = f32[16,64,128]{2,0,1:T(8,128)S(1)} fusion(f32[16,8192]{1,0:T(8,128)S(1)} %bitcast_subtract_fusion, f32[8,8192]{1,0:T(8,128)S(1)} %collective-permute-done.3, f32[8,8192]{1,0:T(8,128)S(1)} %collective-permute-done.2, f32[]{:T(128)} %bitcast.10, f32[]{:T(128)} %bitcast.9, f32[]{:T(128)} %bitcast.8, f32[]{:T(128)} %bitcast.7, ...), kind=kLoop, calls=%fused_computation.373 | loop fusion | flops 5373952 | bytes 1572900 | tf_op jit(solution)/shard_map/reshape | solution.py:69
  98.2 3.2 gather_fusion.2
  101.4 15.1 %fusion.12 = f32[64,16,128]{2,1,0:T(8,128)S(1)} fusion(f32[64,1024,128]{2,1,0:T(8,128)} %add_multiply_fusion, f32[64,8,2,8,128]{4,3,2,1,0:T(8,128)} %bitcast.181), kind=kOutput, calls=%fused_computation.20 | convolution fusion | flops 805306368 | bytes 38273024 | tf_op jit(solution)/shard_map/rkc,drk->drc/dot_general | solution.py:71
  116.7 3.4 collective-permute-start.4
  121.3 4.8 %collective-permute-done.4 = f32[8,8192]{1,0:T(8,128)S(1)} collective-permute-done((f32[8,8192]{1,0:T(8,128)S(1)}, f32[8,8192]{1,0:T(8,128)S(1)}, u32[]{:S(2)}, u32[]{:S(2)}) %collective-permute-start.4) | collective-permute-done | bytes 262176 | tf_op jit(solution)/shard_map/ppermute | solution.py:41
  126.1 4.1 %collective-permute-done.5 = f32[8,8192]{1,0:T(8,128)S(1)} collective-permute-done((f32[8,8192]{1,0:T(8,128)S(1)}, f32[8,8192]{1,0:T(8,128)S(1)}, u32[]{:S(2)}, u32[]{:S(2)}) %collective-permute-start.5) | collective-permute-done | bytes 262176 | tf_op jit(solution)/shard_map/ppermute | solution.py:42
  130.3 7.1 %copy_bitcast_fusion.5 = f32[16,64,128]{2,0,1:T(8,128)S(1)} fusion(f32[16,8192]{1,0:T(8,128)S(1)} %fusion.221, f32[8,8192]{1,0:T(8,128)S(1)} %collective-permute-done.5, f32[8,8192]{1,0:T(8,128)S(1)} %collective-permute-done.4, f32[]{:T(128)} %bitcast.10, f32[]{:T(128)} %bitcast.9, f32[]{:T(128)} %bitcast.8, f32[]{:T(128)} %bitcast.7, f32[]{:T(128)} %bitcast.6, ...), kind=kLoop, calls=%fused_computation.372 | loop fusion | flops 5373952 | bytes 1572900 | tf_op jit(solution)/shard_map/reshape | solution.py:69
  137.3 3.2 gather_fusion.3
  140.5 15.9 %fusion.24 = f32[64,2,8,128]{3,2,1,0:T(8,128)} fusion(f32[64,1024,128]{2,1,0:T(8,128)} %add_multiply_fusion, f32[64,8,2,8,128]{4,3,2,1,0:T(8,128)} %bitcast.182), kind=kOutput, calls=%fused_computation.170 | convolution fusion | flops 805306368 | bytes 38273024 | tf_op jit(solution)/shard_map/rkc,drk->drc/dot_general | solution.py:71
  159.2 4.9 %collective-permute-start.6 = (f32[8,8192]{1,0:T(8,128)}, f32[8,8192]{1,0:T(8,128)S(1)}, u32[]{:S(2)}, u32[]{:S(2)}) collective-permute-start(f32[8,8192]{1,0:T(8,128)} %get-tuple-element.18), channel_id=1, source_target_pairs={{0,16},{16,32},{32,48},{48,64},{64,80},{80,96},{96,112},{112,1},{1... | collective-permute-start | bytes 786440 | tf_op jit(solution)/shard_map/ppermute | solution.py:41
  164.2 1.5 collective-permute-start.7
  167.6 2.1 collective-permute-done.6
  169.7 4.1 %collective-permute-done.7 = f32[8,8192]{1,0:T(8,128)} collective-permute-done((f32[8,8192]{1,0:T(8,128)}, f32[8,8192]{1,0:T(8,128)}, u32[]{:S(2)}, u32[]{:S(2)}) %collective-permute-start.7) | collective-permute-done | bytes 262176 | tf_op jit(solution)/shard_map/ppermute | solution.py:42
  173.9 12.5 %copy_bitcast_fusion.4 = f32[16,64,128]{2,0,1:T(8,128)S(1)} fusion(f32[16,8192]{1,0:T(8,128)} %copy-done.3, f32[8,8192]{1,0:T(8,128)} %collective-permute-done.7, f32[8,8192]{1,0:T(8,128)S(1)} %collective-permute-done.6, f32[]{:T(128)} %bitcast.10, f32[]{:T(128)} %bitcast.9, f32[]{:T(128)} %bitcast.8, f32[]{:T(128)} %bitcast.7, f32[]{:T(128)} %bitcast.6, ...), kind=kLoop, calls=%fused_computation.371 | loop fusion | flops 5373952 | bytes 1572900 | tf_op jit(solution)/shard_map/reshape | solution.py:69
  186.3 3.2 gather_fusion.4
  189.5 17.0 %fusion.251 = (f32[]{:T(128)}, f32[64,16,128]{2,1,0:T(8,128)}) fusion(f32[16,64,128]{2,1,0:T(8,128)} %squeeze.47, f32[64,16,128]{2,1,0:T(8,128)S(1)} %fusion.12, f32[64,1024,128]{2,1,0:T(8,128)} %add_multiply_fusion, f32[64,8,2,8,128]{4,3,2,1,0:T(8,128)} %bitcast.184), kind=kOutput, calls=%fused_computation.422 | convolution fusion | flops 805961728 | bytes 39321604 | tf_op jit(solution)/shard_map/rkc,drk->drc/dot_general | solution.py:71
  206.5 2.1 copy.72
  209.7 2.6 multiply_reduce_fusion.1
  212.3 4.9 %stack.50 = f32[8]{0:T(128)S(1)} concatenate(f32[1]{0:T(128)} %bitcast.26, f32[1]{0:T(128)} %bitcast.33, f32[1]{0:T(128)} %bitcast.34, f32[1]{0:T(128)} %bitcast.26, f32[1]{0:T(128)} %bitcast.26, f32[1]{0:T(128)} %bitcast.26, f32[1]{0:T(128)} %bitcast.26, f32[1]{0:T(128)} %bitcast.26), dimensions={0} | concatenate | bytes 64 | tf_op jit(solution)/shard_map/stack | solution.py:151
  217.9 10.5 %shard_map.68.x_ref = f32[8,128]{1,0:T(8,128)} custom-call(f32[8,128]{1,0:T(8,128)} %add.437.x_ref), custom_call_target="tpu_custom_call" | custom-call | tf_op jit(solution)/shard_map/pallas_call | solution.py:136
  228.4 12.9 %shard_map.69 = f32[8,128]{1,0:T(8,128)} custom-call(f32[8,128]{1,0:T(8,128)} %shard_map.68.x_ref), custom_call_target="tpu_custom_call" | custom-call | tf_op jit(solution)/shard_map/pallas_call | solution.py:136
  247.2 2.5 collective-permute-start.8
  251.0 4.5 %collective-permute-done.8 = f32[8,8192]{1,0:T(8,128)S(1)} collective-permute-done((f32[8,8192]{1,0:T(8,128)S(1)}, f32[8,8192]{1,0:T(8,128)S(1)}, u32[]{:S(2)}, u32[]{:S(2)}) %collective-permute-start.8) | collective-permute-done | bytes 262176 | tf_op jit(solution)/shard_map/ppermute | solution.py:41
  255.5 4.1 %collective-permute-done.9 = f32[8,8192]{1,0:T(8,128)S(1)} collective-permute-done((f32[8,8192]{1,0:T(8,128)S(1)}, f32[8,8192]{1,0:T(8,128)S(1)}, u32[]{:S(2)}, u32[]{:S(2)}) %collective-permute-start.9) | collective-permute-done | bytes 262176 | tf_op jit(solution)/shard_map/ppermute | solution.py:42
  259.6 7.1 %copy_bitcast_fusion.3 = f32[16,64,128]{2,0,1:T(8,128)S(1)} fusion(f32[16,8192]{1,0:T(8,128)S(1)} %fusion.220, f32[8,8192]{1,0:T(8,128)S(1)} %collective-permute-done.9, f32[8,8192]{1,0:T(8,128)S(1)} %collective-permute-done.8, f32[]{:T(128)} %bitcast.10, f32[]{:T(128)} %bitcast.9, f32[]{:T(128)} %bitcast.8, f32[]{:T(128)} %bitcast.7, f32[]{:T(128)} %bitcast.6, ...), kind=kLoop, calls=%fused_computation.370 | loop fusion | flops 5373952 | bytes 1572900 | tf_op jit(solution)/shard_map/reshape | solution.py:69
  266.7 3.2 gather_fusion.5
  269.9 15.0 %fusion.27 = f32[64,2,8,128]{3,2,1,0:T(8,128)S(1)} fusion(f32[64,1024,128]{2,1,0:T(8,128)} %add_multiply_fusion, f32[64,8,2,8,128]{4,3,2,1,0:T(8,128)} %bitcast.183), kind=kOutput, calls=%fused_computation.171 | convolution fusion | flops 805306368 | bytes 38273024 | tf_op jit(solution)/shard_map/rkc,drk->drc/dot_general | solution.py:71
  285.0 3.4 collective-permute-start.10
  288.5 1.6 collective-permute-start.11
  290.0 4.4 %collective-permute-done.10 = f32[8,8192]{1,0:T(8,128)S(1)} collective-permute-done((f32[8,8192]{1,0:T(8,128)S(1)}, f32[8,8192]{1,0:T(8,128)S(1)}, u32[]{:S(2)}, u32[]{:S(2)}) %collective-permute-start.10) | collective-permute-done | bytes 262176 | tf_op jit(solution)/shard_map/ppermute | solution.py:41
  294.4 4.1 %collective-permute-done.11 = f32[8,8192]{1,0:T(8,128)S(1)} collective-permute-done((f32[8,8192]{1,0:T(8,128)S(1)}, f32[8,8192]{1,0:T(8,128)S(1)}, u32[]{:S(2)}, u32[]{:S(2)}) %collective-permute-start.11) | collective-permute-done | bytes 262176 | tf_op jit(solution)/shard_map/ppermute | solution.py:42
  298.6 7.1 %copy_bitcast_fusion.2 = f32[16,64,128]{2,0,1:T(8,128)S(1)} fusion(f32[16,8192]{1,0:T(8,128)S(1)} %bitcast_multiply_fusion, f32[8,8192]{1,0:T(8,128)S(1)} %collective-permute-done.11, f32[8,8192]{1,0:T(8,128)S(1)} %collective-permute-done.10, f32[]{:T(128)} %bitcast.10, f32[]{:T(128)} %bitcast.9, f32[]{:T(128)} %bitcast.8, f32[]{:T(128)} %bitcast.7, ...), kind=kLoop, calls=%fused_computation.369 | loop fusion | flops 5373952 | bytes 1572900 | tf_op jit(solution)/shard_map/reshape | solution.py:69
  305.6 3.2 gather_fusion.6
  308.9 15.1 %fusion.30 = f32[16,64,128]{2,0,1:T(8,128)S(1)} fusion(f32[64,1024,128]{2,1,0:T(8,128)} %add_multiply_fusion, f32[64,8,2,8,128]{4,3,2,1,0:T(8,128)} %bitcast.180), kind=kOutput, calls=%fused_computation.172 | convolution fusion | flops 805306368 | bytes 38273024 | tf_op jit(solution)/shard_map/rkc,drk->drc/dot_general | solution.py:71
  326.2 11.3 %shard_map.70.x_ref = f32[8,128]{1,0:T(8,128)} custom-call(f32[8,128]{1,0:T(8,128)} %add.474.x_ref), custom_call_target="tpu_custom_call" | custom-call | tf_op jit(solution)/shard_map/pallas_call | solution.py:136
  337.5 9.3 %shard_map.71 = f32[8,128]{1,0:T(8,128)} custom-call(f32[8,128]{1,0:T(8,128)} %shard_map.70.x_ref), custom_call_target="tpu_custom_call" | custom-call | tf_op jit(solution)/shard_map/pallas_call | solution.py:136
  349.6 20.0 %all_to_all.10 = f32[8,2,16,1024]{3,2,1,0:T(8,128)S(1)} all-to-all(f32[8,2,16,1024]{3,2,1,0:T(8,128)S(1)} %copy.83), channel_id=1, replica_groups=mesh['space'=8,'tm'=16] {'space'}, dimensions={0} | all-to-all | bytes 2097152 | tf_op jit(solution)/shard_map/all_to_all | solution.py:87
  (71 shorter events, 31.1 us)
Async XLA Ops:
  0.6 11.9 %copy-start.2 = (f32[128,1024]{1,0:T(8,128)S(1)}, f32[128,1024]{1,0:T(8,128)}, u32[]{:S(2)}) copy-start(f32[128,1024]{1,0:T(8,128)} %param.5) | copy-start | bytes 1572868
  1.5 11.0 %collective-permute-start = (f32[8,1024]{1,0:T(8,128)S(1)}, f32[8,1024]{1,0:T(8,128)S(1)}, u32[]{:S(2)}, u32[]{:S(2)}) collective-permute-start(f32[8,1024]{1,0:T(8,128)S(1)} %get-tuple-element.26), channel_id=1, source_target_pairs={{0,1},{1,2},{2,3},{3,4},{4,5},{5,6},{6,7},{7,8},{8,9},{9,10},{10,1... | collective-permute-start | bytes 98312 | tf_op jit(solution)/shard_map/ppermute | solution.py:50
  2.8 9.9 %collective-permute-start.1 = (f32[8,1024]{1,0:T(8,128)S(1)}, f32[8,1024]{1,0:T(8,128)S(1)}, u32[]{:S(2)}, u32[]{:S(2)}) collective-permute-start(f32[8,1024]{1,0:T(8,128)S(1)} %get-tuple-element.27), channel_id=1, source_target_pairs={{1,0},{2,1},{3,2},{4,3},{5,4},{6,5},{7,6},{8,7},{9,8},{10,9},{11,1... | collective-permute-start | bytes 98312 | tf_op jit(solution)/shard_map/ppermute | solution.py:51
  20.7 33.7 %all-to-all-start = ((f32[8,3,16,1024]{3,2,1,0:T(8,128)}), f32[8,3,16,1024]{3,2,1,0:T(8,128)}, u32[]{:S(2)}, u32[]{:S(2)}) async-start(f32[8,3,16,1024]{3,2,1,0:T(8,128)} %copy.53), calls=%async_computation | async-start | bytes 3145728 | tf_op jit(solution)/shard_map/all_to_all | solution.py:79
  57.6 24.5 %copy-start.5 = (f32[1,16,8,1024]{3,2,1,0:T(8,128)}, f32[1,16,8,1024]{3,2,1,0:T(8,128)S(1)}, u32[]{:S(2)}) copy-start(f32[1,16,8,1024]{3,2,1,0:T(8,128)S(1)} %get-tuple-element.9) | copy-start | bytes 1572868
  58.0 3.2 copy-start.8
  76.8 9.6 %collective-permute-start.2 = (f32[8,8192]{1,0:T(8,128)S(1)}, f32[8,8192]{1,0:T(8,128)S(1)}, u32[]{:S(2)}, u32[]{:S(2)}) collective-permute-start(f32[8,8192]{1,0:T(8,128)S(1)} %get-tuple-element.22), channel_id=1, source_target_pairs={{0,16},{16,32},{32,48},{48,64},{64,80},{80,96},{96,112},{112,1},{1... | collective-permute-start | bytes 786440 | tf_op jit(solution)/shard_map/ppermute | solution.py:41
  80.6 10.5 %collective-permute-start.3 = (f32[8,8192]{1,0:T(8,128)S(1)}, f32[8,8192]{1,0:T(8,128)S(1)}, u32[]{:S(2)}, u32[]{:S(2)}) collective-permute-start(f32[8,8192]{1,0:T(8,128)S(1)} %get-tuple-element.23), channel_id=1, source_target_pairs={{16,0},{32,16},{48,32},{64,48},{80,64},{96,80},{112,96},{1,112},{1... | collective-permute-start | bytes 786440 | tf_op jit(solution)/shard_map/ppermute | solution.py:42
  101.4 15.1 %copy-start.7 = (f32[2,8,8,1024]{3,1,2,0:T(8,128)S(1)}, f32[2,8,8,1024]{3,1,2,0:T(8,128)}, u32[]{:S(2)}) copy-start(f32[2,8,8,1024]{3,1,2,0:T(8,128)} %copy.116) | copy-start | bytes 1572868
  116.6 13.7 %copy-start = (f32[16,8192]{1,0:T(8,128)}, f32[16,8192]{1,0:T(8,128)S(1)}, u32[]{:S(2)}) copy-start(f32[16,8192]{1,0:T(8,128)S(1)} %fusion.221) | copy-start | bytes 1572868
  116.7 9.5 %collective-permute-start.4 = (f32[8,8192]{1,0:T(8,128)S(1)}, f32[8,8192]{1,0:T(8,128)S(1)}, u32[]{:S(2)}, u32[]{:S(2)}) collective-permute-start(f32[8,8192]{1,0:T(8,128)S(1)} %get-tuple-element.20), channel_id=1, source_target_pairs={{0,16},{16,32},{32,48},{48,64},{64,80},{80,96},{96,112},{112,1},{1... | collective-permute-start | bytes 786440 | tf_op jit(solution)/shard_map/ppermute | solution.py:41
  120.0 10.2 %collective-permute-start.5 = (f32[8,8192]{1,0:T(8,128)S(1)}, f32[8,8192]{1,0:T(8,128)S(1)}, u32[]{:S(2)}, u32[]{:S(2)}) collective-permute-start(f32[8,8192]{1,0:T(8,128)S(1)} %get-tuple-element.21), channel_id=1, source_target_pairs={{16,0},{32,16},{48,32},{64,48},{80,64},{96,80},{112,96},{1,112},{1... | collective-permute-start | bytes 786440 | tf_op jit(solution)/shard_map/ppermute | solution.py:42
  140.5 25.1 %copy-start.6 = (f32[1,16,8,1024]{3,2,1,0:T(8,128)S(1)}, f32[1,16,8,1024]{3,2,1,0:T(8,128)}, u32[]{:S(2)}) copy-start(f32[1,16,8,1024]{3,2,1,0:T(8,128)} %copy-done.5) | copy-start | bytes 1572868
  157.6 0.8 copy-start.3
  159.2 10.5 %collective-permute-start.6 = (f32[8,8192]{1,0:T(8,128)}, f32[8,8192]{1,0:T(8,128)S(1)}, u32[]{:S(2)}, u32[]{:S(2)}) collective-permute-start(f32[8,8192]{1,0:T(8,128)} %get-tuple-element.18), channel_id=1, source_target_pairs={{0,16},{16,32},{32,48},{48,64},{64,80},{80,96},{96,112},{112,1},{1... | collective-permute-start | bytes 786440 | tf_op jit(solution)/shard_map/ppermute | solution.py:41
  164.2 9.7 %collective-permute-start.7 = (f32[8,8192]{1,0:T(8,128)}, f32[8,8192]{1,0:T(8,128)}, u32[]{:S(2)}, u32[]{:S(2)}) collective-permute-start(f32[8,8192]{1,0:T(8,128)} %get-tuple-element.19), channel_id=1, source_target_pairs={{16,0},{32,16},{48,32},{64,48},{80,64},{96,80},{112,96},{1,112},{1... | collective-permute-start | bytes 786440 | tf_op jit(solution)/shard_map/ppermute | solution.py:42
  206.5 39.5 %copy-start.1 = (f32[16,8192]{1,0:T(8,128)S(1)}, f32[16,8192]{1,0:T(8,128)}, u32[]{:S(2)}) copy-start(f32[16,8192]{1,0:T(8,128)} %copy-done) | copy-start | bytes 1572868
  247.2 8.3 %collective-permute-start.8 = (f32[8,8192]{1,0:T(8,128)S(1)}, f32[8,8192]{1,0:T(8,128)S(1)}, u32[]{:S(2)}, u32[]{:S(2)}) collective-permute-start(f32[8,8192]{1,0:T(8,128)S(1)} %get-tuple-element.16), channel_id=1, source_target_pairs={{0,16},{16,32},{32,48},{48,64},{64,80},{80,96},{96,112},{112,1},{1... | collective-permute-start | bytes 786440 | tf_op jit(solution)/shard_map/ppermute | solution.py:41
  249.7 9.9 %collective-permute-start.9 = (f32[8,8192]{1,0:T(8,128)S(1)}, f32[8,8192]{1,0:T(8,128)S(1)}, u32[]{:S(2)}, u32[]{:S(2)}) collective-permute-start(f32[8,8192]{1,0:T(8,128)S(1)} %get-tuple-element.17), channel_id=1, source_target_pairs={{16,0},{32,16},{48,32},{64,48},{80,64},{96,80},{112,96},{1,112},{1... | collective-permute-start | bytes 786440 | tf_op jit(solution)/shard_map/ppermute | solution.py:42
  285.0 9.4 %collective-permute-start.10 = (f32[8,8192]{1,0:T(8,128)S(1)}, f32[8,8192]{1,0:T(8,128)S(1)}, u32[]{:S(2)}, u32[]{:S(2)}) collective-permute-start(f32[8,8192]{1,0:T(8,128)S(1)} %get-tuple-element.14), channel_id=1, source_target_pairs={{0,16},{16,32},{32,48},{48,64},{64,80},{80,96},{96,112},{112,1},{1... | collective-permute-start | bytes 786440 | tf_op jit(solution)/shard_map/ppermute | solution.py:41
  288.5 10.1 %collective-permute-start.11 = (f32[8,8192]{1,0:T(8,128)S(1)}, f32[8,8192]{1,0:T(8,128)S(1)}, u32[]{:S(2)}, u32[]{:S(2)}) collective-permute-start(f32[8,8192]{1,0:T(8,128)S(1)} %get-tuple-element.15), channel_id=1, source_target_pairs={{16,0},{32,16},{48,32},{64,48},{80,64},{96,80},{112,96},{1,112},{1... | collective-permute-start | bytes 786440 | tf_op jit(solution)/shard_map/ppermute | solution.py:42
  308.9 15.4 %copy-start.4 = (f32[1,16,8,1024]{3,2,1,0:T(8,128)S(1)}, f32[1,16,8,1024]{3,2,1,0:T(8,128)}, u32[]{:S(2)}) copy-start(f32[1,16,8,1024]{3,2,1,0:T(8,128)} %get-tuple-element.6) | copy-start | bytes 1572868

commit v2 on v1

--- a/solution.py
+++ b/solution.py
@@ -88,69 +88,68 @@
     return got.transpose(1, 0, 2, 3).reshape(k, n * days, cells // n)
 
 
-def group_sum_kernel(axis, x_ref, o_ref, slots, send, recv):
+def all_sum_kernel(times, x_ref, o_ref, slots, send, recv):
     n = slots.shape[0]
-    me = lax.axis_index(axis)
+    me = lax.axis_index("space") * times + lax.axis_index("tm")
 
     def peer(index):
-        return {axis: index}
+        return (lax.div(index, times), lax.rem(index, times))
 
-    barrier = pltpu.get_barrier_semaphore()
-    for k in range(1, n):
-        pl.semaphore_signal(barrier, 1, device_id=peer(lax.rem(me + k, n)), device_id_type=pl.DeviceIdType.MESH)
-    pl.semaphore_wait(barrier, n - 1)
-    copies = []
-    for k in range(1, n):
-        target = lax.rem(me + k, n)
-        copy = pltpu.make_async_remote_copy(
+    def copy_with(slot, target):
+        return pltpu.make_async_remote_copy(
             src_ref=x_ref,
-            dst_ref=slots.at[me],
+            dst_ref=slots.at[slot],
             send_sem=send.at[target],
-            recv_sem=recv.at[me],
+            recv_sem=recv.at[slot],
             device_id=peer(target),
             device_id_type=pl.DeviceIdType.MESH,
         )
-        copy.start()
-        copies.append(copy)
+
+    barrier = pltpu.get_barrier_semaphore()
+
+    @pl.loop(1, n)
+    def _(k):
+        pl.semaphore_signal(barrier, 1, device_id=peer(lax.rem(me + k, n)), device_id_type=pl.DeviceIdType.MESH)
+
+    pl.semaphore_wait(barrier, n - 1)
+
+    @pl.loop(1, n)
+    def _(k):
+        copy_with(me, lax.rem(me + k, n)).start()
+
     slots[me] = x_ref[...]
-    for k in range(1, n):
+
+    @pl.loop(1, n)
+    def _(k):
         source = lax.rem(me - k + n, n)
-        pltpu.make_async_remote_copy(
-            src_ref=x_ref,
-            dst_ref=slots.at[source],
-            send_sem=send.at[source],
-            recv_sem=recv.at[source],
-            device_id=peer(source),
-            device_id_type=pl.DeviceIdType.MESH,
-        ).wait_recv()
-    for copy in copies:
-        copy.wait_send()
+        copy_with(source, source).wait_recv()
+
+    @pl.loop(1, n)
+    def _(k):
+        copy_with(me, lax.rem(me + k, n)).wait_send()
+
     acc = slots[0]
     for j in range(1, n):
         acc = acc + slots[j]
     o_ref[...] = acc
 
 
-def group_sum(tile, axis, collective_id):
-    n = lax.axis_size(axis)
-    return pl.pallas_call(
-        functools.partial(group_sum_kernel, axis),
+def total(values):
+    spaces, times = lax.axis_size("space"), lax.axis_size("tm")
+    tile = jnp.zeros((8, 128), jnp.float32) + jnp.stack(values + [values[0]] * (8 - len(values)))[:, None]
+    summed = pl.pallas_call(
+        functools.partial(all_sum_kernel, times),
         out_shape=jax.ShapeDtypeStruct(tile.shape, tile.dtype),
         in_specs=[pl.BlockSpec(memory_space=pltpu.VMEM)],
         out_specs=pl.BlockSpec(memory_space=pltpu.VMEM),
         scratch_shapes=[
-            pltpu.VMEM((n,) + tile.shape, tile.dtype),
-            pltpu.SemaphoreType.DMA((n,)),
-            pltpu.SemaphoreType.DMA((n,)),
+            pltpu.VMEM((spaces * times,) + tile.shape, tile.dtype),
+            pltpu.SemaphoreType.DMA((spaces * times,)),
+            pltpu.SemaphoreType.DMA((spaces * times,)),
         ],
-        compiler_params=pltpu.CompilerParams(collective_id=collective_id, has_side_effects=True),
+        compiler_params=pltpu.CompilerParams(collective_id=0, has_side_effects=True),
     )(tile)
-
-
-def total(values):
-    tile = jnp.zeros((8, 128), jnp.float32) + jnp.stack(values + [values[0]] * (8 - len(values)))[:, None]
-    tile = group_sum(group_sum(tile, "space", 0), "tm", 1)
-    return [tile[i, 0] for i in range(len(values))]
+    return [summed[i, 0] for i in range(len(values))]
 
 
 def shards(coefficients, counts, coords, pattern, temporal_taps):

time: 373 us -> 380 us (1.019)
  Pallas kernels: 44 us -> 52.2 us
    pallas_call x4 -> x2, Pallas kernels: 44 us -> 52.2 us  [total(): pl.pallas_call(functools.partial(all_sum_kernel, times), out_shape=jax.Sh...]
where the time goes in v2:
time: 380 us; the launch traced here: 378 us
  matrix products  93.2 us (25%)
  other arithmetic  82.2 us (22%)
  Pallas kernels  52.2 us (14%)
  local copies, waits for them, and re-layouts  51.5 us (14%)
  waiting for transfers between devices  39.7 us (10%)
  starting transfers between devices  34.9 us (9%)
  blocking collectives  19.5 us (5%)
  between operations  5.13 us (1%)
    dot_general x6, matrix products, block_product(): jnp.einsum('rkc,drk->drc', weights, picked, precision=lax.Precision.HIGH)  93.2 us
    pallas_call x2, Pallas kernels, total(): pl.pallas_call(functools.partial(all_sum_kernel, times), out_shape=jax.Sh...  52.2 us
    reshape x5, other arithmetic, block_product(): blocked = field.reshape(day_count, blocks, BLOCK)  40.8 us
    mul x1, other arithmetic, wendland(): return amplitude * remain ** 4 * (1.0 + 4.0 * scaled)  26.8 us
    ppermute x5, waiting for transfers between devices, day_order_halo(): high = lax.ppermute(field[:BW], axes, backward)  21.4 us
    all_to_all x1, blocking collectives, to_cells(): lax.all_to_all(chunked, 'space', split_axis=0, concat_axis=0, tiled=True)  19.5 us
    gather x6, local copies, waits for them, and re-layouts, block_product(): blocked[:, pattern].reshape(day_count, blocks, pattern.shape[1] * BLOCK)  19.2 us
    ppermute x5, starting transfers between devices, day_order_halo(): low = lax.ppermute(field[field.shape[0] - BW:], axes, forward)  18.4 us
  transfers between devices with their start and end apart: 13, of which 10 were waited for; matrix products, arithmetic and copies ran while one was open for 10% of the time, Pallas kernels for 0%

profile of v2, /device:TPU:0, one launch (start us, length us, event | category | flops | bytes accessed | tf_op | source)
XLA Modules:
  0.0 378.3 jit_solution(3395629878919477369)
XLA Ops:
  5.9 2.3 gather_fusion.1
  9.7 1.7 fusion.263
  12.7 6.6 %fusion.233 = f32[128,1024]{1,0:T(8,128)S(1)} fusion(f32[136,1024]{1,0:T(8,128)S(1)} %constant_dynamic-update-slice_fusion.2, f32[136,1024]{1,0:T(8,128)S(1)} %get-tuple-element.24, f32[128,1024]{1,0:T(8,128)S(1)} %copy-done.2, f32[]{:T(128)} %bitcast.10, f32[]{:T(128)} %bitcast.9, f32[]{:T(128)} %bitcast.8, f32[]{:T(128)} %bitcast.7, f32[]{:T(128)} %bitcast.6, ...), kind=kLoop, calls=%fused_computation.396 | loop fusion | flops 3276800 | bytes 9437220 | tf_op jit(solution)/shard_map/add | solution.py:60
  20.7 6.9 %all-to-all-start = ((f32[8,3,16,1024]{3,2,1,0:T(8,128)}), f32[8,3,16,1024]{3,2,1,0:T(8,128)}, u32[]{:S(2)}, u32[]{:S(2)}) async-start(f32[8,3,16,1024]{3,2,1,0:T(8,128)} %copy.53), calls=%async_computation | async-start | bytes 3145728 | tf_op jit(solution)/shard_map/all_to_all | solution.py:79
  27.6 26.8 %add_multiply_fusion = f32[64,1024,128]{2,1,0:T(8,128)} fusion(f32[64,1024]{1,0:T(8,128)S(1)} %get-tuple-element.44, f32[64,128]{1,0:T(8,128)S(1)} %bitcast.204, f32[64,1024]{1,0:T(8,128)S(1)} %get-tuple-element.45, f32[64,128]{1,0:T(8,128)S(1)} %bitcast.203), kind=kLoop, calls=%fused_computation.7 | loop fusion | flops 117440512 | bytes 34144256 | tf_op jit(solution)/shard_map/mul | solution.py:21
  54.4 2.3 copy.178
  58.1 3.2 gather_fusion
  61.6 15.1 %fusion.21 = f32[64,2,8,128]{3,2,1,0:T(8,128)S(1)} fusion(f32[64,1024,128]{2,1,0:T(8,128)} %add_multiply_fusion, f32[64,8,2,8,128]{4,3,2,1,0:T(8,128)} %bitcast.179), kind=kOutput, calls=%fused_computation.169 | convolution fusion | flops 805306368 | bytes 38273024 | tf_op jit(solution)/shard_map/rkc,drk->drc/dot_general | solution.py:71
  76.8 3.8 %collective-permute-start.2 = (f32[8,8192]{1,0:T(8,128)S(1)}, f32[8,8192]{1,0:T(8,128)S(1)}, u32[]{:S(2)}, u32[]{:S(2)}) collective-permute-start(f32[8,8192]{1,0:T(8,128)S(1)} %get-tuple-element.22), channel_id=1, source_target_pairs={{0,16},{16,32},{32,48},{48,64},{64,80},{80,96},{96,112},{112,1},{1... | collective-permute-start | bytes 786440 | tf_op jit(solution)/shard_map/ppermute | solution.py:41
  80.6 1.5 collective-permute-start.3
  83.2 3.2 collective-permute-done.2
  86.4 4.7 %collective-permute-done.3 = f32[8,8192]{1,0:T(8,128)S(1)} collective-permute-done((f32[8,8192]{1,0:T(8,128)S(1)}, f32[8,8192]{1,0:T(8,128)S(1)}, u32[]{:S(2)}, u32[]{:S(2)}) %collective-permute-start.3) | collective-permute-done | bytes 262176 | tf_op jit(solution)/shard_map/ppermute | solution.py:42
  91.1 7.1 %copy_bitcast_fusion.6 = f32[16,64,128]{2,0,1:T(8,128)S(1)} fusion(f32[16,8192]{1,0:T(8,128)S(1)} %bitcast_subtract_fusion, f32[8,8192]{1,0:T(8,128)S(1)} %collective-permute-done.3, f32[8,8192]{1,0:T(8,128)S(1)} %collective-permute-done.2, f32[]{:T(128)} %bitcast.10, f32[]{:T(128)} %bitcast.9, f32[]{:T(128)} %bitcast.8, f32[]{:T(128)} %bitcast.7, ...), kind=kLoop, calls=%fused_computation.373 | loop fusion | flops 5373952 | bytes 1572900 | tf_op jit(solution)/shard_map/reshape | solution.py:69
  98.2 3.2 gather_fusion.2
  101.4 15.1 %fusion.12 = f32[64,16,128]{2,1,0:T(8,128)S(1)} fusion(f32[64,1024,128]{2,1,0:T(8,128)} %add_multiply_fusion, f32[64,8,2,8,128]{4,3,2,1,0:T(8,128)} %bitcast.181), kind=kOutput, calls=%fused_computation.20 | convolution fusion | flops 805306368 | bytes 38273024 | tf_op jit(solution)/shard_map/rkc,drk->drc/dot_general | solution.py:71
  116.7 3.4 collective-permute-start.4
  121.3 4.8 %collective-permute-done.4 = f32[8,8192]{1,0:T(8,128)S(1)} collective-permute-done((f32[8,8192]{1,0:T(8,128)S(1)}, f32[8,8192]{1,0:T(8,128)S(1)}, u32[]{:S(2)}, u32[]{:S(2)}) %collective-permute-start.4) | collective-permute-done | bytes 262176 | tf_op jit(solution)/shard_map/ppermute | solution.py:41
  126.1 4.1 %collective-permute-done.5 = f32[8,8192]{1,0:T(8,128)S(1)} collective-permute-done((f32[8,8192]{1,0:T(8,128)S(1)}, f32[8,8192]{1,0:T(8,128)S(1)}, u32[]{:S(2)}, u32[]{:S(2)}) %collective-permute-start.5) | collective-permute-done | bytes 262176 | tf_op jit(solution)/shard_map/ppermute | solution.py:42
  130.3 7.1 %copy_bitcast_fusion.5 = f32[16,64,128]{2,0,1:T(8,128)S(1)} fusion(f32[16,8192]{1,0:T(8,128)S(1)} %fusion.221, f32[8,8192]{1,0:T(8,128)S(1)} %collective-permute-done.5, f32[8,8192]{1,0:T(8,128)S(1)} %collective-permute-done.4, f32[]{:T(128)} %bitcast.10, f32[]{:T(128)} %bitcast.9, f32[]{:T(128)} %bitcast.8, f32[]{:T(128)} %bitcast.7, f32[]{:T(128)} %bitcast.6, ...), kind=kLoop, calls=%fused_computation.372 | loop fusion | flops 5373952 | bytes 1572900 | tf_op jit(solution)/shard_map/reshape | solution.py:69
  137.3 3.2 gather_fusion.3
  140.5 15.9 %fusion.24 = f32[64,2,8,128]{3,2,1,0:T(8,128)} fusion(f32[64,1024,128]{2,1,0:T(8,128)} %add_multiply_fusion, f32[64,8,2,8,128]{4,3,2,1,0:T(8,128)} %bitcast.182), kind=kOutput, calls=%fused_computation.170 | convolution fusion | flops 805306368 | bytes 38273024 | tf_op jit(solution)/shard_map/rkc,drk->drc/dot_general | solution.py:71
  159.2 4.9 %collective-permute-start.6 = (f32[8,8192]{1,0:T(8,128)}, f32[8,8192]{1,0:T(8,128)S(1)}, u32[]{:S(2)}, u32[]{:S(2)}) collective-permute-start(f32[8,8192]{1,0:T(8,128)} %get-tuple-element.18), channel_id=1, source_target_pairs={{0,16},{16,32},{32,48},{48,64},{64,80},{80,96},{96,112},{112,1},{1... | collective-permute-start | bytes 786440 | tf_op jit(solution)/shard_map/ppermute | solution.py:41
  164.2 1.5 collective-permute-start.7
  167.6 2.1 collective-permute-done.6
  169.7 4.1 %collective-permute-done.7 = f32[8,8192]{1,0:T(8,128)} collective-permute-done((f32[8,8192]{1,0:T(8,128)}, f32[8,8192]{1,0:T(8,128)}, u32[]{:S(2)}, u32[]{:S(2)}) %collective-permute-start.7) | collective-permute-done | bytes 262176 | tf_op jit(solution)/shard_map/ppermute | solution.py:42
  173.9 12.5 %copy_bitcast_fusion.4 = f32[16,64,128]{2,0,1:T(8,128)S(1)} fusion(f32[16,8192]{1,0:T(8,128)} %copy-done.3, f32[8,8192]{1,0:T(8,128)} %collective-permute-done.7, f32[8,8192]{1,0:T(8,128)S(1)} %collective-permute-done.6, f32[]{:T(128)} %bitcast.10, f32[]{:T(128)} %bitcast.9, f32[]{:T(128)} %bitcast.8, f32[]{:T(128)} %bitcast.7, f32[]{:T(128)} %bitcast.6, ...), kind=kLoop, calls=%fused_computation.371 | loop fusion | flops 5373952 | bytes 1572900 | tf_op jit(solution)/shard_map/reshape | solution.py:69
  186.3 3.2 gather_fusion.4
  189.5 17.0 %fusion.251 = (f32[]{:T(128)}, f32[64,16,128]{2,1,0:T(8,128)}) fusion(f32[16,64,128]{2,1,0:T(8,128)} %squeeze.47, f32[64,16,128]{2,1,0:T(8,128)S(1)} %fusion.12, f32[64,1024,128]{2,1,0:T(8,128)} %add_multiply_fusion, f32[64,8,2,8,128]{4,3,2,1,0:T(8,128)} %bitcast.184), kind=kOutput, calls=%fused_computation.422 | convolution fusion | flops 805961728 | bytes 39321604 | tf_op jit(solution)/shard_map/rkc,drk->drc/dot_general | solution.py:71
  206.5 2.1 copy.72
  209.7 2.6 multiply_reduce_fusion.1
  212.3 4.9 %stack.50 = f32[8]{0:T(128)S(1)} concatenate(f32[1]{0:T(128)} %bitcast.26, f32[1]{0:T(128)} %bitcast.33, f32[1]{0:T(128)} %bitcast.34, f32[1]{0:T(128)} %bitcast.26, f32[1]{0:T(128)} %bitcast.26, f32[1]{0:T(128)} %bitcast.26, f32[1]{0:T(128)} %bitcast.26, f32[1]{0:T(128)} %bitcast.26), dimensions={0} | concatenate | bytes 64 | tf_op jit(solution)/shard_map/stack | solution.py:139
  217.9 27.7 %shard_map.68 = f32[8,128]{1,0:T(8,128)} custom-call(f32[8,128]{1,0:T(8,128)} %add.437.x_ref), custom_call_target="tpu_custom_call" | custom-call | tf_op jit(solution)/shard_map/pallas_call | solution.py:140
  245.6 1.4 fusion.262
  251.5 2.6 collective-permute-start.8
  255.4 4.5 %collective-permute-done.8 = f32[8,8192]{1,0:T(8,128)S(1)} collective-permute-done((f32[8,8192]{1,0:T(8,128)S(1)}, f32[8,8192]{1,0:T(8,128)S(1)}, u32[]{:S(2)}, u32[]{:S(2)}) %collective-permute-start.8) | collective-permute-done | bytes 262176 | tf_op jit(solution)/shard_map/ppermute | solution.py:41
  259.8 4.4 %collective-permute-done.9 = f32[8,8192]{1,0:T(8,128)S(1)} collective-permute-done((f32[8,8192]{1,0:T(8,128)S(1)}, f32[8,8192]{1,0:T(8,128)S(1)}, u32[]{:S(2)}, u32[]{:S(2)}) %collective-permute-start.9) | collective-permute-done | bytes 262176 | tf_op jit(solution)/shard_map/ppermute | solution.py:42
  264.2 7.1 %copy_bitcast_fusion.3 = f32[16,64,128]{2,0,1:T(8,128)S(1)} fusion(f32[16,8192]{1,0:T(8,128)S(1)} %fusion.220, f32[8,8192]{1,0:T(8,128)S(1)} %collective-permute-done.9, f32[8,8192]{1,0:T(8,128)S(1)} %collective-permute-done.8, f32[]{:T(128)} %bitcast.10, f32[]{:T(128)} %bitcast.9, f32[]{:T(128)} %bitcast.8, f32[]{:T(128)} %bitcast.7, f32[]{:T(128)} %bitcast.6, ...), kind=kLoop, calls=%fused_computation.370 | loop fusion | flops 5373952 | bytes 1572900 | tf_op jit(solution)/shard_map/reshape | solution.py:69
  271.3 3.2 gather_fusion.5
  274.5 15.0 %fusion.27 = f32[64,2,8,128]{3,2,1,0:T(8,128)S(1)} fusion(f32[64,1024,128]{2,1,0:T(8,128)} %add_multiply_fusion, f32[64,8,2,8,128]{4,3,2,1,0:T(8,128)} %bitcast.183), kind=kOutput, calls=%fused_computation.171 | convolution fusion | flops 805306368 | bytes 38273024 | tf_op jit(solution)/shard_map/rkc,drk->drc/dot_general | solution.py:71
  289.7 3.7 collective-permute-start.10
  293.3 1.6 collective-permute-start.11
  294.9 3.6 collective-permute-done.10
  298.5 4.1 %collective-permute-done.11 = f32[8,8192]{1,0:T(8,128)S(1)} collective-permute-done((f32[8,8192]{1,0:T(8,128)S(1)}, f32[8,8192]{1,0:T(8,128)S(1)}, u32[]{:S(2)}, u32[]{:S(2)}) %collective-permute-start.11) | collective-permute-done | bytes 262176 | tf_op jit(solution)/shard_map/ppermute | solution.py:42
  302.6 7.1 %copy_bitcast_fusion.2 = f32[16,64,128]{2,0,1:T(8,128)S(1)} fusion(f32[16,8192]{1,0:T(8,128)S(1)} %bitcast_multiply_fusion, f32[8,8192]{1,0:T(8,128)S(1)} %collective-permute-done.11, f32[8,8192]{1,0:T(8,128)S(1)} %collective-permute-done.10, f32[]{:T(128)} %bitcast.10, f32[]{:T(128)} %bitcast.9, f32[]{:T(128)} %bitcast.8, f32[]{:T(128)} %bitcast.7, ...), kind=kLoop, calls=%fused_computation.369 | loop fusion | flops 5373952 | bytes 1572900 | tf_op jit(solution)/shard_map/reshape | solution.py:69
  309.7 3.2 gather_fusion.6
  312.9 15.1 %fusion.30 = f32[16,64,128]{2,0,1:T(8,128)S(1)} fusion(f32[64,1024,128]{2,1,0:T(8,128)} %add_multiply_fusion, f32[64,8,2,8,128]{4,3,2,1,0:T(8,128)} %bitcast.180), kind=kOutput, calls=%fused_computation.172 | convolution fusion | flops 805306368 | bytes 38273024 | tf_op jit(solution)/shard_map/rkc,drk->drc/dot_general | solution.py:71
  330.3 24.5 %shard_map.69 = f32[8,128]{1,0:T(8,128)} custom-call(f32[8,128]{1,0:T(8,128)} %add.474.x_ref), custom_call_target="tpu_custom_call" | custom-call | tf_op jit(solution)/shard_map/pallas_call | solution.py:140
  357.6 19.5 %all_to_all.10 = f32[8,2,16,1024]{3,2,1,0:T(8,128)S(1)} all-to-all(f32[8,2,16,1024]{3,2,1,0:T(8,128)S(1)} %copy.83), channel_id=1, replica_groups=mesh['space'=8,'tm'=16] {'space'}, dimensions={0} | all-to-all | bytes 2097152 | tf_op jit(solution)/shard_map/all_to_all | solution.py:87
  (69 shorter events, 28.2 us)
Async XLA Ops:
  0.6 11.9 %copy-start.2 = (f32[128,1024]{1,0:T(8,128)S(1)}, f32[128,1024]{1,0:T(8,128)}, u32[]{:S(2)}) copy-start(f32[128,1024]{1,0:T(8,128)} %param.5) | copy-start | bytes 1572868
  1.5 11.0 %collective-permute-start = (f32[8,1024]{1,0:T(8,128)S(1)}, f32[8,1024]{1,0:T(8,128)S(1)}, u32[]{:S(2)}, u32[]{:S(2)}) collective-permute-start(f32[8,1024]{1,0:T(8,128)S(1)} %get-tuple-element.26), channel_id=1, source_target_pairs={{0,1},{1,2},{2,3},{3,4},{4,5},{5,6},{6,7},{7,8},{8,9},{9,10},{10,1... | collective-permute-start | bytes 98312 | tf_op jit(solution)/shard_map/ppermute | solution.py:50
  2.8 9.9 %collective-permute-start.1 = (f32[8,1024]{1,0:T(8,128)S(1)}, f32[8,1024]{1,0:T(8,128)S(1)}, u32[]{:S(2)}, u32[]{:S(2)}) collective-permute-start(f32[8,1024]{1,0:T(8,128)S(1)} %get-tuple-element.27), channel_id=1, source_target_pairs={{1,0},{2,1},{3,2},{4,3},{5,4},{6,5},{7,6},{8,7},{9,8},{10,9},{11,1... | collective-permute-start | bytes 98312 | tf_op jit(solution)/shard_map/ppermute | solution.py:51
  20.7 33.7 %all-to-all-start = ((f32[8,3,16,1024]{3,2,1,0:T(8,128)}), f32[8,3,16,1024]{3,2,1,0:T(8,128)}, u32[]{:S(2)}, u32[]{:S(2)}) async-start(f32[8,3,16,1024]{3,2,1,0:T(8,128)} %copy.53), calls=%async_computation | async-start | bytes 3145728 | tf_op jit(solution)/shard_map/all_to_all | solution.py:79
  57.6 24.5 %copy-start.5 = (f32[1,16,8,1024]{3,2,1,0:T(8,128)}, f32[1,16,8,1024]{3,2,1,0:T(8,128)S(1)}, u32[]{:S(2)}) copy-start(f32[1,16,8,1024]{3,2,1,0:T(8,128)S(1)} %get-tuple-element.9) | copy-start | bytes 1572868
  58.0 3.2 copy-start.8
  76.8 9.6 %collective-permute-start.2 = (f32[8,8192]{1,0:T(8,128)S(1)}, f32[8,8192]{1,0:T(8,128)S(1)}, u32[]{:S(2)}, u32[]{:S(2)}) collective-permute-start(f32[8,8192]{1,0:T(8,128)S(1)} %get-tuple-element.22), channel_id=1, source_target_pairs={{0,16},{16,32},{32,48},{48,64},{64,80},{80,96},{96,112},{112,1},{1... | collective-permute-start | bytes 786440 | tf_op jit(solution)/shard_map/ppermute | solution.py:41
  80.6 10.5 %collective-permute-start.3 = (f32[8,8192]{1,0:T(8,128)S(1)}, f32[8,8192]{1,0:T(8,128)S(1)}, u32[]{:S(2)}, u32[]{:S(2)}) collective-permute-start(f32[8,8192]{1,0:T(8,128)S(1)} %get-tuple-element.23), channel_id=1, source_target_pairs={{16,0},{32,16},{48,32},{64,48},{80,64},{96,80},{112,96},{1,112},{1... | collective-permute-start | bytes 786440 | tf_op jit(solution)/shard_map/ppermute | solution.py:42
  101.4 15.1 %copy-start.7 = (f32[2,8,8,1024]{3,1,2,0:T(8,128)S(1)}, f32[2,8,8,1024]{3,1,2,0:T(8,128)}, u32[]{:S(2)}) copy-start(f32[2,8,8,1024]{3,1,2,0:T(8,128)} %copy.116) | copy-start | bytes 1572868
  116.6 13.7 %copy-start = (f32[16,8192]{1,0:T(8,128)}, f32[16,8192]{1,0:T(8,128)S(1)}, u32[]{:S(2)}) copy-start(f32[16,8192]{1,0:T(8,128)S(1)} %fusion.221) | copy-start | bytes 1572868
  116.7 9.5 %collective-permute-start.4 = (f32[8,8192]{1,0:T(8,128)S(1)}, f32[8,8192]{1,0:T(8,128)S(1)}, u32[]{:S(2)}, u32[]{:S(2)}) collective-permute-start(f32[8,8192]{1,0:T(8,128)S(1)} %get-tuple-element.20), channel_id=1, source_target_pairs={{0,16},{16,32},{32,48},{48,64},{64,80},{80,96},{96,112},{112,1},{1... | collective-permute-start | bytes 786440 | tf_op jit(solution)/shard_map/ppermute | solution.py:41
  120.0 10.2 %collective-permute-start.5 = (f32[8,8192]{1,0:T(8,128)S(1)}, f32[8,8192]{1,0:T(8,128)S(1)}, u32[]{:S(2)}, u32[]{:S(2)}) collective-permute-start(f32[8,8192]{1,0:T(8,128)S(1)} %get-tuple-element.21), channel_id=1, source_target_pairs={{16,0},{32,16},{48,32},{64,48},{80,64},{96,80},{112,96},{1,112},{1... | collective-permute-start | bytes 786440 | tf_op jit(solution)/shard_map/ppermute | solution.py:42
  140.5 25.1 %copy-start.6 = (f32[1,16,8,1024]{3,2,1,0:T(8,128)S(1)}, f32[1,16,8,1024]{3,2,1,0:T(8,128)}, u32[]{:S(2)}) copy-start(f32[1,16,8,1024]{3,2,1,0:T(8,128)} %copy-done.5) | copy-start | bytes 1572868
  157.6 0.8 copy-start.3
  159.2 10.5 %collective-permute-start.6 = (f32[8,8192]{1,0:T(8,128)}, f32[8,8192]{1,0:T(8,128)S(1)}, u32[]{:S(2)}, u32[]{:S(2)}) collective-permute-start(f32[8,8192]{1,0:T(8,128)} %get-tuple-element.18), channel_id=1, source_target_pairs={{0,16},{16,32},{32,48},{48,64},{64,80},{80,96},{96,112},{112,1},{1... | collective-permute-start | bytes 786440 | tf_op jit(solution)/shard_map/ppermute | solution.py:41
  164.2 9.7 %collective-permute-start.7 = (f32[8,8192]{1,0:T(8,128)}, f32[8,8192]{1,0:T(8,128)}, u32[]{:S(2)}, u32[]{:S(2)}) collective-permute-start(f32[8,8192]{1,0:T(8,128)} %get-tuple-element.19), channel_id=1, source_target_pairs={{16,0},{32,16},{48,32},{64,48},{80,64},{96,80},{112,96},{1,112},{1... | collective-permute-start | bytes 786440 | tf_op jit(solution)/shard_map/ppermute | solution.py:42
  206.5 43.7 %copy-start.1 = (f32[16,8192]{1,0:T(8,128)S(1)}, f32[16,8192]{1,0:T(8,128)}, u32[]{:S(2)}) copy-start(f32[16,8192]{1,0:T(8,128)} %copy-done) | copy-start | bytes 1572868
  251.5 8.4 %collective-permute-start.8 = (f32[8,8192]{1,0:T(8,128)S(1)}, f32[8,8192]{1,0:T(8,128)S(1)}, u32[]{:S(2)}, u32[]{:S(2)}) collective-permute-start(f32[8,8192]{1,0:T(8,128)S(1)} %get-tuple-element.16), channel_id=1, source_target_pairs={{0,16},{16,32},{32,48},{48,64},{64,80},{80,96},{96,112},{112,1},{1... | collective-permute-start | bytes 786440 | tf_op jit(solution)/shard_map/ppermute | solution.py:41
  254.1 10.2 %collective-permute-start.9 = (f32[8,8192]{1,0:T(8,128)S(1)}, f32[8,8192]{1,0:T(8,128)S(1)}, u32[]{:S(2)}, u32[]{:S(2)}) collective-permute-start(f32[8,8192]{1,0:T(8,128)S(1)} %get-tuple-element.17), channel_id=1, source_target_pairs={{16,0},{32,16},{48,32},{64,48},{80,64},{96,80},{112,96},{1,112},{1... | collective-permute-start | bytes 786440 | tf_op jit(solution)/shard_map/ppermute | solution.py:42
  289.7 8.8 %collective-permute-start.10 = (f32[8,8192]{1,0:T(8,128)S(1)}, f32[8,8192]{1,0:T(8,128)S(1)}, u32[]{:S(2)}, u32[]{:S(2)}) collective-permute-start(f32[8,8192]{1,0:T(8,128)S(1)} %get-tuple-element.14), channel_id=1, source_target_pairs={{0,16},{16,32},{32,48},{48,64},{64,80},{80,96},{96,112},{112,1},{1... | collective-permute-start | bytes 786440 | tf_op jit(solution)/shard_map/ppermute | solution.py:41
  293.3 9.3 %collective-permute-start.11 = (f32[8,8192]{1,0:T(8,128)S(1)}, f32[8,8192]{1,0:T(8,128)S(1)}, u32[]{:S(2)}, u32[]{:S(2)}) collective-permute-start(f32[8,8192]{1,0:T(8,128)S(1)} %get-tuple-element.15), channel_id=1, source_target_pairs={{16,0},{32,16},{48,32},{64,48},{80,64},{96,80},{112,96},{1,112},{1... | collective-permute-start | bytes 786440 | tf_op jit(solution)/shard_map/ppermute | solution.py:42
  312.9 15.4 %copy-start.4 = (f32[1,16,8,1024]{3,2,1,0:T(8,128)S(1)}, f32[1,16,8,1024]{3,2,1,0:T(8,128)}, u32[]{:S(2)}) copy-start(f32[1,16,8,1024]{3,2,1,0:T(8,128)} %get-tuple-element.6) | copy-start | bytes 1572868

commit v3 on v1

--- a/solution.py
+++ b/solution.py
@@ -34,7 +34,8 @@
 
 def day_order_halo(field):
     spaces, times = lax.axis_size("space"), lax.axis_size("tm")
-    place = [(rank % spaces) * times + rank // spaces for rank in range(spaces * times)]
+    order = snake(spaces)
+    place = [order[rank % spaces] * times + rank // spaces for rank in range(spaces * times)]
     forward = [(place[i], place[i + 1]) for i in range(len(place) - 1)]
     backward = [(place[i + 1], place[i]) for i in range(len(place) - 1)]
     axes = ("space", "tm")
@@ -72,10 +73,15 @@
     return out.reshape(day_count, blocks * BLOCK)
 
 
+def snake(spaces):
+    half = spaces // 2
+    return [i if i < half else spaces + half - 1 - i for i in range(spaces)]
+
+
 def to_days(field):
     n = lax.axis_size("space")
     k, days, cells = field.shape
-    chunked = field.reshape(k, n, days // n, cells).transpose(1, 0, 2, 3)
+    chunked = field.reshape(k, n, days // n, cells)[:, jnp.array(snake(n))].transpose(1, 0, 2, 3)
     got = lax.all_to_all(chunked, "space", split_axis=0, concat_axis=0, tiled=True)
     return got.transpose(1, 2, 0, 3).reshape(k, days // n, n * cells)
 
@@ -85,7 +91,7 @@
     k, days, cells = field.shape
     chunked = field.reshape(k, days, n, cells // n).transpose(2, 0, 1, 3)
     got = lax.all_to_all(chunked, "space", split_axis=0, concat_axis=0, tiled=True)
-    return got.transpose(1, 0, 2, 3).reshape(k, n * days, cells // n)
+    return got[jnp.array(snake(n))].transpose(1, 0, 2, 3).reshape(k, n * days, cells // n)
 
 
 def group_sum_kernel(axis, x_ref, o_ref, slots, send, recv):

time: 373 us -> 362 us (0.971)
  Pallas kernels: 44 us -> 37.8 us
    pallas_call x4, Pallas kernels: 44 us -> 37.8 us  [group_sum(): pl.pallas_call(functools.partial(group_sum_kernel, axis), out_shape=jax.S...]
  transfers between devices with their start and end apart: 13 -> 13, of which waited for: 10 -> 9; matrix products, arithmetic and copies ran while one was open for 10% -> 11% of each run, Pallas kernels for 0% -> 0%
where the time goes in v3:
time: 362 us; the launch traced here: 360 us
  matrix products  93.2 us (26%)
  other arithmetic  84.2 us (23%)
  local copies, waits for them, and re-layouts  51.5 us (14%)
  Pallas kernels  37.8 us (10%)
  waiting for transfers between devices  36.7 us (10%)
  starting transfers between devices  32.5 us (9%)
  blocking collectives  19.5 us (5%)
  between operations  5.15 us (1%)
    dot_general x6, matrix products, block_product(): jnp.einsum('rkc,drk->drc', weights, picked, precision=lax.Precision.HIGH)  93.2 us
    reshape x5, other arithmetic, block_product(): blocked = field.reshape(day_count, blocks, BLOCK)  40.8 us
    pallas_call x4, Pallas kernels, group_sum(): pl.pallas_call(functools.partial(group_sum_kernel, axis), out_shape=jax.S...  37.8 us
    mul x1, other arithmetic, wendland(): return amplitude * remain ** 4 * (1.0 + 4.0 * scaled)  26.8 us
    ppermute x5, waiting for transfers between devices, day_order_halo(): high = lax.ppermute(field[:BW], axes, backward)  20.8 us
    all_to_all x1, blocking collectives, to_cells(): lax.all_to_all(chunked, 'space', split_axis=0, concat_axis=0, tiled=True)  19.5 us
    gather x6, local copies, waits for them, and re-layouts, block_product(): blocked[:, pattern].reshape(day_count, blocks, pattern.shape[1] * BLOCK)  19.2 us
    ppermute x5, waiting for transfers between devices, day_order_halo(): low = lax.ppermute(field[field.shape[0] - BW:], axes, forward)  15.9 us
  transfers between devices with their start and end apart: 13, of which 9 were waited for; matrix products, arithmetic and copies ran while one was open for 11% of the time, Pallas kernels for 0%

profile of v3, /device:TPU:0, one launch (start us, length us, event | category | flops | bytes accessed | tf_op | source)
XLA Modules:
  0.0 360.5 jit_solution(4972444639270807505)
XLA Ops:
  6.6 2.3 gather_fusion.2
  10.3 1.7 fusion.262
  13.3 6.6 %fusion.233 = f32[128,1024]{1,0:T(8,128)S(1)} fusion(f32[136,1024]{1,0:T(8,128)S(1)} %constant_dynamic-update-slice_fusion.2, f32[136,1024]{1,0:T(8,128)S(1)} %get-tuple-element.24, f32[128,1024]{1,0:T(8,128)S(1)} %copy-done.2, f32[]{:T(128)} %bitcast.10, f32[]{:T(128)} %bitcast.9, f32[]{:T(128)} %bitcast.8, f32[]{:T(128)} %bitcast.7, f32[]{:T(128)} %bitcast.6, ...), kind=kLoop, calls=%fused_computation.396 | loop fusion | flops 3276800 | bytes 9437220 | tf_op jit(solution)/shard_map/add | solution.py:61
  20.1 1.8 gather_fusion
  21.9 6.9 %all-to-all-start = ((f32[8,3,16,1024]{3,2,1,0:T(8,128)}), f32[8,3,16,1024]{3,2,1,0:T(8,128)S(1)}, u32[]{:S(2)}, u32[]{:S(2)}) async-start(f32[8,3,16,1024]{3,2,1,0:T(8,128)} %gather_fusion), calls=%async_computation | async-start | bytes 3145728 | tf_op jit(solution)/shard_map/all_to_all | solution.py:85
  28.8 26.8 %add_multiply_fusion = f32[64,1024,128]{2,1,0:T(8,128)} fusion(f32[64,1024]{1,0:T(8,128)S(1)} %bitcast.197, f32[64,128]{1,0:T(8,128)S(1)} %bitcast.204, f32[64,1024]{1,0:T(8,128)S(1)} %bitcast.198, f32[64,128]{1,0:T(8,128)S(1)} %bitcast.203), kind=kLoop, calls=%fused_computation.9 | loop fusion | flops 117440512 | bytes 34144256 | tf_op jit(solution)/shard_map/mul | solution.py:21
  57.2 3.2 gather_fusion.1
  60.5 15.1 %fusion.21 = f32[64,2,8,128]{3,2,1,0:T(8,128)S(1)} fusion(f32[64,1024,128]{2,1,0:T(8,128)} %add_multiply_fusion, f32[64,8,2,8,128]{4,3,2,1,0:T(8,128)} %bitcast.177), kind=kOutput, calls=%fused_computation.170 | convolution fusion | flops 805306368 | bytes 38273024 | tf_op jit(solution)/shard_map/rkc,drk->drc/dot_general | solution.py:72
  75.7 3.8 %collective-permute-start.2 = (f32[8,8192]{1,0:T(8,128)S(1)}, f32[8,8192]{1,0:T(8,128)S(1)}, u32[]{:S(2)}, u32[]{:S(2)}) collective-permute-start(f32[8,8192]{1,0:T(8,128)S(1)} %get-tuple-element.22), channel_id=1, source_target_pairs={{0,16},{16,32},{32,48},{48,112},{112,96},{96,80},{80,64},{64,1},{1... | collective-permute-start | bytes 786440 | tf_op jit(solution)/shard_map/ppermute | solution.py:42
  81.8 3.5 collective-permute-done.2
  85.3 4.7 %collective-permute-done.3 = f32[8,8192]{1,0:T(8,128)S(1)} collective-permute-done((f32[8,8192]{1,0:T(8,128)S(1)}, f32[8,8192]{1,0:T(8,128)S(1)}, u32[]{:S(2)}, u32[]{:S(2)}) %collective-permute-start.3) | collective-permute-done | bytes 262176 | tf_op jit(solution)/shard_map/ppermute | solution.py:43
  90.0 7.1 %copy_bitcast_fusion.4 = f32[16,64,128]{2,0,1:T(8,128)S(1)} fusion(f32[16,8192]{1,0:T(8,128)S(1)} %bitcast_subtract_fusion, f32[8,8192]{1,0:T(8,128)S(1)} %collective-permute-done.3, f32[8,8192]{1,0:T(8,128)S(1)} %collective-permute-done.2, f32[]{:T(128)} %bitcast.10, f32[]{:T(128)} %bitcast.9, f32[]{:T(128)} %bitcast.8, f32[]{:T(128)} %bitcast.7, ...), kind=kLoop, calls=%fused_computation.373 | loop fusion | flops 5373952 | bytes 1572900 | tf_op jit(solution)/shard_map/reshape | solution.py:70
  97.1 3.2 gather_fusion.3
  100.3 15.1 %fusion.12 = f32[64,16,128]{2,1,0:T(8,128)S(1)} fusion(f32[64,1024,128]{2,1,0:T(8,128)} %add_multiply_fusion, f32[64,8,2,8,128]{4,3,2,1,0:T(8,128)} %bitcast.179), kind=kOutput, calls=%fused_computation.22 | convolution fusion | flops 805306368 | bytes 38273024 | tf_op jit(solution)/shard_map/rkc,drk->drc/dot_general | solution.py:72
  115.6 3.4 collective-permute-start.4
  120.2 4.8 %collective-permute-done.4 = f32[8,8192]{1,0:T(8,128)S(1)} collective-permute-done((f32[8,8192]{1,0:T(8,128)S(1)}, f32[8,8192]{1,0:T(8,128)S(1)}, u32[]{:S(2)}, u32[]{:S(2)}) %collective-permute-start.4) | collective-permute-done | bytes 262176 | tf_op jit(solution)/shard_map/ppermute | solution.py:42
  125.0 4.1 %collective-permute-done.5 = f32[8,8192]{1,0:T(8,128)S(1)} collective-permute-done((f32[8,8192]{1,0:T(8,128)S(1)}, f32[8,8192]{1,0:T(8,128)S(1)}, u32[]{:S(2)}, u32[]{:S(2)}) %collective-permute-start.5) | collective-permute-done | bytes 262176 | tf_op jit(solution)/shard_map/ppermute | solution.py:43
  129.2 7.1 %copy_bitcast_fusion.3 = f32[16,64,128]{2,0,1:T(8,128)S(1)} fusion(f32[16,8192]{1,0:T(8,128)S(1)} %fusion.221, f32[8,8192]{1,0:T(8,128)S(1)} %collective-permute-done.5, f32[8,8192]{1,0:T(8,128)S(1)} %collective-permute-done.4, f32[]{:T(128)} %bitcast.10, f32[]{:T(128)} %bitcast.9, f32[]{:T(128)} %bitcast.8, f32[]{:T(128)} %bitcast.7, f32[]{:T(128)} %bitcast.6, ...), kind=kLoop, calls=%fused_computation.372 | loop fusion | flops 5373952 | bytes 1572900 | tf_op jit(solution)/shard_map/reshape | solution.py:70
  136.2 3.2 gather_fusion.4
  139.4 15.9 %fusion.24 = f32[64,2,8,128]{3,2,1,0:T(8,128)} fusion(f32[64,1024,128]{2,1,0:T(8,128)} %add_multiply_fusion, f32[64,8,2,8,128]{4,3,2,1,0:T(8,128)} %bitcast.180), kind=kOutput, calls=%fused_computation.171 | convolution fusion | flops 805306368 | bytes 38273024 | tf_op jit(solution)/shard_map/rkc,drk->drc/dot_general | solution.py:72
  158.1 3.1 collective-permute-start.6
  161.2 1.5 collective-permute-start.7
  163.9 1.9 squeeze.47
  166.8 3.8 %collective-permute-done.7 = f32[8,8192]{1,0:T(8,128)} collective-permute-done((f32[8,8192]{1,0:T(8,128)}, f32[8,8192]{1,0:T(8,128)}, u32[]{:S(2)}, u32[]{:S(2)}) %collective-permute-start.7) | collective-permute-done | bytes 262176 | tf_op jit(solution)/shard_map/ppermute | solution.py:43
  170.6 12.5 %copy_bitcast_fusion.2 = f32[16,64,128]{2,0,1:T(8,128)S(1)} fusion(f32[16,8192]{1,0:T(8,128)} %copy-done.3, f32[8,8192]{1,0:T(8,128)} %collective-permute-done.7, f32[8,8192]{1,0:T(8,128)S(1)} %collective-permute-done.6, f32[]{:T(128)} %bitcast.10, f32[]{:T(128)} %bitcast.9, f32[]{:T(128)} %bitcast.8, f32[]{:T(128)} %bitcast.7, f32[]{:T(128)} %bitcast.6, ...), kind=kLoop, calls=%fused_computation.371 | loop fusion | flops 5373952 | bytes 1572900 | tf_op jit(solution)/shard_map/reshape | solution.py:70
  183.1 3.2 gather_fusion.5
  186.3 17.0 %fusion.251 = (f32[]{:T(128)}, f32[64,16,128]{2,1,0:T(8,128)}) fusion(f32[16,64,128]{2,1,0:T(8,128)} %squeeze.47, f32[64,16,128]{2,1,0:T(8,128)S(1)} %fusion.12, f32[64,1024,128]{2,1,0:T(8,128)} %add_multiply_fusion, f32[64,8,2,8,128]{4,3,2,1,0:T(8,128)} %bitcast.182), kind=kOutput, calls=%fused_computation.423 | convolution fusion | flops 805961728 | bytes 39321604 | tf_op jit(solution)/shard_map/rkc,drk->drc/dot_general | solution.py:72
  203.3 2.1 copy.48
  206.5 3.0 multiply_reduce_fusion.1
  209.6 4.9 %stack.50 = f32[8]{0:T(128)S(1)} concatenate(f32[1]{0:T(128)} %bitcast.25, f32[1]{0:T(128)} %bitcast.32, f32[1]{0:T(128)} %bitcast.33, f32[1]{0:T(128)} %bitcast.25, f32[1]{0:T(128)} %bitcast.25, f32[1]{0:T(128)} %bitcast.25, f32[1]{0:T(128)} %bitcast.25, f32[1]{0:T(128)} %bitcast.25), dimensions={0} | concatenate | bytes 64 | tf_op jit(solution)/shard_map/stack | solution.py:157
  215.1 8.1 %shard_map.86.x_ref = f32[8,128]{1,0:T(8,128)} custom-call(f32[8,128]{1,0:T(8,128)} %add.444.x_ref), custom_call_target="tpu_custom_call" | custom-call | tf_op jit(solution)/shard_map/pallas_call | solution.py:142
  223.2 11.0 %shard_map.87 = f32[8,128]{1,0:T(8,128)} custom-call(f32[8,128]{1,0:T(8,128)} %shard_map.86.x_ref), custom_call_target="tpu_custom_call" | custom-call | tf_op jit(solution)/shard_map/pallas_call | solution.py:142
  240.1 2.5 collective-permute-start.8
  243.9 4.5 %collective-permute-done.8 = f32[8,8192]{1,0:T(8,128)S(1)} collective-permute-done((f32[8,8192]{1,0:T(8,128)S(1)}, f32[8,8192]{1,0:T(8,128)S(1)}, u32[]{:S(2)}, u32[]{:S(2)}) %collective-permute-start.8) | collective-permute-done | bytes 262176 | tf_op jit(solution)/shard_map/ppermute | solution.py:42
  248.4 4.1 %collective-permute-done.9 = f32[8,8192]{1,0:T(8,128)S(1)} collective-permute-done((f32[8,8192]{1,0:T(8,128)S(1)}, f32[8,8192]{1,0:T(8,128)S(1)}, u32[]{:S(2)}, u32[]{:S(2)}) %collective-permute-start.9) | collective-permute-done | bytes 262176 | tf_op jit(solution)/shard_map/ppermute | solution.py:43
  252.5 7.1 %copy_bitcast_fusion.1 = f32[16,64,128]{2,0,1:T(8,128)S(1)} fusion(f32[16,8192]{1,0:T(8,128)S(1)} %fusion.220, f32[8,8192]{1,0:T(8,128)S(1)} %collective-permute-done.9, f32[8,8192]{1,0:T(8,128)S(1)} %collective-permute-done.8, f32[]{:T(128)} %bitcast.10, f32[]{:T(128)} %bitcast.9, f32[]{:T(128)} %bitcast.8, f32[]{:T(128)} %bitcast.7, f32[]{:T(128)} %bitcast.6, ...), kind=kLoop, calls=%fused_computation.370 | loop fusion | flops 5373952 | bytes 1572900 | tf_op jit(solution)/shard_map/reshape | solution.py:70
  259.6 3.2 gather_fusion.6
  262.8 15.0 %fusion.27 = f32[64,2,8,128]{3,2,1,0:T(8,128)S(1)} fusion(f32[64,1024,128]{2,1,0:T(8,128)} %add_multiply_fusion, f32[64,8,2,8,128]{4,3,2,1,0:T(8,128)} %bitcast.181), kind=kOutput, calls=%fused_computation.172 | convolution fusion | flops 805306368 | bytes 38273024 | tf_op jit(solution)/shard_map/rkc,drk->drc/dot_general | solution.py:72
  277.9 3.1 collective-permute-start.10
  281.1 1.6 collective-permute-start.11
  282.6 3.1 collective-permute-done.10
  285.7 4.1 %collective-permute-done.11 = f32[8,8192]{1,0:T(8,128)S(1)} collective-permute-done((f32[8,8192]{1,0:T(8,128)S(1)}, f32[8,8192]{1,0:T(8,128)S(1)}, u32[]{:S(2)}, u32[]{:S(2)}) %collective-permute-start.11) | collective-permute-done | bytes 262176 | tf_op jit(solution)/shard_map/ppermute | solution.py:43
  289.8 7.1 %copy_bitcast_fusion = f32[16,64,128]{2,0,1:T(8,128)S(1)} fusion(f32[16,8192]{1,0:T(8,128)S(1)} %bitcast_multiply_fusion, f32[8,8192]{1,0:T(8,128)S(1)} %collective-permute-done.11, f32[8,8192]{1,0:T(8,128)S(1)} %collective-permute-done.10, f32[]{:T(128)} %bitcast.10, f32[]{:T(128)} %bitcast.9, f32[]{:T(128)} %bitcast.8, f32[]{:T(128)} %bitcast.7, ...), kind=kLoop, calls=%fused_computation.369 | loop fusion | flops 5373952 | bytes 1572900 | tf_op jit(solution)/shard_map/reshape | solution.py:70
  296.9 3.2 gather_fusion.7
  300.1 15.1 %fusion.30 = f32[16,64,128]{2,0,1:T(8,128)S(1)} fusion(f32[64,1024,128]{2,1,0:T(8,128)} %add_multiply_fusion, f32[64,8,2,8,128]{4,3,2,1,0:T(8,128)} %bitcast.178), kind=kOutput, calls=%fused_computation.173 | convolution fusion | flops 805306368 | bytes 38273024 | tf_op jit(solution)/shard_map/rkc,drk->drc/dot_general | solution.py:72
  318.0 8.3 %shard_map.88.x_ref = f32[8,128]{1,0:T(8,128)} custom-call(f32[8,128]{1,0:T(8,128)} %add.481.x_ref), custom_call_target="tpu_custom_call" | custom-call | tf_op jit(solution)/shard_map/pallas_call | solution.py:142
  326.3 10.4 %shard_map.89 = f32[8,128]{1,0:T(8,128)} custom-call(f32[8,128]{1,0:T(8,128)} %shard_map.88.x_ref), custom_call_target="tpu_custom_call" | custom-call | tf_op jit(solution)/shard_map/pallas_call | solution.py:142
  339.4 19.5 %all_to_all.10 = f32[8,2,16,1024]{3,2,1,0:T(8,128)S(1)} all-to-all(f32[8,2,16,1024]{3,2,1,0:T(8,128)S(1)} %maximum_bitcast_fusion), channel_id=1, replica_groups=mesh['space'=8,'tm'=16] {'space'}, dimensions={0} | all-to-all | bytes 2097152 | tf_op jit(solution)/shard_map/all_to_all | solution.py:93
  (72 shorter events, 31.2 us)
Async XLA Ops:
  0.6 12.6 %copy-start.2 = (f32[128,1024]{1,0:T(8,128)S(1)}, f32[128,1024]{1,0:T(8,128)}, u32[]{:S(2)}) copy-start(f32[128,1024]{1,0:T(8,128)} %param.7) | copy-start | bytes 1572868
  1.5 11.7 %collective-permute-start = (f32[8,1024]{1,0:T(8,128)S(1)}, f32[8,1024]{1,0:T(8,128)S(1)}, u32[]{:S(2)}, u32[]{:S(2)}) collective-permute-start(f32[8,1024]{1,0:T(8,128)S(1)} %get-tuple-element.26), channel_id=1, source_target_pairs={{0,1},{1,2},{2,3},{3,4},{4,5},{5,6},{6,7},{7,8},{8,9},{9,10},{10,1... | collective-permute-start | bytes 98312 | tf_op jit(solution)/shard_map/ppermute | solution.py:51
  2.8 10.5 %collective-permute-start.1 = (f32[8,1024]{1,0:T(8,128)S(1)}, f32[8,1024]{1,0:T(8,128)S(1)}, u32[]{:S(2)}, u32[]{:S(2)}) collective-permute-start(f32[8,1024]{1,0:T(8,128)S(1)} %get-tuple-element.27), channel_id=1, source_target_pairs={{1,0},{2,1},{3,2},{4,3},{5,4},{6,5},{7,6},{8,7},{9,8},{10,9},{11,1... | collective-permute-start | bytes 98312 | tf_op jit(solution)/shard_map/ppermute | solution.py:52
  21.9 33.7 %all-to-all-start = ((f32[8,3,16,1024]{3,2,1,0:T(8,128)}), f32[8,3,16,1024]{3,2,1,0:T(8,128)S(1)}, u32[]{:S(2)}, u32[]{:S(2)}) async-start(f32[8,3,16,1024]{3,2,1,0:T(8,128)} %gather_fusion), calls=%async_computation | async-start | bytes 3145728 | tf_op jit(solution)/shard_map/all_to_all | solution.py:85
  56.5 24.5 %copy-start.5 = (f32[1,16,8,1024]{3,1,0,2:T(8,128)}, f32[1,16,8,1024]{3,1,0,2:T(8,128)S(1)}, u32[]{:S(2)}) copy-start(f32[1,16,8,1024]{3,1,0,2:T(8,128)S(1)} %get-tuple-element.9) | copy-start | bytes 1572868
  57.2 3.2 copy-start.8
  75.7 9.6 %collective-permute-start.2 = (f32[8,8192]{1,0:T(8,128)S(1)}, f32[8,8192]{1,0:T(8,128)S(1)}, u32[]{:S(2)}, u32[]{:S(2)}) collective-permute-start(f32[8,8192]{1,0:T(8,128)S(1)} %get-tuple-element.22), channel_id=1, source_target_pairs={{0,16},{16,32},{32,48},{48,112},{112,96},{96,80},{80,64},{64,1},{1... | collective-permute-start | bytes 786440 | tf_op jit(solution)/shard_map/ppermute | solution.py:42
  79.5 10.5 %collective-permute-start.3 = (f32[8,8192]{1,0:T(8,128)S(1)}, f32[8,8192]{1,0:T(8,128)S(1)}, u32[]{:S(2)}, u32[]{:S(2)}) collective-permute-start(f32[8,8192]{1,0:T(8,128)S(1)} %get-tuple-element.23), channel_id=1, source_target_pairs={{16,0},{32,16},{48,32},{112,48},{96,112},{80,96},{64,80},{1,64},{1... | collective-permute-start | bytes 786440 | tf_op jit(solution)/shard_map/ppermute | solution.py:43
  100.3 15.1 %copy-start.7 = (f32[2,8,8,1024]{3,1,2,0:T(8,128)S(1)}, f32[2,8,8,1024]{3,1,2,0:T(8,128)}, u32[]{:S(2)}) copy-start(f32[2,8,8,1024]{3,1,2,0:T(8,128)} %copy.93) | copy-start | bytes 1572868
  115.5 13.7 %copy-start = (f32[16,8192]{1,0:T(8,128)}, f32[16,8192]{1,0:T(8,128)S(1)}, u32[]{:S(2)}) copy-start(f32[16,8192]{1,0:T(8,128)S(1)} %fusion.221) | copy-start | bytes 1572868
  115.6 9.5 %collective-permute-start.4 = (f32[8,8192]{1,0:T(8,128)S(1)}, f32[8,8192]{1,0:T(8,128)S(1)}, u32[]{:S(2)}, u32[]{:S(2)}) collective-permute-start(f32[8,8192]{1,0:T(8,128)S(1)} %get-tuple-element.20), channel_id=1, source_target_pairs={{0,16},{16,32},{32,48},{48,112},{112,96},{96,80},{80,64},{64,1},{1... | collective-permute-start | bytes 786440 | tf_op jit(solution)/shard_map/ppermute | solution.py:42
  118.9 10.2 %collective-permute-start.5 = (f32[8,8192]{1,0:T(8,128)S(1)}, f32[8,8192]{1,0:T(8,128)S(1)}, u32[]{:S(2)}, u32[]{:S(2)}) collective-permute-start(f32[8,8192]{1,0:T(8,128)S(1)} %get-tuple-element.21), channel_id=1, source_target_pairs={{16,0},{32,16},{48,32},{112,48},{96,112},{80,96},{64,80},{1,64},{1... | collective-permute-start | bytes 786440 | tf_op jit(solution)/shard_map/ppermute | solution.py:43
  139.4 23.3 %copy-start.6 = (f32[1,16,8,1024]{3,1,0,2:T(8,128)S(1)}, f32[1,16,8,1024]{3,1,0,2:T(8,128)}, u32[]{:S(2)}) copy-start(f32[1,16,8,1024]{3,1,0,2:T(8,128)} %copy-done.5) | copy-start | bytes 1572868
  156.5 0.8 copy-start.3
  158.1 8.7 %collective-permute-start.6 = (f32[8,8192]{1,0:T(8,128)}, f32[8,8192]{1,0:T(8,128)S(1)}, u32[]{:S(2)}, u32[]{:S(2)}) collective-permute-start(f32[8,8192]{1,0:T(8,128)} %get-tuple-element.18), channel_id=1, source_target_pairs={{0,16},{16,32},{32,48},{48,112},{112,96},{96,80},{80,64},{64,1},{1... | collective-permute-start | bytes 786440 | tf_op jit(solution)/shard_map/ppermute | solution.py:42
  161.2 9.4 %collective-permute-start.7 = (f32[8,8192]{1,0:T(8,128)}, f32[8,8192]{1,0:T(8,128)}, u32[]{:S(2)}, u32[]{:S(2)}) collective-permute-start(f32[8,8192]{1,0:T(8,128)} %get-tuple-element.19), channel_id=1, source_target_pairs={{16,0},{32,16},{48,32},{112,48},{96,112},{80,96},{64,80},{1,64},{1... | collective-permute-start | bytes 786440 | tf_op jit(solution)/shard_map/ppermute | solution.py:43
  203.3 35.6 %copy-start.1 = (f32[16,8192]{1,0:T(8,128)S(1)}, f32[16,8192]{1,0:T(8,128)}, u32[]{:S(2)}) copy-start(f32[16,8192]{1,0:T(8,128)} %copy-done) | copy-start | bytes 1572868
  240.1 8.3 %collective-permute-start.8 = (f32[8,8192]{1,0:T(8,128)S(1)}, f32[8,8192]{1,0:T(8,128)S(1)}, u32[]{:S(2)}, u32[]{:S(2)}) collective-permute-start(f32[8,8192]{1,0:T(8,128)S(1)} %get-tuple-element.16), channel_id=1, source_target_pairs={{0,16},{16,32},{32,48},{48,112},{112,96},{96,80},{80,64},{64,1},{1... | collective-permute-start | bytes 786440 | tf_op jit(solution)/shard_map/ppermute | solution.py:42
  242.6 9.9 %collective-permute-start.9 = (f32[8,8192]{1,0:T(8,128)S(1)}, f32[8,8192]{1,0:T(8,128)S(1)}, u32[]{:S(2)}, u32[]{:S(2)}) collective-permute-start(f32[8,8192]{1,0:T(8,128)S(1)} %get-tuple-element.17), channel_id=1, source_target_pairs={{16,0},{32,16},{48,32},{112,48},{96,112},{80,96},{64,80},{1,64},{1... | collective-permute-start | bytes 786440 | tf_op jit(solution)/shard_map/ppermute | solution.py:43
  277.9 7.8 %collective-permute-start.10 = (f32[8,8192]{1,0:T(8,128)S(1)}, f32[8,8192]{1,0:T(8,128)S(1)}, u32[]{:S(2)}, u32[]{:S(2)}) collective-permute-start(f32[8,8192]{1,0:T(8,128)S(1)} %get-tuple-element.14), channel_id=1, source_target_pairs={{0,16},{16,32},{32,48},{48,112},{112,96},{96,80},{80,64},{64,1},{1... | collective-permute-start | bytes 786440 | tf_op jit(solution)/shard_map/ppermute | solution.py:42
  281.1 8.8 %collective-permute-start.11 = (f32[8,8192]{1,0:T(8,128)S(1)}, f32[8,8192]{1,0:T(8,128)S(1)}, u32[]{:S(2)}, u32[]{:S(2)}) collective-permute-start(f32[8,8192]{1,0:T(8,128)S(1)} %get-tuple-element.15), channel_id=1, source_target_pairs={{16,0},{32,16},{48,32},{112,48},{96,112},{80,96},{64,80},{1,64},{1... | collective-permute-start | bytes 786440 | tf_op jit(solution)/shard_map/ppermute | solution.py:43
  300.1 15.4 %copy-start.4 = (f32[1,16,8,1024]{3,1,0,2:T(8,128)S(1)}, f32[1,16,8,1024]{3,1,0,2:T(8,128)}, u32[]{:S(2)}) copy-start(f32[1,16,8,1024]{3,1,0,2:T(8,128)} %get-tuple-element.6) | copy-start | bytes 1572868

commit v4 on v1

--- a/solution.py
+++ b/solution.py
@@ -34,7 +34,7 @@
 
 def day_order_halo(field):
     spaces, times = lax.axis_size("space"), lax.axis_size("tm")
-    place = [(rank % spaces) * times + rank // spaces for rank in range(spaces * times)]
+    place = [snake(spaces, rank // spaces % 2 == 1)[rank % spaces] * times + rank // spaces for rank in range(spaces * times)]
     forward = [(place[i], place[i + 1]) for i in range(len(place) - 1)]
     backward = [(place[i + 1], place[i]) for i in range(len(place) - 1)]
     axes = ("space", "tm")
@@ -72,10 +72,27 @@
     return out.reshape(day_count, blocks * BLOCK)
 
 
+def snake(spaces, odd):
+    half = spaces // 2
+    order = [i if i < half else spaces + half - 1 - i for i in range(spaces)]
+    return order[::-1] if odd else order
+
+
+def chain_of(spaces, odd):
+    order = snake(spaces, odd)
+    return [order.index(i) for i in range(spaces)]
+
+
+def row_pick(table_even, table_odd):
+    odd = lax.rem(lax.axis_index("tm"), 2) == 1
+    return jnp.where(odd, jnp.array(table_odd), jnp.array(table_even))
+
+
 def to_days(field):
     n = lax.axis_size("space")
     k, days, cells = field.shape
-    chunked = field.reshape(k, n, days // n, cells).transpose(1, 0, 2, 3)
+    picks = row_pick(chain_of(n, False), chain_of(n, True))
+    chunked = field.reshape(k, n, days // n, cells)[:, picks].transpose(1, 0, 2, 3)
     got = lax.all_to_all(chunked, "space", split_axis=0, concat_axis=0, tiled=True)
     return got.transpose(1, 2, 0, 3).reshape(k, days // n, n * cells)
 
@@ -85,7 +102,8 @@
     k, days, cells = field.shape
     chunked = field.reshape(k, days, n, cells // n).transpose(2, 0, 1, 3)
     got = lax.all_to_all(chunked, "space", split_axis=0, concat_axis=0, tiled=True)
-    return got.transpose(1, 0, 2, 3).reshape(k, n * days, cells // n)
+    picks = row_pick(snake(n, False), snake(n, True))
+    return got[picks].transpose(1, 0, 2, 3).reshape(k, n * days, cells // n)
 
 
 def group_sum_kernel(axis, x_ref, o_ref, slots, send, recv):

time: 373 us -> 369 us (0.989)
  blocking collectives: 20 us -> 0 us
  Pallas kernels: 44 us -> 50.3 us
  waiting for transfers between devices: 40.2 us -> 45.2 us
    all_to_all x1 -> x0, blocking collectives: 20 us -> none  [to_cells(): lax.all_to_all(chunked, 'space', split_axis=0, concat_axis=0, tiled=True)]
    all_to_all x0 -> x1, waiting for transfers between devices: none -> 15.3 us  [to_cells(): lax.all_to_all(chunked, 'space', split_axis=0, concat_axis=0, tiled=True)]
    ppermute x5, waiting for transfers between devices: 19 us -> 10.4 us  [day_order_halo(): low = lax.ppermute(field[field.shape[0] - BW:], axes, forward)]
    pallas_call x4, Pallas kernels: 44 us -> 50.3 us  [group_sum(): pl.pallas_call(functools.partial(group_sum_kernel, axis), out_shape=jax.S...]
  transfers between devices with their start and end apart: 13 -> 14, of which waited for: 10 -> 10; matrix products, arithmetic and copies ran while one was open for 10% -> 11% of each run, Pallas kernels for 0% -> 0%
where the time goes in v4:
time: 369 us; the launch traced here: 367 us
  matrix products  93.3 us (25%)
  other arithmetic  85.7 us (23%)
  local copies, waits for them, and re-layouts  51.3 us (14%)
  Pallas kernels  50.3 us (14%)
  waiting for transfers between devices  45.2 us (12%)
  starting transfers between devices  35.9 us (10%)
  between operations  5.27 us (1%)
    dot_general x6, matrix products, block_product(): jnp.einsum('rkc,drk->drc', weights, picked, precision=lax.Precision.HIGH)  93.3 us
    pallas_call x4, Pallas kernels, group_sum(): pl.pallas_call(functools.partial(group_sum_kernel, axis), out_shape=jax.S...  50.3 us
    reshape x5, other arithmetic, block_product(): blocked = field.reshape(day_count, blocks, BLOCK)  41.2 us
    mul x1, other arithmetic, wendland(): return amplitude * remain ** 4 * (1.0 + 4.0 * scaled)  26.8 us
    ppermute x5, waiting for transfers between devices, day_order_halo(): high = lax.ppermute(field[:BW], axes, backward)  19.5 us
    gather x6, local copies, waits for them, and re-layouts, block_product(): blocked[:, pattern].reshape(day_count, blocks, pattern.shape[1] * BLOCK)  19.2 us
    ppermute x5, starting transfers between devices, day_order_halo(): low = lax.ppermute(field[field.shape[0] - BW:], axes, forward)  15.8 us
    all_to_all x1, waiting for transfers between devices, to_cells(): lax.all_to_all(chunked, 'space', split_axis=0, concat_axis=0, tiled=True)  15.3 us
  transfers between devices with their start and end apart: 14, of which 10 were waited for; matrix products, arithmetic and copies ran while one was open for 11% of the time, Pallas kernels for 0%

profile of v4, /device:TPU:0, one launch (start us, length us, event | category | flops | bytes accessed | tf_op | source)
XLA Modules:
  0.0 366.9 jit_solution(7452717743293013061)
XLA Ops:
  6.6 2.3 gather_fusion.2
  10.3 1.7 fusion.262
  13.4 6.7 %fusion.233 = f32[128,1024]{1,0:T(8,128)S(1)} fusion(f32[136,1024]{1,0:T(8,128)S(1)} %constant_dynamic-update-slice_fusion.2, f32[136,1024]{1,0:T(8,128)S(1)} %get-tuple-element.24, f32[128,1024]{1,0:T(8,128)S(1)} %copy-done.2, f32[]{:T(128)} %bitcast.10, f32[]{:T(128)} %bitcast.9, f32[]{:T(128)} %bitcast.8, f32[]{:T(128)} %bitcast.7, f32[]{:T(128)} %bitcast.6, ...), kind=kLoop, calls=%fused_computation.396 | loop fusion | flops 3276800 | bytes 9437220 | tf_op jit(solution)/shard_map/add | solution.py:60
  20.2 1.8 gather_fusion
  22.0 6.9 %all-to-all-start = ((f32[8,3,16,1024]{3,2,1,0:T(8,128)}), f32[8,3,16,1024]{3,2,1,0:T(8,128)S(1)}, u32[]{:S(2)}, u32[]{:S(2)}) async-start(f32[8,3,16,1024]{3,2,1,0:T(8,128)} %gather_fusion), calls=%async_computation | async-start | bytes 3145728 | tf_op jit(solution)/shard_map/all_to_all | solution.py:96
  28.9 26.8 %add_multiply_fusion = f32[64,1024,128]{2,1,0:T(8,128)} fusion(f32[64,1024]{1,0:T(8,128)S(1)} %bitcast.197, f32[64,128]{1,0:T(8,128)S(1)} %bitcast.204, f32[64,1024]{1,0:T(8,128)S(1)} %bitcast.198, f32[64,128]{1,0:T(8,128)S(1)} %bitcast.203), kind=kLoop, calls=%fused_computation.9 | loop fusion | flops 117440512 | bytes 34144256 | tf_op jit(solution)/shard_map/mul | solution.py:21
  57.4 3.2 gather_fusion.1
  60.6 15.1 %fusion.21 = f32[64,2,8,128]{3,2,1,0:T(8,128)S(1)} fusion(f32[64,1024,128]{2,1,0:T(8,128)} %add_multiply_fusion, f32[64,8,2,8,128]{4,3,2,1,0:T(8,128)} %bitcast.177), kind=kOutput, calls=%fused_computation.170 | convolution fusion | flops 805306368 | bytes 38273024 | tf_op jit(solution)/shard_map/rkc,drk->drc/dot_general | solution.py:71
  75.8 3.8 %collective-permute-start.2 = (f32[8,8192]{1,0:T(8,128)S(1)}, f32[8,8192]{1,0:T(8,128)S(1)}, u32[]{:S(2)}, u32[]{:S(2)}) collective-permute-start(f32[8,8192]{1,0:T(8,128)S(1)} %get-tuple-element.22), channel_id=1, source_target_pairs={{0,16},{16,32},{32,48},{48,112},{112,96},{96,80},{80,64},{64,65},{... | collective-permute-start | bytes 786440 | tf_op jit(solution)/shard_map/ppermute | solution.py:41
  82.0 1.5 collective-permute-done.2
  83.6 4.6 %collective-permute-done.3 = f32[8,8192]{1,0:T(8,128)S(1)} collective-permute-done((f32[8,8192]{1,0:T(8,128)S(1)}, f32[8,8192]{1,0:T(8,128)S(1)}, u32[]{:S(2)}, u32[]{:S(2)}) %collective-permute-start.3) | collective-permute-done | bytes 262176 | tf_op jit(solution)/shard_map/ppermute | solution.py:42
  88.1 7.2 %copy_bitcast_fusion.4 = f32[16,64,128]{2,0,1:T(8,128)S(1)} fusion(f32[16,8192]{1,0:T(8,128)S(1)} %bitcast_subtract_fusion, f32[8,8192]{1,0:T(8,128)S(1)} %collective-permute-done.3, f32[8,8192]{1,0:T(8,128)S(1)} %collective-permute-done.2, f32[]{:T(128)} %bitcast.10, f32[]{:T(128)} %bitcast.9, f32[]{:T(128)} %bitcast.8, f32[]{:T(128)} %bitcast.7, ...), kind=kLoop, calls=%fused_computation.373 | loop fusion | flops 5373952 | bytes 1572900 | tf_op jit(solution)/shard_map/reshape | solution.py:69
  95.3 3.2 gather_fusion.3
  98.5 15.1 %fusion.12 = f32[64,16,128]{2,1,0:T(8,128)S(1)} fusion(f32[64,1024,128]{2,1,0:T(8,128)} %add_multiply_fusion, f32[64,8,2,8,128]{4,3,2,1,0:T(8,128)} %bitcast.179), kind=kOutput, calls=%fused_computation.22 | convolution fusion | flops 805306368 | bytes 38273024 | tf_op jit(solution)/shard_map/rkc,drk->drc/dot_general | solution.py:71
  113.8 3.6 collective-permute-start.4
  118.6 2.6 collective-permute-done.4
  121.2 4.4 %collective-permute-done.5 = f32[8,8192]{1,0:T(8,128)S(1)} collective-permute-done((f32[8,8192]{1,0:T(8,128)S(1)}, f32[8,8192]{1,0:T(8,128)S(1)}, u32[]{:S(2)}, u32[]{:S(2)}) %collective-permute-start.5) | collective-permute-done | bytes 262176 | tf_op jit(solution)/shard_map/ppermute | solution.py:42
  125.6 7.2 %copy_bitcast_fusion.3 = f32[16,64,128]{2,0,1:T(8,128)S(1)} fusion(f32[16,8192]{1,0:T(8,128)S(1)} %fusion.221, f32[8,8192]{1,0:T(8,128)S(1)} %collective-permute-done.5, f32[8,8192]{1,0:T(8,128)S(1)} %collective-permute-done.4, f32[]{:T(128)} %bitcast.10, f32[]{:T(128)} %bitcast.9, f32[]{:T(128)} %bitcast.8, f32[]{:T(128)} %bitcast.7, f32[]{:T(128)} %bitcast.6, ...), kind=kLoop, calls=%fused_computation.372 | loop fusion | flops 5373952 | bytes 1572900 | tf_op jit(solution)/shard_map/reshape | solution.py:69
  132.8 3.2 gather_fusion.4
  136.0 15.9 %fusion.24 = f32[64,2,8,128]{3,2,1,0:T(8,128)} fusion(f32[64,1024,128]{2,1,0:T(8,128)} %add_multiply_fusion, f32[64,8,2,8,128]{4,3,2,1,0:T(8,128)} %bitcast.180), kind=kOutput, calls=%fused_computation.171 | convolution fusion | flops 805306368 | bytes 38273024 | tf_op jit(solution)/shard_map/rkc,drk->drc/dot_general | solution.py:71
  154.7 3.4 collective-permute-start.6
  160.7 1.9 squeeze.47
  163.7 3.2 collective-permute-done.7
  166.9 12.4 %copy_bitcast_fusion.2 = f32[16,64,128]{2,0,1:T(8,128)S(1)} fusion(f32[16,8192]{1,0:T(8,128)} %copy-done.3, f32[8,8192]{1,0:T(8,128)} %collective-permute-done.7, f32[8,8192]{1,0:T(8,128)S(1)} %collective-permute-done.6, f32[]{:T(128)} %bitcast.10, f32[]{:T(128)} %bitcast.9, f32[]{:T(128)} %bitcast.8, f32[]{:T(128)} %bitcast.7, f32[]{:T(128)} %bitcast.6, ...), kind=kLoop, calls=%fused_computation.371 | loop fusion | flops 5373952 | bytes 1572900 | tf_op jit(solution)/shard_map/reshape | solution.py:69
  179.2 3.2 gather_fusion.5
  182.5 17.0 %fusion.251 = (f32[]{:T(128)}, f32[64,16,128]{2,1,0:T(8,128)}) fusion(f32[16,64,128]{2,1,0:T(8,128)} %squeeze.47, f32[64,16,128]{2,1,0:T(8,128)S(1)} %fusion.12, f32[64,1024,128]{2,1,0:T(8,128)} %add_multiply_fusion, f32[64,8,2,8,128]{4,3,2,1,0:T(8,128)} %bitcast.182), kind=kOutput, calls=%fused_computation.423 | convolution fusion | flops 805961728 | bytes 39321604 | tf_op jit(solution)/shard_map/rkc,drk->drc/dot_general | solution.py:71
  199.5 2.1 copy.50
  202.7 3.0 multiply_reduce_fusion.1
  205.7 4.7 %stack.50 = f32[8]{0:T(128)S(1)} concatenate(f32[1]{0:T(128)} %bitcast.25, f32[1]{0:T(128)} %bitcast.32, f32[1]{0:T(128)} %bitcast.33, f32[1]{0:T(128)} %bitcast.25, f32[1]{0:T(128)} %bitcast.25, f32[1]{0:T(128)} %bitcast.25, f32[1]{0:T(128)} %bitcast.25, f32[1]{0:T(128)} %bitcast.25), dimensions={0} | concatenate | bytes 64 | tf_op jit(solution)/shard_map/stack | solution.py:169
  211.1 7.5 %shard_map.104.x_ref = f32[8,128]{1,0:T(8,128)} custom-call(f32[8,128]{1,0:T(8,128)} %add.444.x_ref), custom_call_target="tpu_custom_call" | custom-call | tf_op jit(solution)/shard_map/pallas_call | solution.py:154
  218.6 21.1 %shard_map.105 = f32[8,128]{1,0:T(8,128)} custom-call(f32[8,128]{1,0:T(8,128)} %shard_map.104.x_ref), custom_call_target="tpu_custom_call" | custom-call | tf_op jit(solution)/shard_map/pallas_call | solution.py:154
  245.8 2.5 collective-permute-start.8
  249.6 3.2 collective-permute-done.8
  252.8 3.8 %collective-permute-done.9 = f32[8,8192]{1,0:T(8,128)S(1)} collective-permute-done((f32[8,8192]{1,0:T(8,128)S(1)}, f32[8,8192]{1,0:T(8,128)S(1)}, u32[]{:S(2)}, u32[]{:S(2)}) %collective-permute-start.9) | collective-permute-done | bytes 262176 | tf_op jit(solution)/shard_map/ppermute | solution.py:42
  256.6 7.2 %copy_bitcast_fusion.1 = f32[16,64,128]{2,0,1:T(8,128)S(1)} fusion(f32[16,8192]{1,0:T(8,128)S(1)} %fusion.220, f32[8,8192]{1,0:T(8,128)S(1)} %collective-permute-done.9, f32[8,8192]{1,0:T(8,128)S(1)} %collective-permute-done.8, f32[]{:T(128)} %bitcast.10, f32[]{:T(128)} %bitcast.9, f32[]{:T(128)} %bitcast.8, f32[]{:T(128)} %bitcast.7, f32[]{:T(128)} %bitcast.6, ...), kind=kLoop, calls=%fused_computation.370 | loop fusion | flops 5373952 | bytes 1572900 | tf_op jit(solution)/shard_map/reshape | solution.py:69
  263.8 3.2 gather_fusion.6
  267.0 15.0 %fusion.27 = f32[64,2,8,128]{3,2,1,0:T(8,128)S(1)} fusion(f32[64,1024,128]{2,1,0:T(8,128)} %add_multiply_fusion, f32[64,8,2,8,128]{4,3,2,1,0:T(8,128)} %bitcast.181), kind=kOutput, calls=%fused_computation.172 | convolution fusion | flops 805306368 | bytes 38273024 | tf_op jit(solution)/shard_map/rkc,drk->drc/dot_general | solution.py:71
  282.1 2.5 collective-permute-start.10
  284.7 1.6 collective-permute-start.11
  286.2 3.1 collective-permute-done.10
  289.4 3.6 collective-permute-done.11
  292.9 7.2 %copy_bitcast_fusion = f32[16,64,128]{2,0,1:T(8,128)S(1)} fusion(f32[16,8192]{1,0:T(8,128)S(1)} %bitcast_multiply_fusion, f32[8,8192]{1,0:T(8,128)S(1)} %collective-permute-done.11, f32[8,8192]{1,0:T(8,128)S(1)} %collective-permute-done.10, f32[]{:T(128)} %bitcast.10, f32[]{:T(128)} %bitcast.9, f32[]{:T(128)} %bitcast.8, f32[]{:T(128)} %bitcast.7, ...), kind=kLoop, calls=%fused_computation.369 | loop fusion | flops 5373952 | bytes 1572900 | tf_op jit(solution)/shard_map/reshape | solution.py:69
  300.1 3.2 gather_fusion.7
  303.3 15.1 %fusion.30 = f32[16,64,128]{2,0,1:T(8,128)S(1)} fusion(f32[64,1024,128]{2,1,0:T(8,128)} %add_multiply_fusion, f32[64,8,2,8,128]{4,3,2,1,0:T(8,128)} %bitcast.178), kind=kOutput, calls=%fused_computation.173 | convolution fusion | flops 805306368 | bytes 38273024 | tf_op jit(solution)/shard_map/rkc,drk->drc/dot_general | solution.py:71
  321.2 8.1 %shard_map.106.x_ref = f32[8,128]{1,0:T(8,128)} custom-call(f32[8,128]{1,0:T(8,128)} %add.481.x_ref), custom_call_target="tpu_custom_call" | custom-call | tf_op jit(solution)/shard_map/pallas_call | solution.py:154
  329.3 13.5 %shard_map.107 = f32[8,128]{1,0:T(8,128)} custom-call(f32[8,128]{1,0:T(8,128)} %shard_map.106.x_ref), custom_call_target="tpu_custom_call" | custom-call | tf_op jit(solution)/shard_map/pallas_call | solution.py:154
  346.4 3.6 all-to-all-start.1
  350.0 15.3 %all-to-all-done.1 = f32[8,2,16,1024]{3,2,1,0:T(8,128)S(1)} async-done(((f32[8,2,16,1024]{3,2,1,0:T(8,128)}), f32[8,2,16,1024]{3,2,1,0:T(8,128)S(1)}, u32[]{:S(2)}, u32[]{:S(2)}) %all-to-all-start.1) | async-done | bytes 1048608 | tf_op jit(solution)/shard_map/all_to_all | solution.py:104
  (75 shorter events, 33.7 us)
Async XLA Ops:
  0.6 12.6 %copy-start.2 = (f32[128,1024]{1,0:T(8,128)S(1)}, f32[128,1024]{1,0:T(8,128)}, u32[]{:S(2)}) copy-start(f32[128,1024]{1,0:T(8,128)} %param.9) | copy-start | bytes 1572868
  1.5 11.7 %collective-permute-start = (f32[8,1024]{1,0:T(8,128)S(1)}, f32[8,1024]{1,0:T(8,128)S(1)}, u32[]{:S(2)}, u32[]{:S(2)}) collective-permute-start(f32[8,1024]{1,0:T(8,128)S(1)} %get-tuple-element.26), channel_id=1, source_target_pairs={{0,1},{1,2},{2,3},{3,4},{4,5},{5,6},{6,7},{7,8},{8,9},{9,10},{10,1... | collective-permute-start | bytes 98312 | tf_op jit(solution)/shard_map/ppermute | solution.py:50
  2.8 10.6 %collective-permute-start.1 = (f32[8,1024]{1,0:T(8,128)S(1)}, f32[8,1024]{1,0:T(8,128)S(1)}, u32[]{:S(2)}, u32[]{:S(2)}) collective-permute-start(f32[8,1024]{1,0:T(8,128)S(1)} %get-tuple-element.27), channel_id=1, source_target_pairs={{1,0},{2,1},{3,2},{4,3},{5,4},{6,5},{7,6},{8,7},{9,8},{10,9},{11,1... | collective-permute-start | bytes 98312 | tf_op jit(solution)/shard_map/ppermute | solution.py:51
  22.0 33.7 %all-to-all-start = ((f32[8,3,16,1024]{3,2,1,0:T(8,128)}), f32[8,3,16,1024]{3,2,1,0:T(8,128)S(1)}, u32[]{:S(2)}, u32[]{:S(2)}) async-start(f32[8,3,16,1024]{3,2,1,0:T(8,128)} %gather_fusion), calls=%async_computation | async-start | bytes 3145728 | tf_op jit(solution)/shard_map/all_to_all | solution.py:96
  56.7 24.5 %copy-start.5 = (f32[1,16,8,1024]{3,1,0,2:T(8,128)}, f32[1,16,8,1024]{3,1,0,2:T(8,128)S(1)}, u32[]{:S(2)}) copy-start(f32[1,16,8,1024]{3,1,0,2:T(8,128)S(1)} %get-tuple-element.9) | copy-start | bytes 1572868
  57.4 3.2 copy-start.8
  75.8 7.7 %collective-permute-start.2 = (f32[8,8192]{1,0:T(8,128)S(1)}, f32[8,8192]{1,0:T(8,128)S(1)}, u32[]{:S(2)}, u32[]{:S(2)}) collective-permute-start(f32[8,8192]{1,0:T(8,128)S(1)} %get-tuple-element.22), channel_id=1, source_target_pairs={{0,16},{16,32},{32,48},{48,112},{112,96},{96,80},{80,64},{64,65},{... | collective-permute-start | bytes 786440 | tf_op jit(solution)/shard_map/ppermute | solution.py:41
  79.7 8.4 %collective-permute-start.3 = (f32[8,8192]{1,0:T(8,128)S(1)}, f32[8,8192]{1,0:T(8,128)S(1)}, u32[]{:S(2)}, u32[]{:S(2)}) collective-permute-start(f32[8,8192]{1,0:T(8,128)S(1)} %get-tuple-element.23), channel_id=1, source_target_pairs={{16,0},{32,16},{48,32},{112,48},{96,112},{80,96},{64,80},{65,64},{... | collective-permute-start | bytes 786440 | tf_op jit(solution)/shard_map/ppermute | solution.py:42
  98.5 15.1 %copy-start.7 = (f32[2,8,8,1024]{3,1,2,0:T(8,128)S(1)}, f32[2,8,8,1024]{3,1,2,0:T(8,128)}, u32[]{:S(2)}) copy-start(f32[2,8,8,1024]{3,1,2,0:T(8,128)} %copy.95) | copy-start | bytes 1572868
  113.7 11.9 %copy-start = (f32[16,8192]{1,0:T(8,128)}, f32[16,8192]{1,0:T(8,128)S(1)}, u32[]{:S(2)}) copy-start(f32[16,8192]{1,0:T(8,128)S(1)} %fusion.221) | copy-start | bytes 1572868
  113.8 7.4 %collective-permute-start.4 = (f32[8,8192]{1,0:T(8,128)S(1)}, f32[8,8192]{1,0:T(8,128)S(1)}, u32[]{:S(2)}, u32[]{:S(2)}) collective-permute-start(f32[8,8192]{1,0:T(8,128)S(1)} %get-tuple-element.20), channel_id=1, source_target_pairs={{0,16},{16,32},{32,48},{48,112},{112,96},{96,80},{80,64},{64,65},{... | collective-permute-start | bytes 786440 | tf_op jit(solution)/shard_map/ppermute | solution.py:41
  117.3 8.3 %collective-permute-start.5 = (f32[8,8192]{1,0:T(8,128)S(1)}, f32[8,8192]{1,0:T(8,128)S(1)}, u32[]{:S(2)}, u32[]{:S(2)}) collective-permute-start(f32[8,8192]{1,0:T(8,128)S(1)} %get-tuple-element.21), channel_id=1, source_target_pairs={{16,0},{32,16},{48,32},{112,48},{96,112},{80,96},{64,80},{65,64},{... | collective-permute-start | bytes 786440 | tf_op jit(solution)/shard_map/ppermute | solution.py:42
  136.0 23.6 %copy-start.6 = (f32[1,16,8,1024]{3,1,0,2:T(8,128)S(1)}, f32[1,16,8,1024]{3,1,0,2:T(8,128)}, u32[]{:S(2)}) copy-start(f32[1,16,8,1024]{3,1,0,2:T(8,128)} %copy-done.5) | copy-start | bytes 1572868
  153.1 0.8 copy-start.3
  154.7 9.0 %collective-permute-start.6 = (f32[8,8192]{1,0:T(8,128)}, f32[8,8192]{1,0:T(8,128)S(1)}, u32[]{:S(2)}, u32[]{:S(2)}) collective-permute-start(f32[8,8192]{1,0:T(8,128)} %get-tuple-element.18), channel_id=1, source_target_pairs={{0,16},{16,32},{32,48},{48,112},{112,96},{96,80},{80,64},{64,65},{... | collective-permute-start | bytes 786440 | tf_op jit(solution)/shard_map/ppermute | solution.py:41
  158.1 8.8 %collective-permute-start.7 = (f32[8,8192]{1,0:T(8,128)}, f32[8,8192]{1,0:T(8,128)}, u32[]{:S(2)}, u32[]{:S(2)}) collective-permute-start(f32[8,8192]{1,0:T(8,128)} %get-tuple-element.19), channel_id=1, source_target_pairs={{16,0},{32,16},{48,32},{112,48},{96,112},{80,96},{64,80},{65,64},{... | collective-permute-start | bytes 786440 | tf_op jit(solution)/shard_map/ppermute | solution.py:42
  199.5 45.1 %copy-start.1 = (f32[16,8192]{1,0:T(8,128)S(1)}, f32[16,8192]{1,0:T(8,128)}, u32[]{:S(2)}) copy-start(f32[16,8192]{1,0:T(8,128)} %copy-done) | copy-start | bytes 1572868
  245.8 7.0 %collective-permute-start.8 = (f32[8,8192]{1,0:T(8,128)S(1)}, f32[8,8192]{1,0:T(8,128)S(1)}, u32[]{:S(2)}, u32[]{:S(2)}) collective-permute-start(f32[8,8192]{1,0:T(8,128)S(1)} %get-tuple-element.16), channel_id=1, source_target_pairs={{0,16},{16,32},{32,48},{48,112},{112,96},{96,80},{80,64},{64,65},{... | collective-permute-start | bytes 786440 | tf_op jit(solution)/shard_map/ppermute | solution.py:41
  248.3 8.3 %collective-permute-start.9 = (f32[8,8192]{1,0:T(8,128)S(1)}, f32[8,8192]{1,0:T(8,128)S(1)}, u32[]{:S(2)}, u32[]{:S(2)}) collective-permute-start(f32[8,8192]{1,0:T(8,128)S(1)} %get-tuple-element.17), channel_id=1, source_target_pairs={{16,0},{32,16},{48,32},{112,48},{96,112},{80,96},{64,80},{65,64},{... | collective-permute-start | bytes 786440 | tf_op jit(solution)/shard_map/ppermute | solution.py:42
  282.1 7.2 %collective-permute-start.10 = (f32[8,8192]{1,0:T(8,128)S(1)}, f32[8,8192]{1,0:T(8,128)S(1)}, u32[]{:S(2)}, u32[]{:S(2)}) collective-permute-start(f32[8,8192]{1,0:T(8,128)S(1)} %get-tuple-element.14), channel_id=1, source_target_pairs={{0,16},{16,32},{32,48},{48,112},{112,96},{96,80},{80,64},{64,65},{... | collective-permute-start | bytes 786440 | tf_op jit(solution)/shard_map/ppermute | solution.py:41
  284.7 8.3 %collective-permute-start.11 = (f32[8,8192]{1,0:T(8,128)S(1)}, f32[8,8192]{1,0:T(8,128)S(1)}, u32[]{:S(2)}, u32[]{:S(2)}) collective-permute-start(f32[8,8192]{1,0:T(8,128)S(1)} %get-tuple-element.15), channel_id=1, source_target_pairs={{16,0},{32,16},{48,32},{112,48},{96,112},{80,96},{64,80},{65,64},{... | collective-permute-start | bytes 786440 | tf_op jit(solution)/shard_map/ppermute | solution.py:42
  303.3 15.4 %copy-start.4 = (f32[1,16,8,1024]{3,1,0,2:T(8,128)S(1)}, f32[1,16,8,1024]{3,1,0,2:T(8,128)}, u32[]{:S(2)}) copy-start(f32[1,16,8,1024]{3,1,0,2:T(8,128)} %get-tuple-element.6) | copy-start | bytes 1572868
  346.4 18.8 %all-to-all-start.1 = ((f32[8,2,16,1024]{3,2,1,0:T(8,128)}), f32[8,2,16,1024]{3,2,1,0:T(8,128)S(1)}, u32[]{:S(2)}, u32[]{:S(2)}) async-start(f32[8,2,16,1024]{3,2,1,0:T(8,128)} %maximum_bitcast_fusion), calls=%async_computation.1 | async-start | bytes 2097152 | tf_op jit(solution)/shard_map/all_to_all | solution.py:104

commit v5 on v3

--- a/solution.py
+++ b/solution.py
@@ -39,9 +39,9 @@
     forward = [(place[i], place[i + 1]) for i in range(len(place) - 1)]
     backward = [(place[i + 1], place[i]) for i in range(len(place) - 1)]
     axes = ("space", "tm")
-    low = lax.ppermute(field[field.shape[0] - BW :], axes, forward)
-    high = lax.ppermute(field[:BW], axes, backward)
-    return jnp.concatenate([low, field, high], axis=0)
+    low = lax.ppermute(field[:, field.shape[1] - BW :], axes, forward)
+    high = lax.ppermute(field[:, :BW], axes, backward)
+    return jnp.concatenate([low, field, high], axis=1)
 
 
 def tm_halo(field):
@@ -53,24 +53,23 @@
     return jnp.concatenate([low, field, high], axis=0)
 
 
-def band_product(field, temporal_taps, halo=None):
-    length = field.shape[0]
+def band_product(field, temporal_taps, halo=None, axis=1):
+    length = field.shape[axis]
     padded = (halo or day_order_halo)(field)
+
+    def days(start):
+        return lax.slice_in_dim(padded, start, start + length, axis=axis)
+
     summed = temporal_taps[0] * field
     for offset in range(1, BW + 1):
-        summed = summed + temporal_taps[offset] * (
-            padded[BW - offset : BW - offset + length] + padded[BW + offset : BW + offset + length]
-        )
+        summed = summed + temporal_taps[offset] * (days(BW - offset) + days(BW + offset))
     return summed
 
 
 def block_product(field, weights, pattern):
-    day_count = field.shape[0]
-    blocks = pattern.shape[0]
-    blocked = field.reshape(day_count, blocks, BLOCK)
-    picked = blocked[:, pattern].reshape(day_count, blocks, pattern.shape[1] * BLOCK)
-    out = jnp.einsum("rkc,drk->drc", weights, picked, precision=lax.Precision.HIGH)
-    return out.reshape(day_count, blocks * BLOCK)
+    blocks, day_count, _ = field.shape
+    picked = field[pattern].transpose(0, 2, 1, 3).reshape(blocks, day_count, pattern.shape[1] * BLOCK)
+    return jnp.einsum("rkc,rdk->rdc", weights, picked, precision=lax.Precision.HIGH)
 
 
 def snake(spaces):
@@ -83,13 +82,16 @@
     k, days, cells = field.shape
     chunked = field.reshape(k, n, days // n, cells)[:, jnp.array(snake(n))].transpose(1, 0, 2, 3)
     got = lax.all_to_all(chunked, "space", split_axis=0, concat_axis=0, tiled=True)
-    return got.transpose(1, 2, 0, 3).reshape(k, days // n, n * cells)
+    got = got.reshape(n, k, days // n, cells // BLOCK, BLOCK).transpose(1, 0, 3, 2, 4)
+    return got.reshape(k, n * cells // BLOCK, days // n, BLOCK)
 
 
 def to_cells(field):
     n = lax.axis_size("space")
-    k, days, cells = field.shape
-    chunked = field.reshape(k, days, n, cells // n).transpose(2, 0, 1, 3)
+    k, blocks, days, _ = field.shape
+    cells = blocks * BLOCK
+    chunked = field.reshape(k, n, blocks // n, days, BLOCK).transpose(1, 0, 3, 2, 4)
+    chunked = chunked.reshape(n, k, days, cells // n)
     got = lax.all_to_all(chunked, "space", split_axis=0, concat_axis=0, tiled=True)
     return got[jnp.array(snake(n))].transpose(1, 0, 2, 3).reshape(k, n * days, cells // n)
 
@@ -165,7 +167,7 @@
     def spread(field):
         return block_product(band_product(field, temporal_taps), weights, pattern)
 
-    banded = band_product(coefficients, temporal_taps, tm_halo)
+    banded = band_product(coefficients, temporal_taps, tm_halo, axis=0)
     moved = to_days(jnp.stack([coefficients, counts.astype(jnp.float32), banded]))
     coef, cnt = moved[0], moved[1]
     latent = block_product(moved[2], weights, pattern)

time: 362 us -> 343 us (0.948)
  other arithmetic: 84.2 us -> 70.7 us
  local copies, waits for them, and re-layouts: 51.5 us -> 41.5 us
  waiting for transfers between devices: 36.7 us -> 41.3 us
    reshape x5 -> x0, other arithmetic: 40.8 us -> none  [block_product(): blocked = field.reshape(day_count, blocks, BLOCK)]
    add x1 -> x6, other arithmetic: 6.61 us -> 41 us  [band_product(): summed + temporal_taps[offset] * (days(BW - offset) + days(BW + offset))]
    ppermute x10, waiting for transfers between devices: 36.7 us -> 41.3 us  [the longest x5 21.2 us: day_order_halo(): high = lax.ppermute(field[:, :BW], axes, backward)]
    reduce_sum x2 -> x0, other arithmetic: 4.29 us -> none  [the longest x1 3.05 us: shards(): jnp.sum(direction * curved)]
  transfers between devices with their start and end apart: 13 -> 13, of which waited for: 9 -> 10; matrix products, arithmetic and copies ran while one was open for 11% -> 11% of each run, Pallas kernels for 0% -> 0%
where the time goes in v5:
time: 343 us; the launch traced here: 341 us
  matrix products  93.2 us (27%)
  other arithmetic  70.7 us (21%)
  local copies, waits for them, and re-layouts  41.5 us (12%)
  waiting for transfers between devices  41.3 us (12%)
  Pallas kernels  37.8 us (11%)
  starting transfers between devices  32.5 us (9%)
  blocking collectives  19.5 us (6%)
  between operations  5.16 us (2%)
    dot_general x6, matrix products, block_product(): jnp.einsum('rkc,rdk->rdc', weights, picked, precision=lax.Precision.HIGH)  93.2 us
    add x6, other arithmetic, band_product(): summed + temporal_taps[offset] * (days(BW - offset) + days(BW + offset))  41 us
    pallas_call x4, Pallas kernels, group_sum(): pl.pallas_call(functools.partial(group_sum_kernel, axis), out_shape=jax.S...  37.8 us
    mul x1, other arithmetic, wendland(): return amplitude * remain ** 4 * (1.0 + 4.0 * scaled)  26.8 us
    ppermute x5, waiting for transfers between devices, day_order_halo(): high = lax.ppermute(field[:, :BW], axes, backward)  21.2 us
    ppermute x5, waiting for transfers between devices, day_order_halo(): low = lax.ppermute(field[:, field.shape[1] - BW:], axes, forward)  20.1 us
    all_to_all x1, blocking collectives, to_cells(): lax.all_to_all(chunked, 'space', split_axis=0, concat_axis=0, tiled=True)  19.5 us
    gather x6, local copies, waits for them, and re-layouts, block_product(): field[pattern].transpose(0, 2, 1, 3)  19.1 us
  transfers between devices with their start and end apart: 13, of which 10 were waited for; matrix products, arithmetic and copies ran while one was open for 11% of the time, Pallas kernels for 0%

profile of v5, /device:TPU:0, one launch (start us, length us, event | category | flops | bytes accessed | tf_op | source)
XLA Modules:
  0.0 341.5 jit_solution(12505911822622059850)
XLA Ops:
  6.6 2.3 gather_fusion.2
  10.3 1.7 fusion.252
  13.3 6.5 %fusion.227 = f32[128,1024]{1,0:T(8,128)S(1)} fusion(f32[136,1024]{1,0:T(8,128)S(1)} %constant_dynamic-update-slice_fusion.2, f32[136,1024]{1,0:T(8,128)S(1)} %get-tuple-element.24, f32[128,1024]{1,0:T(8,128)S(1)} %copy-done, f32[]{:T(128)} %bitcast.10, f32[]{:T(128)} %bitcast.9, f32[]{:T(128)} %bitcast.8, f32[]{:T(128)} %bitcast.7, f32[]{:T(128)} %bitcast.6, ...), kind=kLoop, calls=%fused_computation.378 | loop fusion | flops 3276800 | bytes 9437220 | tf_op jit(solution)/shard_map/add | solution.py:65
  20.0 1.8 gather_fusion
  21.8 6.9 %all-to-all-start = ((f32[8,3,16,1024]{3,2,1,0:T(8,128)}), f32[8,3,16,1024]{3,2,1,0:T(8,128)S(1)}, u32[]{:S(2)}, u32[]{:S(2)}) async-start(f32[8,3,16,1024]{3,2,1,0:T(8,128)} %gather_fusion), calls=%async_computation | async-start | bytes 3145728 | tf_op jit(solution)/shard_map/all_to_all | solution.py:84
  28.7 26.8 %add_multiply_fusion = f32[64,1024,128]{2,1,0:T(8,128)} fusion(f32[64,1024]{1,0:T(8,128)S(1)} %bitcast.140, f32[64,128]{1,0:T(8,128)S(1)} %bitcast.146, f32[64,1024]{1,0:T(8,128)S(1)} %bitcast.139, f32[64,128]{1,0:T(8,128)S(1)} %bitcast.145), kind=kLoop, calls=%fused_computation.9 | loop fusion | flops 117440512 | bytes 34144256 | tf_op jit(solution)/shard_map/mul | solution.py:21
  56.2 3.2 gather_fusion.1
  59.3 15.3 %bitcast_subtract_fusion = (f32[64,16,128]{2,1,0:T(8,128)S(1)}, f32[64,16,128]{2,1,0:T(8,128)S(1)}) fusion(f32[1,8,8,16,128]{4,3,2,1,0:T(8,128)S(1)} %copy.28, f32[64,1024,128]{2,1,0:T(8,128)} %add_multiply_fusion, f32[64,8,2,8,128]{4,3,2,1,0:T(8,128)} %bitcast.124), kind=kOutput, calls=%fused_computation.400 | convolution fusion | flops 805437440 | bytes 39321600 | tf_op jit(solution)/shard_map/rkc,rdk->rdc/dot_general | solution.py:72
  74.7 3.8 %collective-permute-start.2 = (f32[64,8,128]{2,1,0:T(8,128)S(1)}, f32[64,8,128]{2,1,0:T(8,128)S(1)}, u32[]{:S(2)}, u32[]{:S(2)}) collective-permute-start(f32[64,8,128]{2,1,0:T(8,128)S(1)} %get-tuple-element.22), channel_id=1, source_target_pairs={{0,16},{16,32},{32,48},{48,112},{112,96},{96,80},{80,64},{64,1},{1... | collective-permute-start | bytes 786440 | tf_op jit(solution)/shard_map/ppermute | solution.py:42
  78.6 1.5 collective-permute-start.3
  80.1 4.2 %collective-permute-done.2 = f32[64,8,128]{2,1,0:T(8,128)S(1)} collective-permute-done((f32[64,8,128]{2,1,0:T(8,128)S(1)}, f32[64,8,128]{2,1,0:T(8,128)S(1)}, u32[]{:S(2)}, u32[]{:S(2)}) %collective-permute-start.2) | collective-permute-done | bytes 262176 | tf_op jit(solution)/shard_map/ppermute | solution.py:42
  84.4 4.7 %collective-permute-done.3 = f32[64,8,128]{2,1,0:T(8,128)S(1)} collective-permute-done((f32[64,8,128]{2,1,0:T(8,128)S(1)}, f32[64,8,128]{2,1,0:T(8,128)S(1)}, u32[]{:S(2)}, u32[]{:S(2)}) %collective-permute-start.3) | collective-permute-done | bytes 262176 | tf_op jit(solution)/shard_map/ppermute | solution.py:43
  89.1 6.9 %fusion.184 = f32[64,16,128]{2,1,0:T(8,128)S(1)} fusion(f32[64,16,128]{2,1,0:T(8,128)S(1)} %get-tuple-element.42, f32[64,8,128]{2,1,0:T(8,128)S(1)} %collective-permute-done.3, f32[64,8,128]{2,1,0:T(8,128)S(1)} %collective-permute-done.2, f32[]{:T(128)} %bitcast.10, f32[]{:T(128)} %bitcast.9, f32[]{:T(128)} %bitcast.8, f32[]{:T(128)} %bitcast.7, ...), kind=kLoop, calls=%fused_computation.324 | loop fusion | flops 5373952 | bytes 1572900 | tf_op jit(solution)/shard_map/add | solution.py:65
  96.0 3.2 gather_fusion.3
  99.1 15.3 %fusion.253 = (f32[64,16,128]{2,1,0:T(8,128)S(1)}, f32[64,16,128]{2,1,0:T(8,128)S(1)}) fusion(f32[64,16,128]{2,1,0:T(8,128)S(1)} %bitcast.133, f32[64,1024,128]{2,1,0:T(8,128)} %add_multiply_fusion, f32[64,8,2,8,128]{4,3,2,1,0:T(8,128)} %bitcast.125), kind=kOutput, calls=%fused_computation.431 | convolution fusion | flops 805568512 | bytes 39321600 | tf_op jit(solution)/shard_map/rkc,rdk->rdc/dot_general | solution.py:72
  114.5 3.4 collective-permute-start.4
  119.2 4.8 %collective-permute-done.4 = f32[64,8,128]{2,1,0:T(8,128)S(1)} collective-permute-done((f32[64,8,128]{2,1,0:T(8,128)S(1)}, f32[64,8,128]{2,1,0:T(8,128)S(1)}, u32[]{:S(2)}, u32[]{:S(2)}) %collective-permute-start.4) | collective-permute-done | bytes 262176 | tf_op jit(solution)/shard_map/ppermute | solution.py:42
  124.0 4.1 %collective-permute-done.5 = f32[64,8,128]{2,1,0:T(8,128)S(1)} collective-permute-done((f32[64,8,128]{2,1,0:T(8,128)S(1)}, f32[64,8,128]{2,1,0:T(8,128)S(1)}, u32[]{:S(2)}, u32[]{:S(2)}) %collective-permute-start.5) | collective-permute-done | bytes 262176 | tf_op jit(solution)/shard_map/ppermute | solution.py:43
  128.1 6.9 %fusion.148 = f32[64,16,128]{2,1,0:T(8,128)S(1)} fusion(f32[64,16,128]{2,1,0:T(8,128)S(1)} %get-tuple-element.44, f32[64,8,128]{2,1,0:T(8,128)S(1)} %collective-permute-done.5, f32[64,8,128]{2,1,0:T(8,128)S(1)} %collective-permute-done.4, f32[]{:T(128)} %bitcast.10, f32[]{:T(128)} %bitcast.9, f32[]{:T(128)} %bitcast.8, f32[]{:T(128)} %bitcast.7, ...), kind=kLoop, calls=%fused_computation.288 | loop fusion | flops 5373952 | bytes 1572900 | tf_op jit(solution)/shard_map/add | solution.py:65
  135.0 3.2 gather_fusion.4
  138.2 15.3 %fusion.24 = f32[64,16,128]{2,1,0:T(8,128)S(1)} fusion(f32[64,16,128]{2,1,0:T(8,128)S(1)} %get-tuple-element.43, f32[64,1024,128]{2,1,0:T(8,128)} %add_multiply_fusion, f32[64,8,2,8,128]{4,3,2,1,0:T(8,128)} %bitcast.126), kind=kOutput, calls=%fused_computation.171 | convolution fusion | flops 805437440 | bytes 38797312 | tf_op jit(solution)/shard_map/rkc,rdk->rdc/dot_general | solution.py:72
  153.5 3.1 collective-permute-start.6
  156.6 1.5 collective-permute-start.7
  158.1 3.5 %collective-permute-done.6 = f32[64,8,128]{2,1,0:T(8,128)S(1)} collective-permute-done((f32[64,8,128]{2,1,0:T(8,128)S(1)}, f32[64,8,128]{2,1,0:T(8,128)S(1)}, u32[]{:S(2)}, u32[]{:S(2)}) %collective-permute-start.6) | collective-permute-done | bytes 262176 | tf_op jit(solution)/shard_map/ppermute | solution.py:42
  161.6 4.1 %collective-permute-done.7 = f32[64,8,128]{2,1,0:T(8,128)S(1)} collective-permute-done((f32[64,8,128]{2,1,0:T(8,128)S(1)}, f32[64,8,128]{2,1,0:T(8,128)S(1)}, u32[]{:S(2)}, u32[]{:S(2)}) %collective-permute-start.7) | collective-permute-done | bytes 262176 | tf_op jit(solution)/shard_map/ppermute | solution.py:43
  165.7 6.9 %fusion.112 = f32[64,16,128]{2,1,0:T(8,128)S(1)} fusion(f32[64,16,128]{2,1,0:T(8,128)S(1)} %fusion.24, f32[64,8,128]{2,1,0:T(8,128)S(1)} %collective-permute-done.7, f32[64,8,128]{2,1,0:T(8,128)S(1)} %collective-permute-done.6, f32[]{:T(128)} %bitcast.10, f32[]{:T(128)} %bitcast.9, f32[]{:T(128)} %bitcast.8, f32[]{:T(128)} %bitcast.7, f32[]{:T(128)} %bitcast.6, ...), kind=kLoop, calls=%fused_computation.252 | loop fusion | flops 5373952 | bytes 1572900 | tf_op jit(solution)/shard_map/add | solution.py:65
  172.6 3.2 gather_fusion.5
  175.8 16.1 %multiply_reduce_fusion.1 = (f32[]{:T(128)}, f32[]{:T(128)}, f32[]{:T(128)}, f32[64,16,128]{2,1,0:T(8,128)S(1)}) fusion(f32[64,16,128]{2,1,0:T(8,128)S(1)} %get-tuple-element.45, f32[64,1024,128]{2,1,0:T(8,128)} %add_multiply_fusion, f32[64,8,2,8,128]{4,3,2,1,0:T(8,128)} %bitcast.122), kind=kOutput, calls=%fused_computation.406 | convolution fusion | flops 806354944 | bytes 38797324 | tf_op jit(solution)/shard_map/rkc,rdk->rdc/dot_general | solution.py:72
  191.9 5.5 %stack.54 = f32[8]{0:T(128)S(1)} concatenate(f32[1]{0:T(128)} %bitcast.26, f32[1]{0:T(128)} %bitcast.31, f32[1]{0:T(128)} %bitcast.32, f32[1]{0:T(128)} %bitcast.26, f32[1]{0:T(128)} %bitcast.26, f32[1]{0:T(128)} %bitcast.26, f32[1]{0:T(128)} %bitcast.26, f32[1]{0:T(128)} %bitcast.26), dimensions={0} | concatenate | bytes 64 | tf_op jit(solution)/shard_map/stack | solution.py:159
  198.0 8.1 %shard_map.86.x_ref = f32[8,128]{1,0:T(8,128)} custom-call(f32[8,128]{1,0:T(8,128)} %add.406.x_ref), custom_call_target="tpu_custom_call" | custom-call | tf_op jit(solution)/shard_map/pallas_call | solution.py:144
  206.1 11.0 %shard_map.87 = f32[8,128]{1,0:T(8,128)} custom-call(f32[8,128]{1,0:T(8,128)} %shard_map.86.x_ref), custom_call_target="tpu_custom_call" | custom-call | tf_op jit(solution)/shard_map/pallas_call | solution.py:144
  217.1 1.4 fusion.251
  222.0 2.5 collective-permute-start.8
  225.8 4.5 %collective-permute-done.8 = f32[64,8,128]{2,1,0:T(8,128)S(1)} collective-permute-done((f32[64,8,128]{2,1,0:T(8,128)S(1)}, f32[64,8,128]{2,1,0:T(8,128)S(1)}, u32[]{:S(2)}, u32[]{:S(2)}) %collective-permute-start.8) | collective-permute-done | bytes 262176 | tf_op jit(solution)/shard_map/ppermute | solution.py:42
  230.3 4.1 %collective-permute-done.9 = f32[64,8,128]{2,1,0:T(8,128)S(1)} collective-permute-done((f32[64,8,128]{2,1,0:T(8,128)S(1)}, f32[64,8,128]{2,1,0:T(8,128)S(1)}, u32[]{:S(2)}, u32[]{:S(2)}) %collective-permute-start.9) | collective-permute-done | bytes 262176 | tf_op jit(solution)/shard_map/ppermute | solution.py:43
  234.4 6.9 %fusion.76 = f32[64,16,128]{2,1,0:T(8,128)S(1)} fusion(f32[64,16,128]{2,1,0:T(8,128)S(1)} %multiply_add_fusion.1, f32[64,8,128]{2,1,0:T(8,128)S(1)} %collective-permute-done.9, f32[64,8,128]{2,1,0:T(8,128)S(1)} %collective-permute-done.8, f32[]{:T(128)} %bitcast.10, f32[]{:T(128)} %bitcast.9, f32[]{:T(128)} %bitcast.8, f32[]{:T(128)} %bitcast.7, ...), kind=kLoop, calls=%fused_computation.216 | loop fusion | flops 5373952 | bytes 1572900 | tf_op jit(solution)/shard_map/add | solution.py:65
  241.3 3.2 gather_fusion.6
  244.5 15.3 %fusion.30 = f32[64,16,128]{2,1,0:T(8,128)S(1)} fusion(f32[64,16,128]{2,1,0:T(8,128)S(1)} %get-tuple-element.43, f32[64,1024,128]{2,1,0:T(8,128)} %add_multiply_fusion, f32[64,8,2,8,128]{4,3,2,1,0:T(8,128)} %bitcast.127), kind=kOutput, calls=%fused_computation.173 | convolution fusion | flops 805437440 | bytes 38797312 | tf_op jit(solution)/shard_map/rkc,rdk->rdc/dot_general | solution.py:72
  259.8 3.1 collective-permute-start.10
  263.0 1.6 collective-permute-start.11
  264.5 3.1 collective-permute-done.10
  267.6 4.1 %collective-permute-done.11 = f32[64,8,128]{2,1,0:T(8,128)S(1)} collective-permute-done((f32[64,8,128]{2,1,0:T(8,128)S(1)}, f32[64,8,128]{2,1,0:T(8,128)S(1)}, u32[]{:S(2)}, u32[]{:S(2)}) %collective-permute-start.11) | collective-permute-done | bytes 262176 | tf_op jit(solution)/shard_map/ppermute | solution.py:43
  271.7 6.9 %fusion.40 = f32[64,16,128]{2,1,0:T(8,128)S(1)} fusion(f32[64,16,128]{2,1,0:T(8,128)S(1)} %fusion.30, f32[64,8,128]{2,1,0:T(8,128)S(1)} %collective-permute-done.11, f32[64,8,128]{2,1,0:T(8,128)S(1)} %collective-permute-done.10, f32[]{:T(128)} %bitcast.10, f32[]{:T(128)} %bitcast.9, f32[]{:T(128)} %bitcast.8, f32[]{:T(128)} %bitcast.7, f32[]{:T(128)} %bitcast.6, ...), kind=kLoop, calls=%fused_computation.180 | loop fusion | flops 5373952 | bytes 1572900 | tf_op jit(solution)/shard_map/add | solution.py:65
  278.6 3.2 gather_fusion.7
  281.8 15.9 %multiply_reduce_fusion = (f32[]{:T(128)}, f32[64,16,128]{2,1,0:T(8,128)S(1)}) fusion(f32[64,16,128]{2,1,0:T(8,128)S(1)} %multiply_add_fusion.1, f32[64,1024,128]{2,1,0:T(8,128)} %add_multiply_fusion, f32[64,8,2,8,128]{4,3,2,1,0:T(8,128)} %bitcast.123), kind=kOutput, calls=%fused_computation.403 | convolution fusion | flops 805699584 | bytes 38797316 | tf_op jit(solution)/shard_map/rkc,rdk->rdc/dot_general | solution.py:72
  299.0 8.3 %shard_map.88.x_ref = f32[8,128]{1,0:T(8,128)} custom-call(f32[8,128]{1,0:T(8,128)} %add.441.x_ref), custom_call_target="tpu_custom_call" | custom-call | tf_op jit(solution)/shard_map/pallas_call | solution.py:144
  307.3 10.4 %shard_map.89 = f32[8,128]{1,0:T(8,128)} custom-call(f32[8,128]{1,0:T(8,128)} %shard_map.88.x_ref), custom_call_target="tpu_custom_call" | custom-call | tf_op jit(solution)/shard_map/pallas_call | solution.py:144
  320.4 19.5 %all_to_all.10 = f32[8,2,16,1024]{3,2,1,0:T(8,128)S(1)} all-to-all(f32[8,2,16,1024]{3,2,1,0:T(8,128)S(1)} %reshape.83), channel_id=1, replica_groups=mesh['space'=8,'tm'=16] {'space'}, dimensions={0} | all-to-all | bytes 2097152 | tf_op jit(solution)/shard_map/all_to_all | solution.py:95
  (44 shorter events, 17.8 us)
Async XLA Ops:
  0.6 12.5 %copy-start = (f32[128,1024]{1,0:T(8,128)S(1)}, f32[128,1024]{1,0:T(8,128)}, u32[]{:S(2)}) copy-start(f32[128,1024]{1,0:T(8,128)} %param.7) | copy-start | bytes 1572868
  1.5 11.7 %collective-permute-start = (f32[8,1024]{1,0:T(8,128)S(1)}, f32[8,1024]{1,0:T(8,128)S(1)}, u32[]{:S(2)}, u32[]{:S(2)}) collective-permute-start(f32[8,1024]{1,0:T(8,128)S(1)} %get-tuple-element.26), channel_id=1, source_target_pairs={{0,1},{1,2},{2,3},{3,4},{4,5},{5,6},{6,7},{7,8},{8,9},{9,10},{10,1... | collective-permute-start | bytes 98312 | tf_op jit(solution)/shard_map/ppermute | solution.py:51
  2.8 10.5 %collective-permute-start.1 = (f32[8,1024]{1,0:T(8,128)S(1)}, f32[8,1024]{1,0:T(8,128)S(1)}, u32[]{:S(2)}, u32[]{:S(2)}) collective-permute-start(f32[8,1024]{1,0:T(8,128)S(1)} %get-tuple-element.27), channel_id=1, source_target_pairs={{1,0},{2,1},{3,2},{4,3},{5,4},{6,5},{7,6},{8,7},{9,8},{10,9},{11,1... | collective-permute-start | bytes 98312 | tf_op jit(solution)/shard_map/ppermute | solution.py:52
  21.8 33.7 %all-to-all-start = ((f32[8,3,16,1024]{3,2,1,0:T(8,128)}), f32[8,3,16,1024]{3,2,1,0:T(8,128)S(1)}, u32[]{:S(2)}, u32[]{:S(2)}) async-start(f32[8,3,16,1024]{3,2,1,0:T(8,128)} %gather_fusion), calls=%async_computation | async-start | bytes 3145728 | tf_op jit(solution)/shard_map/all_to_all | solution.py:84
  74.7 9.6 %collective-permute-start.2 = (f32[64,8,128]{2,1,0:T(8,128)S(1)}, f32[64,8,128]{2,1,0:T(8,128)S(1)}, u32[]{:S(2)}, u32[]{:S(2)}) collective-permute-start(f32[64,8,128]{2,1,0:T(8,128)S(1)} %get-tuple-element.22), channel_id=1, source_target_pairs={{0,16},{16,32},{32,48},{48,112},{112,96},{96,80},{80,64},{64,1},{1... | collective-permute-start | bytes 786440 | tf_op jit(solution)/shard_map/ppermute | solution.py:42
  78.6 10.5 %collective-permute-start.3 = (f32[64,8,128]{2,1,0:T(8,128)S(1)}, f32[64,8,128]{2,1,0:T(8,128)S(1)}, u32[]{:S(2)}, u32[]{:S(2)}) collective-permute-start(f32[64,8,128]{2,1,0:T(8,128)S(1)} %get-tuple-element.23), channel_id=1, source_target_pairs={{16,0},{32,16},{48,32},{112,48},{96,112},{80,96},{64,80},{1,64},{1... | collective-permute-start | bytes 786440 | tf_op jit(solution)/shard_map/ppermute | solution.py:43
  114.5 9.5 %collective-permute-start.4 = (f32[64,8,128]{2,1,0:T(8,128)S(1)}, f32[64,8,128]{2,1,0:T(8,128)S(1)}, u32[]{:S(2)}, u32[]{:S(2)}) collective-permute-start(f32[64,8,128]{2,1,0:T(8,128)S(1)} %get-tuple-element.20), channel_id=1, source_target_pairs={{0,16},{16,32},{32,48},{48,112},{112,96},{96,80},{80,64},{64,1},{1... | collective-permute-start | bytes 786440 | tf_op jit(solution)/shard_map/ppermute | solution.py:42
  117.9 10.2 %collective-permute-start.5 = (f32[64,8,128]{2,1,0:T(8,128)S(1)}, f32[64,8,128]{2,1,0:T(8,128)S(1)}, u32[]{:S(2)}, u32[]{:S(2)}) collective-permute-start(f32[64,8,128]{2,1,0:T(8,128)S(1)} %get-tuple-element.21), channel_id=1, source_target_pairs={{16,0},{32,16},{48,32},{112,48},{96,112},{80,96},{64,80},{1,64},{1... | collective-permute-start | bytes 786440 | tf_op jit(solution)/shard_map/ppermute | solution.py:43
  153.5 8.1 %collective-permute-start.6 = (f32[64,8,128]{2,1,0:T(8,128)S(1)}, f32[64,8,128]{2,1,0:T(8,128)S(1)}, u32[]{:S(2)}, u32[]{:S(2)}) collective-permute-start(f32[64,8,128]{2,1,0:T(8,128)S(1)} %get-tuple-element.18), channel_id=1, source_target_pairs={{0,16},{16,32},{32,48},{48,112},{112,96},{96,80},{80,64},{64,1},{1... | collective-permute-start | bytes 786440 | tf_op jit(solution)/shard_map/ppermute | solution.py:42
  156.6 9.1 %collective-permute-start.7 = (f32[64,8,128]{2,1,0:T(8,128)S(1)}, f32[64,8,128]{2,1,0:T(8,128)S(1)}, u32[]{:S(2)}, u32[]{:S(2)}) collective-permute-start(f32[64,8,128]{2,1,0:T(8,128)S(1)} %get-tuple-element.19), channel_id=1, source_target_pairs={{16,0},{32,16},{48,32},{112,48},{96,112},{80,96},{64,80},{1,64},{1... | collective-permute-start | bytes 786440 | tf_op jit(solution)/shard_map/ppermute | solution.py:43
  222.0 8.3 %collective-permute-start.8 = (f32[64,8,128]{2,1,0:T(8,128)S(1)}, f32[64,8,128]{2,1,0:T(8,128)S(1)}, u32[]{:S(2)}, u32[]{:S(2)}) collective-permute-start(f32[64,8,128]{2,1,0:T(8,128)S(1)} %get-tuple-element.16), channel_id=1, source_target_pairs={{0,16},{16,32},{32,48},{48,112},{112,96},{96,80},{80,64},{64,1},{1... | collective-permute-start | bytes 786440 | tf_op jit(solution)/shard_map/ppermute | solution.py:42
  224.5 9.9 %collective-permute-start.9 = (f32[64,8,128]{2,1,0:T(8,128)S(1)}, f32[64,8,128]{2,1,0:T(8,128)S(1)}, u32[]{:S(2)}, u32[]{:S(2)}) collective-permute-start(f32[64,8,128]{2,1,0:T(8,128)S(1)} %get-tuple-element.17), channel_id=1, source_target_pairs={{16,0},{32,16},{48,32},{112,48},{96,112},{80,96},{64,80},{1,64},{1... | collective-permute-start | bytes 786440 | tf_op jit(solution)/shard_map/ppermute | solution.py:43
  259.8 7.8 %collective-permute-start.10 = (f32[64,8,128]{2,1,0:T(8,128)S(1)}, f32[64,8,128]{2,1,0:T(8,128)S(1)}, u32[]{:S(2)}, u32[]{:S(2)}) collective-permute-start(f32[64,8,128]{2,1,0:T(8,128)S(1)} %get-tuple-element.14), channel_id=1, source_target_pairs={{0,16},{16,32},{32,48},{48,112},{112,96},{96,80},{80,64},{64,1},{1... | collective-permute-start | bytes 786440 | tf_op jit(solution)/shard_map/ppermute | solution.py:42
  263.0 8.8 %collective-permute-start.11 = (f32[64,8,128]{2,1,0:T(8,128)S(1)}, f32[64,8,128]{2,1,0:T(8,128)S(1)}, u32[]{:S(2)}, u32[]{:S(2)}) collective-permute-start(f32[64,8,128]{2,1,0:T(8,128)S(1)} %get-tuple-element.15), channel_id=1, source_target_pairs={{16,0},{32,16},{48,32},{112,48},{96,112},{80,96},{64,80},{1,64},{1... | collective-permute-start | bytes 786440 | tf_op jit(solution)/shard_map/ppermute | solution.py:43

commit v6 on v5

--- a/solution.py
+++ b/solution.py
@@ -155,10 +155,12 @@
     )(tile)
 
 
-def total(values):
-    tile = jnp.zeros((8, 128), jnp.float32) + jnp.stack(values + [values[0]] * (8 - len(values)))[:, None]
+def total(products):
+    count = len(products)
+    lanes = jnp.stack(products).reshape(count, -1, 128).sum(axis=1)
+    tile = jnp.pad(lanes, ((0, 8 - count), (0, 0)))
     tile = group_sum(group_sum(tile, "space", 0), "tm", 1)
-    return [tile[i, 0] for i in range(len(values))]
+    return [jnp.sum(tile[i]) for i in range(count)]
 
 
 def shards(coefficients, counts, coords, pattern, temporal_taps):
@@ -177,9 +179,7 @@
     direction = residual
     image = spread(direction)
     curved = direction + spread(intensity * image)
-    norm_now, curvature, curved_sq = total(
-        [jnp.sum(residual * residual), jnp.sum(direction * curved), jnp.sum(curved * curved)]
-    )
+    norm_now, curvature, curved_sq = total([residual * residual, direction * curved, curved * curved])
     step_size = norm_now / curvature
     newton_step = step_size * direction
     residual = residual - step_size * curved
@@ -188,7 +188,7 @@
     norm_now = norm_next
     image = spread(direction)
     curved = direction + spread(intensity * image)
-    (curvature,) = total([jnp.sum(direction * curved)])
+    (curvature,) = total([direction * curved])
     step_size = norm_now / curvature
     newton_step = newton_step + step_size * direction
     residual = residual - step_size * curved

time: 343 us -> 336 us (0.980)
  local copies, waits for them, and re-layouts: 41.5 us -> 32.8 us
    another operation x1 -> x0, local copies, waits for them, and re-layouts: 5.47 us -> none  [total(): jnp.stack(values + [values[0]] * (8 - len(values)))[:, None]]
where the time goes in v6:
time: 336 us; the launch traced here: 334 us
  matrix products  91.7 us (27%)
  other arithmetic  73.9 us (22%)
  waiting for transfers between devices  41.3 us (12%)
  Pallas kernels  37.8 us (11%)
  local copies, waits for them, and re-layouts  32.8 us (10%)
  starting transfers between devices  32.5 us (10%)
  blocking collectives  19.5 us (6%)
  between operations  4.98 us (1%)
    dot_general x6, matrix products, block_product(): jnp.einsum('rkc,rdk->rdc', weights, picked, precision=lax.Precision.HIGH)  91.7 us
    add x6, other arithmetic, band_product(): summed + temporal_taps[offset] * (days(BW - offset) + days(BW + offset))  41.4 us
    pallas_call x4, Pallas kernels, group_sum(): pl.pallas_call(functools.partial(group_sum_kernel, axis), out_shape=jax.S...  37.8 us
    mul x1, other arithmetic, wendland(): return amplitude * remain ** 4 * (1.0 + 4.0 * scaled)  26.8 us
    ppermute x5, waiting for transfers between devices, day_order_halo(): high = lax.ppermute(field[:, :BW], axes, backward)  21.2 us
    ppermute x5, waiting for transfers between devices, day_order_halo(): low = lax.ppermute(field[:, field.shape[1] - BW:], axes, forward)  20.1 us
    all_to_all x1, blocking collectives, to_cells(): lax.all_to_all(chunked, 'space', split_axis=0, concat_axis=0, tiled=True)  19.5 us
    gather x6, local copies, waits for them, and re-layouts, block_product(): field[pattern].transpose(0, 2, 1, 3)  19.1 us
  transfers between devices with their start and end apart: 13, of which 10 were waited for; matrix products, arithmetic and copies ran while one was open for 11% of the time, Pallas kernels for 0%

profile of v6, /device:TPU:0, one launch (start us, length us, event | category | flops | bytes accessed | tf_op | source)
XLA Modules:
  0.0 334.4 jit_solution(11224099086831419785)
XLA Ops:
  6.6 2.3 gather_fusion.2
  8.9 1.4 slice_reduce_fusion.1
  10.3 1.7 fusion.251
  13.3 6.6 %fusion.227 = f32[128,1024]{1,0:T(8,128)S(1)} fusion(f32[136,1024]{1,0:T(8,128)S(1)} %constant_dynamic-update-slice_fusion.2, f32[136,1024]{1,0:T(8,128)S(1)} %get-tuple-element.27, f32[128,1024]{1,0:T(8,128)S(1)} %copy-done, f32[]{:T(128)} %bitcast.10, f32[]{:T(128)} %bitcast.9, f32[]{:T(128)} %bitcast.8, f32[]{:T(128)} %bitcast.7, f32[]{:T(128)} %bitcast.6, ...), kind=kLoop, calls=%fused_computation.379 | loop fusion | flops 3276800 | bytes 9437220 | tf_op jit(solution)/shard_map/add | solution.py:65
  20.1 1.8 gather_fusion
  21.9 6.9 %all-to-all-start = ((f32[8,3,16,1024]{3,2,1,0:T(8,128)}), f32[8,3,16,1024]{3,2,1,0:T(8,128)S(1)}, u32[]{:S(2)}, u32[]{:S(2)}) async-start(f32[8,3,16,1024]{3,2,1,0:T(8,128)} %gather_fusion), calls=%async_computation | async-start | bytes 3145728 | tf_op jit(solution)/shard_map/all_to_all | solution.py:84
  28.7 26.8 %add_multiply_fusion = f32[64,1024,128]{2,1,0:T(8,128)} fusion(f32[64,1024]{1,0:T(8,128)S(1)} %bitcast.140, f32[64,128]{1,0:T(8,128)S(1)} %bitcast.146, f32[64,1024]{1,0:T(8,128)S(1)} %bitcast.139, f32[64,128]{1,0:T(8,128)S(1)} %bitcast.145), kind=kLoop, calls=%fused_computation.9 | loop fusion | flops 117440512 | bytes 34144256 | tf_op jit(solution)/shard_map/mul | solution.py:21
  56.2 3.2 gather_fusion.1
  59.4 15.3 %bitcast_subtract_fusion = (f32[64,16,128]{2,1,0:T(8,128)S(1)}, f32[64,16,128]{2,1,0:T(8,128)S(1)}) fusion(f32[1,8,8,16,128]{4,3,2,1,0:T(8,128)S(1)} %copy.28, f32[64,1024,128]{2,1,0:T(8,128)} %add_multiply_fusion, f32[64,8,2,8,128]{4,3,2,1,0:T(8,128)} %bitcast.121), kind=kOutput, calls=%fused_computation.401 | convolution fusion | flops 805437440 | bytes 39321600 | tf_op jit(solution)/shard_map/rkc,rdk->rdc/dot_general | solution.py:72
  74.8 3.8 %collective-permute-start.2 = (f32[64,8,128]{2,1,0:T(8,128)S(1)}, f32[64,8,128]{2,1,0:T(8,128)S(1)}, u32[]{:S(2)}, u32[]{:S(2)}) collective-permute-start(f32[64,8,128]{2,1,0:T(8,128)S(1)} %get-tuple-element.25), channel_id=1, source_target_pairs={{0,16},{16,32},{32,48},{48,112},{112,96},{96,80},{80,64},{64,1},{1... | collective-permute-start | bytes 786440 | tf_op jit(solution)/shard_map/ppermute | solution.py:42
  78.6 1.5 collective-permute-start.3
  80.2 4.2 %collective-permute-done.2 = f32[64,8,128]{2,1,0:T(8,128)S(1)} collective-permute-done((f32[64,8,128]{2,1,0:T(8,128)S(1)}, f32[64,8,128]{2,1,0:T(8,128)S(1)}, u32[]{:S(2)}, u32[]{:S(2)}) %collective-permute-start.2) | collective-permute-done | bytes 262176 | tf_op jit(solution)/shard_map/ppermute | solution.py:42
  84.4 4.7 %collective-permute-done.3 = f32[64,8,128]{2,1,0:T(8,128)S(1)} collective-permute-done((f32[64,8,128]{2,1,0:T(8,128)S(1)}, f32[64,8,128]{2,1,0:T(8,128)S(1)}, u32[]{:S(2)}, u32[]{:S(2)}) %collective-permute-start.3) | collective-permute-done | bytes 262176 | tf_op jit(solution)/shard_map/ppermute | solution.py:43
  89.1 7.0 %fusion.184 = f32[64,16,128]{2,1,0:T(8,128)S(1)} fusion(f32[64,16,128]{2,1,0:T(8,128)S(1)} %get-tuple-element.42, f32[64,8,128]{2,1,0:T(8,128)S(1)} %collective-permute-done.3, f32[64,8,128]{2,1,0:T(8,128)S(1)} %collective-permute-done.2, f32[]{:T(128)} %bitcast.10, f32[]{:T(128)} %bitcast.9, f32[]{:T(128)} %bitcast.8, f32[]{:T(128)} %bitcast.7, ...), kind=kLoop, calls=%fused_computation.325 | loop fusion | flops 5373952 | bytes 1572900 | tf_op jit(solution)/shard_map/add | solution.py:65
  96.1 3.2 gather_fusion.3
  99.3 15.3 %fusion.252 = (f32[64,16,128]{2,1,0:T(8,128)S(1)}, f32[64,16,128]{2,1,0:T(8,128)S(1)}) fusion(f32[64,16,128]{2,1,0:T(8,128)S(1)} %bitcast.130, f32[64,1024,128]{2,1,0:T(8,128)} %add_multiply_fusion, f32[64,8,2,8,128]{4,3,2,1,0:T(8,128)} %bitcast.122), kind=kOutput, calls=%fused_computation.433 | convolution fusion | flops 805568512 | bytes 39321600 | tf_op jit(solution)/shard_map/rkc,rdk->rdc/dot_general | solution.py:72
  114.6 3.4 %collective-permute-start.4 = (f32[64,8,128]{2,1,0:T(8,128)S(1)}, f32[64,8,128]{2,1,0:T(8,128)S(1)}, u32[]{:S(2)}, u32[]{:S(2)}) collective-permute-start(f32[64,8,128]{2,1,0:T(8,128)S(1)} %get-tuple-element.23), channel_id=1, source_target_pairs={{0,16},{16,32},{32,48},{48,112},{112,96},{96,80},{80,64},{64,1},{1... | collective-permute-start | bytes 786440 | tf_op jit(solution)/shard_map/ppermute | solution.py:42
  119.3 4.8 %collective-permute-done.4 = f32[64,8,128]{2,1,0:T(8,128)S(1)} collective-permute-done((f32[64,8,128]{2,1,0:T(8,128)S(1)}, f32[64,8,128]{2,1,0:T(8,128)S(1)}, u32[]{:S(2)}, u32[]{:S(2)}) %collective-permute-start.4) | collective-permute-done | bytes 262176 | tf_op jit(solution)/shard_map/ppermute | solution.py:42
  124.1 4.1 %collective-permute-done.5 = f32[64,8,128]{2,1,0:T(8,128)S(1)} collective-permute-done((f32[64,8,128]{2,1,0:T(8,128)S(1)}, f32[64,8,128]{2,1,0:T(8,128)S(1)}, u32[]{:S(2)}, u32[]{:S(2)}) %collective-permute-start.5) | collective-permute-done | bytes 262176 | tf_op jit(solution)/shard_map/ppermute | solution.py:43
  128.2 7.0 %fusion.148 = f32[64,16,128]{2,1,0:T(8,128)S(1)} fusion(f32[64,16,128]{2,1,0:T(8,128)S(1)} %get-tuple-element.44, f32[64,8,128]{2,1,0:T(8,128)S(1)} %collective-permute-done.5, f32[64,8,128]{2,1,0:T(8,128)S(1)} %collective-permute-done.4, f32[]{:T(128)} %bitcast.10, f32[]{:T(128)} %bitcast.9, f32[]{:T(128)} %bitcast.8, f32[]{:T(128)} %bitcast.7, ...), kind=kLoop, calls=%fused_computation.289 | loop fusion | flops 5373952 | bytes 1572900 | tf_op jit(solution)/shard_map/add | solution.py:65
  135.2 3.2 gather_fusion.4
  138.4 15.3 %fusion.24 = f32[64,16,128]{2,1,0:T(8,128)S(1)} fusion(f32[64,16,128]{2,1,0:T(8,128)S(1)} %get-tuple-element.43, f32[64,1024,128]{2,1,0:T(8,128)} %add_multiply_fusion, f32[64,8,2,8,128]{4,3,2,1,0:T(8,128)} %bitcast.123), kind=kOutput, calls=%fused_computation.172 | convolution fusion | flops 805437440 | bytes 38797312 | tf_op jit(solution)/shard_map/rkc,rdk->rdc/dot_general | solution.py:72
  153.7 3.1 collective-permute-start.6
  156.8 1.5 collective-permute-start.7
  158.3 3.5 %collective-permute-done.6 = f32[64,8,128]{2,1,0:T(8,128)S(1)} collective-permute-done((f32[64,8,128]{2,1,0:T(8,128)S(1)}, f32[64,8,128]{2,1,0:T(8,128)S(1)}, u32[]{:S(2)}, u32[]{:S(2)}) %collective-permute-start.6) | collective-permute-done | bytes 262176 | tf_op jit(solution)/shard_map/ppermute | solution.py:42
  161.8 4.1 %collective-permute-done.7 = f32[64,8,128]{2,1,0:T(8,128)S(1)} collective-permute-done((f32[64,8,128]{2,1,0:T(8,128)S(1)}, f32[64,8,128]{2,1,0:T(8,128)S(1)}, u32[]{:S(2)}, u32[]{:S(2)}) %collective-permute-start.7) | collective-permute-done | bytes 262176 | tf_op jit(solution)/shard_map/ppermute | solution.py:43
  165.9 7.0 %fusion.112 = f32[64,16,128]{2,1,0:T(8,128)S(1)} fusion(f32[64,16,128]{2,1,0:T(8,128)S(1)} %fusion.24, f32[64,8,128]{2,1,0:T(8,128)S(1)} %collective-permute-done.7, f32[64,8,128]{2,1,0:T(8,128)S(1)} %collective-permute-done.6, f32[]{:T(128)} %bitcast.10, f32[]{:T(128)} %bitcast.9, f32[]{:T(128)} %bitcast.8, f32[]{:T(128)} %bitcast.7, f32[]{:T(128)} %bitcast.6, ...), kind=kLoop, calls=%fused_computation.253 | loop fusion | flops 5373952 | bytes 1572900 | tf_op jit(solution)/shard_map/add | solution.py:65
  172.9 3.2 gather_fusion.5
  176.0 15.3 %negate_multiply_fusion = (f32[64,16,128]{2,1,0:T(8,128)S(1)}, f32[64,16,128]{2,1,0:T(8,128)S(1)}, f32[64,16,128]{2,1,0:T(8,128)S(1)}, f32[64,16,128]{2,1,0:T(8,128)S(1)}) fusion(f32[64,16,128]{2,1,0:T(8,128)S(1)} %get-tuple-element.45, f32[64,1024,128]{2,1,0:T(8,128)} %add_multiply_fusion, f32[64,8,2,8,128]{4,3,2,1,0:T(8,128)} %bitcast.119), kind=kOutput, calls=%fused_computation.422 | convolution fusion | flops 805961728 | bytes 40370176 | tf_op jit(solution)/shard_map/rkc,rdk->rdc/dot_general | solution.py:72
  192.1 8.1 %shard_map.86.x_ref = f32[8,128]{1,0:T(8,128)} custom-call(f32[8,128]{1,0:T(8,128)} %pad.8.x_ref), custom_call_target="tpu_custom_call" | custom-call | tf_op jit(solution)/shard_map/pallas_call | solution.py:144
  200.2 11.0 %shard_map.87 = f32[8,128]{1,0:T(8,128)} custom-call(f32[8,128]{1,0:T(8,128)} %shard_map.86.x_ref), custom_call_target="tpu_custom_call" | custom-call | tf_op jit(solution)/shard_map/pallas_call | solution.py:144
  211.2 1.4 slice_reduce_fusion.3
  216.0 2.5 collective-permute-start.8
  219.8 4.5 %collective-permute-done.8 = f32[64,8,128]{2,1,0:T(8,128)S(1)} collective-permute-done((f32[64,8,128]{2,1,0:T(8,128)S(1)}, f32[64,8,128]{2,1,0:T(8,128)S(1)}, u32[]{:S(2)}, u32[]{:S(2)}) %collective-permute-start.8) | collective-permute-done | bytes 262176 | tf_op jit(solution)/shard_map/ppermute | solution.py:42
  224.3 4.1 %collective-permute-done.9 = f32[64,8,128]{2,1,0:T(8,128)S(1)} collective-permute-done((f32[64,8,128]{2,1,0:T(8,128)S(1)}, f32[64,8,128]{2,1,0:T(8,128)S(1)}, u32[]{:S(2)}, u32[]{:S(2)}) %collective-permute-start.9) | collective-permute-done | bytes 262176 | tf_op jit(solution)/shard_map/ppermute | solution.py:43
  228.4 7.0 %fusion.76 = f32[64,16,128]{2,1,0:T(8,128)S(1)} fusion(f32[64,16,128]{2,1,0:T(8,128)S(1)} %multiply_add_fusion.1, f32[64,8,128]{2,1,0:T(8,128)S(1)} %collective-permute-done.9, f32[64,8,128]{2,1,0:T(8,128)S(1)} %collective-permute-done.8, f32[]{:T(128)} %bitcast.10, f32[]{:T(128)} %bitcast.9, f32[]{:T(128)} %bitcast.8, f32[]{:T(128)} %bitcast.7, ...), kind=kLoop, calls=%fused_computation.217 | loop fusion | flops 5373952 | bytes 1572900 | tf_op jit(solution)/shard_map/add | solution.py:65
  235.4 3.2 gather_fusion.6
  238.6 15.3 %fusion.30 = f32[64,16,128]{2,1,0:T(8,128)S(1)} fusion(f32[64,16,128]{2,1,0:T(8,128)S(1)} %get-tuple-element.43, f32[64,1024,128]{2,1,0:T(8,128)} %add_multiply_fusion, f32[64,8,2,8,128]{4,3,2,1,0:T(8,128)} %bitcast.124), kind=kOutput, calls=%fused_computation.174 | convolution fusion | flops 805437440 | bytes 38797312 | tf_op jit(solution)/shard_map/rkc,rdk->rdc/dot_general | solution.py:72
  253.9 3.1 collective-permute-start.10
  257.0 1.6 collective-permute-start.11
  258.6 3.1 collective-permute-done.10
  261.7 4.1 %collective-permute-done.11 = f32[64,8,128]{2,1,0:T(8,128)S(1)} collective-permute-done((f32[64,8,128]{2,1,0:T(8,128)S(1)}, f32[64,8,128]{2,1,0:T(8,128)S(1)}, u32[]{:S(2)}, u32[]{:S(2)}) %collective-permute-start.11) | collective-permute-done | bytes 262176 | tf_op jit(solution)/shard_map/ppermute | solution.py:43
  265.8 7.0 %fusion.40 = f32[64,16,128]{2,1,0:T(8,128)S(1)} fusion(f32[64,16,128]{2,1,0:T(8,128)S(1)} %fusion.30, f32[64,8,128]{2,1,0:T(8,128)S(1)} %collective-permute-done.11, f32[64,8,128]{2,1,0:T(8,128)S(1)} %collective-permute-done.10, f32[]{:T(128)} %bitcast.10, f32[]{:T(128)} %bitcast.9, f32[]{:T(128)} %bitcast.8, f32[]{:T(128)} %bitcast.7, f32[]{:T(128)} %bitcast.6, ...), kind=kLoop, calls=%fused_computation.181 | loop fusion | flops 5373952 | bytes 1572900 | tf_op jit(solution)/shard_map/add | solution.py:65
  272.7 3.2 gather_fusion.7
  275.9 15.3 %multiply_reduce_fusion = (f32[128]{0:T(128)S(1)}, f32[64,16,128]{2,1,0:T(8,128)S(1)}) fusion(f32[64,16,128]{2,1,0:T(8,128)S(1)} %multiply_add_fusion.1, f32[64,1024,128]{2,1,0:T(8,128)} %add_multiply_fusion, f32[64,8,2,8,128]{4,3,2,1,0:T(8,128)} %bitcast.120), kind=kOutput, calls=%fused_computation.404 | convolution fusion | flops 805699456 | bytes 38797824 | tf_op jit(solution)/shard_map/rkc,rdk->rdc/dot_general | solution.py:72
  291.8 8.3 %shard_map.88.x_ref = f32[8,128]{1,0:T(8,128)} custom-call(f32[8,128]{1,0:T(8,128)} %pad.9.x_ref), custom_call_target="tpu_custom_call" | custom-call | tf_op jit(solution)/shard_map/pallas_call | solution.py:144
  300.2 10.4 %shard_map.89 = f32[8,128]{1,0:T(8,128)} custom-call(f32[8,128]{1,0:T(8,128)} %shard_map.88.x_ref), custom_call_target="tpu_custom_call" | custom-call | tf_op jit(solution)/shard_map/pallas_call | solution.py:144
  313.3 19.5 %all_to_all.10 = f32[8,2,16,1024]{3,2,1,0:T(8,128)S(1)} all-to-all(f32[8,2,16,1024]{3,2,1,0:T(8,128)S(1)} %reshape.88), channel_id=1, replica_groups=mesh['space'=8,'tm'=16] {'space'}, dimensions={0} | all-to-all | bytes 2097152 | tf_op jit(solution)/shard_map/all_to_all | solution.py:95
  (44 shorter events, 16.0 us)
Async XLA Ops:
  0.6 12.5 %copy-start = (f32[128,1024]{1,0:T(8,128)S(1)}, f32[128,1024]{1,0:T(8,128)}, u32[]{:S(2)}) copy-start(f32[128,1024]{1,0:T(8,128)} %param.7) | copy-start | bytes 1572868
  1.5 11.7 %collective-permute-start = (f32[8,1024]{1,0:T(8,128)S(1)}, f32[8,1024]{1,0:T(8,128)S(1)}, u32[]{:S(2)}, u32[]{:S(2)}) collective-permute-start(f32[8,1024]{1,0:T(8,128)S(1)} %get-tuple-element.29), channel_id=1, source_target_pairs={{0,1},{1,2},{2,3},{3,4},{4,5},{5,6},{6,7},{7,8},{8,9},{9,10},{10,1... | collective-permute-start | bytes 98312 | tf_op jit(solution)/shard_map/ppermute | solution.py:51
  2.8 10.5 %collective-permute-start.1 = (f32[8,1024]{1,0:T(8,128)S(1)}, f32[8,1024]{1,0:T(8,128)S(1)}, u32[]{:S(2)}, u32[]{:S(2)}) collective-permute-start(f32[8,1024]{1,0:T(8,128)S(1)} %get-tuple-element.30), channel_id=1, source_target_pairs={{1,0},{2,1},{3,2},{4,3},{5,4},{6,5},{7,6},{8,7},{9,8},{10,9},{11,1... | collective-permute-start | bytes 98312 | tf_op jit(solution)/shard_map/ppermute | solution.py:52
  21.9 33.7 %all-to-all-start = ((f32[8,3,16,1024]{3,2,1,0:T(8,128)}), f32[8,3,16,1024]{3,2,1,0:T(8,128)S(1)}, u32[]{:S(2)}, u32[]{:S(2)}) async-start(f32[8,3,16,1024]{3,2,1,0:T(8,128)} %gather_fusion), calls=%async_computation | async-start | bytes 3145728 | tf_op jit(solution)/shard_map/all_to_all | solution.py:84
  74.8 9.6 %collective-permute-start.2 = (f32[64,8,128]{2,1,0:T(8,128)S(1)}, f32[64,8,128]{2,1,0:T(8,128)S(1)}, u32[]{:S(2)}, u32[]{:S(2)}) collective-permute-start(f32[64,8,128]{2,1,0:T(8,128)S(1)} %get-tuple-element.25), channel_id=1, source_target_pairs={{0,16},{16,32},{32,48},{48,112},{112,96},{96,80},{80,64},{64,1},{1... | collective-permute-start | bytes 786440 | tf_op jit(solution)/shard_map/ppermute | solution.py:42
  78.6 10.5 %collective-permute-start.3 = (f32[64,8,128]{2,1,0:T(8,128)S(1)}, f32[64,8,128]{2,1,0:T(8,128)S(1)}, u32[]{:S(2)}, u32[]{:S(2)}) collective-permute-start(f32[64,8,128]{2,1,0:T(8,128)S(1)} %get-tuple-element.26), channel_id=1, source_target_pairs={{16,0},{32,16},{48,32},{112,48},{96,112},{80,96},{64,80},{1,64},{1... | collective-permute-start | bytes 786440 | tf_op jit(solution)/shard_map/ppermute | solution.py:43
  114.6 9.5 %collective-permute-start.4 = (f32[64,8,128]{2,1,0:T(8,128)S(1)}, f32[64,8,128]{2,1,0:T(8,128)S(1)}, u32[]{:S(2)}, u32[]{:S(2)}) collective-permute-start(f32[64,8,128]{2,1,0:T(8,128)S(1)} %get-tuple-element.23), channel_id=1, source_target_pairs={{0,16},{16,32},{32,48},{48,112},{112,96},{96,80},{80,64},{64,1},{1... | collective-permute-start | bytes 786440 | tf_op jit(solution)/shard_map/ppermute | solution.py:42
  118.0 10.2 %collective-permute-start.5 = (f32[64,8,128]{2,1,0:T(8,128)S(1)}, f32[64,8,128]{2,1,0:T(8,128)S(1)}, u32[]{:S(2)}, u32[]{:S(2)}) collective-permute-start(f32[64,8,128]{2,1,0:T(8,128)S(1)} %get-tuple-element.24), channel_id=1, source_target_pairs={{16,0},{32,16},{48,32},{112,48},{96,112},{80,96},{64,80},{1,64},{1... | collective-permute-start | bytes 786440 | tf_op jit(solution)/shard_map/ppermute | solution.py:43
  153.7 8.1 %collective-permute-start.6 = (f32[64,8,128]{2,1,0:T(8,128)S(1)}, f32[64,8,128]{2,1,0:T(8,128)S(1)}, u32[]{:S(2)}, u32[]{:S(2)}) collective-permute-start(f32[64,8,128]{2,1,0:T(8,128)S(1)} %get-tuple-element.21), channel_id=1, source_target_pairs={{0,16},{16,32},{32,48},{48,112},{112,96},{96,80},{80,64},{64,1},{1... | collective-permute-start | bytes 786440 | tf_op jit(solution)/shard_map/ppermute | solution.py:42
  156.8 9.1 %collective-permute-start.7 = (f32[64,8,128]{2,1,0:T(8,128)S(1)}, f32[64,8,128]{2,1,0:T(8,128)S(1)}, u32[]{:S(2)}, u32[]{:S(2)}) collective-permute-start(f32[64,8,128]{2,1,0:T(8,128)S(1)} %get-tuple-element.22), channel_id=1, source_target_pairs={{16,0},{32,16},{48,32},{112,48},{96,112},{80,96},{64,80},{1,64},{1... | collective-permute-start | bytes 786440 | tf_op jit(solution)/shard_map/ppermute | solution.py:43
  216.0 8.3 %collective-permute-start.8 = (f32[64,8,128]{2,1,0:T(8,128)S(1)}, f32[64,8,128]{2,1,0:T(8,128)S(1)}, u32[]{:S(2)}, u32[]{:S(2)}) collective-permute-start(f32[64,8,128]{2,1,0:T(8,128)S(1)} %get-tuple-element.19), channel_id=1, source_target_pairs={{0,16},{16,32},{32,48},{48,112},{112,96},{96,80},{80,64},{64,1},{1... | collective-permute-start | bytes 786440 | tf_op jit(solution)/shard_map/ppermute | solution.py:42
  218.5 9.9 %collective-permute-start.9 = (f32[64,8,128]{2,1,0:T(8,128)S(1)}, f32[64,8,128]{2,1,0:T(8,128)S(1)}, u32[]{:S(2)}, u32[]{:S(2)}) collective-permute-start(f32[64,8,128]{2,1,0:T(8,128)S(1)} %get-tuple-element.20), channel_id=1, source_target_pairs={{16,0},{32,16},{48,32},{112,48},{96,112},{80,96},{64,80},{1,64},{1... | collective-permute-start | bytes 786440 | tf_op jit(solution)/shard_map/ppermute | solution.py:43
  253.9 7.8 %collective-permute-start.10 = (f32[64,8,128]{2,1,0:T(8,128)S(1)}, f32[64,8,128]{2,1,0:T(8,128)S(1)}, u32[]{:S(2)}, u32[]{:S(2)}) collective-permute-start(f32[64,8,128]{2,1,0:T(8,128)S(1)} %get-tuple-element.17), channel_id=1, source_target_pairs={{0,16},{16,32},{32,48},{48,112},{112,96},{96,80},{80,64},{64,1},{1... | collective-permute-start | bytes 786440 | tf_op jit(solution)/shard_map/ppermute | solution.py:42
  257.0 8.8 %collective-permute-start.11 = (f32[64,8,128]{2,1,0:T(8,128)S(1)}, f32[64,8,128]{2,1,0:T(8,128)S(1)}, u32[]{:S(2)}, u32[]{:S(2)}) collective-permute-start(f32[64,8,128]{2,1,0:T(8,128)S(1)} %get-tuple-element.18), channel_id=1, source_target_pairs={{16,0},{32,16},{48,32},{112,48},{96,112},{80,96},{64,80},{1,64},{1... | collective-permute-start | bytes 786440 | tf_op jit(solution)/shard_map/ppermute | solution.py:43

commit v7 on v6

--- a/solution.py
+++ b/solution.py
@@ -60,10 +60,14 @@
     def days(start):
         return lax.slice_in_dim(padded, start, start + length, axis=axis)
 
-    summed = temporal_taps[0] * field
-    for offset in range(1, BW + 1):
-        summed = summed + temporal_taps[offset] * (days(BW - offset) + days(BW + offset))
-    return summed
+    if axis == 0:
+        summed = temporal_taps[0] * field
+        for offset in range(1, BW + 1):
+            summed = summed + temporal_taps[offset] * (days(BW - offset) + days(BW + offset))
+        return summed
+    lag = jnp.arange(length + 2 * BW)[None, :] - jnp.arange(length)[:, None] - BW
+    band = jnp.where(jnp.abs(lag) <= BW, temporal_taps[jnp.clip(jnp.abs(lag), 0, BW)], 0.0)
+    return jnp.einsum("de,rec->rdc", band, padded, precision=lax.Precision.HIGHEST)
 
 
 def block_product(field, weights, pattern):

time: 336 us -> 304 us (0.905)
  other arithmetic: 73.9 us -> 39 us
  matrix products: 91.7 us -> 95.2 us
  waiting for transfers between devices: 41.3 us -> 37.8 us
  local copies, waits for them, and re-layouts: 32.8 us -> 36.2 us
    add x6 -> x1, other arithmetic: 41.4 us -> 6.44 us  [band_product(): summed + temporal_taps[offset] * (days(BW - offset) + days(BW + offset))]
    ppermute x5, waiting for transfers between devices: 20.1 us -> 16.7 us  [day_order_halo(): low = lax.ppermute(field[:, field.shape[1] - BW:], axes, forward)]
    gather x0 -> x2, local copies, waits for them, and re-layouts: none -> 3.42 us  [band_product(): temporal_taps[jnp.clip(jnp.abs(lag), 0, BW)]]
    dot_general x0 -> x5, matrix products: none -> 3.42 us  [band_product(): jnp.einsum('de,rec->rdc', band, padded, precision=lax.Precision.HIGHEST)]
  transfers between devices with their start and end apart: 13 -> 13, of which waited for: 10 -> 10; matrix products, arithmetic and copies ran while one was open for 11% -> 13% of each run, Pallas kernels for 0% -> 0%
where the time goes in v7:
time: 304 us; the launch traced here: 303 us
  matrix products  95.2 us (31%)
  other arithmetic  39 us (13%)
  waiting for transfers between devices  37.8 us (12%)
  Pallas kernels  37.8 us (12%)
  local copies, waits for them, and re-layouts  36.2 us (12%)
  starting transfers between devices  32.5 us (11%)
  blocking collectives  19.5 us (6%)
  between operations  5.1 us (2%)
    dot_general x6, matrix products, block_product(): jnp.einsum('rkc,rdk->rdc', weights, picked, precision=lax.Precision.HIGH)  91.7 us
    pallas_call x4, Pallas kernels, group_sum(): pl.pallas_call(functools.partial(group_sum_kernel, axis), out_shape=jax.S...  37.8 us
    mul x1, other arithmetic, wendland(): return amplitude * remain ** 4 * (1.0 + 4.0 * scaled)  26.8 us
    ppermute x5, waiting for transfers between devices, day_order_halo(): high = lax.ppermute(field[:, :BW], axes, backward)  21.2 us
    all_to_all x1, blocking collectives, to_cells(): lax.all_to_all(chunked, 'space', split_axis=0, concat_axis=0, tiled=True)  19.5 us
    gather x6, local copies, waits for them, and re-layouts, block_product(): field[pattern].transpose(0, 2, 1, 3)  19.1 us
    ppermute x5, waiting for transfers between devices, day_order_halo(): low = lax.ppermute(field[:, field.shape[1] - BW:], axes, forward)  16.7 us
    ppermute x5, starting transfers between devices, day_order_halo(): low = lax.ppermute(field[:, field.shape[1] - BW:], axes, forward)  15.9 us
  transfers between devices with their start and end apart: 13, of which 10 were waited for; matrix products, arithmetic and copies ran while one was open for 13% of the time, Pallas kernels for 0%

profile of v7, /device:TPU:0, one launch (start us, length us, event | category | flops | bytes accessed | tf_op | source)
XLA Modules:
  0.0 303.1 jit_solution(6327950861223619455)
XLA Ops:
  1.5 1.3 collective-permute-start
  2.8 1.3 collective-permute-start.1
  4.8 1.7 fusion.102
  7.7 2.3 gather_fusion.2
  10.0 1.4 slice_reduce_fusion.1
  13.4 6.4 %fusion.62 = f32[128,1024]{1,0:T(8,128)S(1)} fusion(f32[136,1024]{1,0:T(8,128)S(1)} %constant_dynamic-update-slice_fusion.2, f32[136,1024]{1,0:T(8,128)S(1)} %get-tuple-element.27, f32[128,1024]{1,0:T(8,128)S(1)} %copy-done.1, f32[]{:T(128)} %bitcast.10, f32[]{:T(128)} %bitcast.9, f32[]{:T(128)} %bitcast.8, f32[]{:T(128)} %bitcast.7, f32[]{:T(128)} %bitcast.6, ...), kind=kLoop, calls=%fused_computation.70 | loop fusion | flops 3276800 | bytes 9437220 | tf_op jit(solution)/shard_map/add | solution.py:66
  20.0 1.8 gather_fusion
  21.8 6.9 %all-to-all-start = ((f32[8,3,16,1024]{3,2,1,0:T(8,128)}), f32[8,3,16,1024]{3,2,1,0:T(8,128)S(1)}, u32[]{:S(2)}, u32[]{:S(2)}) async-start(f32[8,3,16,1024]{3,2,1,0:T(8,128)} %gather_fusion), calls=%async_computation | async-start | bytes 3145728 | tf_op jit(solution)/shard_map/all_to_all | solution.py:88
  28.7 26.8 %add_multiply_fusion = f32[64,1024,128]{2,1,0:T(8,128)} fusion(f32[64,1024]{1,0:T(8,128)S(1)} %bitcast.163, f32[64,128]{1,0:T(8,128)S(1)} %bitcast.169, f32[64,1024]{1,0:T(8,128)S(1)} %bitcast.162, f32[64,128]{1,0:T(8,128)S(1)} %bitcast.168), kind=kLoop, calls=%fused_computation.10 | loop fusion | flops 117440512 | bytes 34144256 | tf_op jit(solution)/shard_map/mul | solution.py:21
  56.1 3.2 %gather_fusion.1 = f32[512,16,128]{2,1,0:T(8,128)} fusion(f32[64,16,128]{2,1,0:T(8,128)S(1)} %bitcast.141, s32[1024]{0:T(1024)S(1)} %get-tuple-element.50), kind=kCustom, calls=%fused_computation.1 | custom fusion | bytes 8390656 | tf_op jit(solution)/shard_map/gather | solution.py:75
  59.3 15.3 %bitcast_subtract_fusion = (f32[64,16,128]{2,1,0:T(8,128)S(1)}, f32[64,16,128]{2,1,0:T(8,128)S(1)}) fusion(f32[1,8,8,16,128]{4,3,2,1,0:T(8,128)S(1)} %copy.28, f32[64,1024,128]{2,1,0:T(8,128)} %add_multiply_fusion, f32[64,8,2,8,128]{4,3,2,1,0:T(8,128)} %bitcast.144), kind=kOutput, calls=%fused_computation.92 | convolution fusion | flops 805437440 | bytes 39321600 | tf_op jit(solution)/shard_map/rkc,rdk->rdc/dot_general | solution.py:76
  74.7 3.8 %collective-permute-start.2 = (f32[64,8,128]{2,1,0:T(8,128)S(1)}, f32[64,8,128]{2,1,0:T(8,128)S(1)}, u32[]{:S(2)}, u32[]{:S(2)}) collective-permute-start(f32[64,8,128]{2,1,0:T(8,128)S(1)} %get-tuple-element.25), channel_id=1, source_target_pairs={{0,16},{16,32},{32,48},{48,112},{112,96},{96,80},{80,64},{64,1},{1... | collective-permute-start | bytes 786440 | tf_op jit(solution)/shard_map/ppermute | solution.py:42
  78.6 1.5 collective-permute-start.3
  80.1 3.3 %gather_fusion.3 = f32[512]{0:T(512)S(1)} fusion(f32[9]{0:T(128)S(1)} %copy-done, s32[1024]{0:T(1024)S(1)} %get-tuple-element.49), kind=kCustom, calls=%fused_computation.3 | custom fusion | bytes 6144 | tf_op jit(solution)/shard_map/gather | solution.py:69
  84.4 4.7 %collective-permute-done.3 = f32[64,8,128]{2,1,0:T(8,128)S(1)} collective-permute-done((f32[64,8,128]{2,1,0:T(8,128)S(1)}, f32[64,8,128]{2,1,0:T(8,128)S(1)}, u32[]{:S(2)}, u32[]{:S(2)}) %collective-permute-start.3) | collective-permute-done | bytes 262176 | tf_op jit(solution)/shard_map/ppermute | solution.py:43
  89.8 3.2 %gather_fusion.4 = f32[512,16,128]{2,1,0:T(8,128)} fusion(f32[64,16,128]{2,1,0:T(8,128)S(1)} %convolution_bitcast_fusion.4, s32[1024]{0:T(1024)S(1)} %get-tuple-element.50), kind=kCustom, calls=%fused_computation.4 | custom fusion | bytes 8390656 | tf_op jit(solution)/shard_map/gather | solution.py:75
  92.9 15.3 %fusion.103 = (f32[64,16,128]{2,1,0:T(8,128)S(1)}, f32[64,16,128]{2,1,0:T(8,128)S(1)}) fusion(f32[64,16,128]{2,1,0:T(8,128)S(1)} %bitcast.153, f32[64,1024,128]{2,1,0:T(8,128)} %add_multiply_fusion, f32[64,8,2,8,128]{4,3,2,1,0:T(8,128)} %bitcast.145), kind=kOutput, calls=%fused_computation.138 | convolution fusion | flops 805568512 | bytes 39321600 | tf_op jit(solution)/shard_map/rkc,rdk->rdc/dot_general | solution.py:76
  108.3 3.4 %collective-permute-start.4 = (f32[64,8,128]{2,1,0:T(8,128)S(1)}, f32[64,8,128]{2,1,0:T(8,128)S(1)}, u32[]{:S(2)}, u32[]{:S(2)}) collective-permute-start(f32[64,8,128]{2,1,0:T(8,128)S(1)} %get-tuple-element.23), channel_id=1, source_target_pairs={{0,16},{16,32},{32,48},{48,112},{112,96},{96,80},{80,64},{64,1},{1... | collective-permute-start | bytes 786440 | tf_op jit(solution)/shard_map/ppermute | solution.py:42
  111.7 1.3 collective-permute-start.5
  113.0 4.8 %collective-permute-done.4 = f32[64,8,128]{2,1,0:T(8,128)S(1)} collective-permute-done((f32[64,8,128]{2,1,0:T(8,128)S(1)}, f32[64,8,128]{2,1,0:T(8,128)S(1)}, u32[]{:S(2)}, u32[]{:S(2)}) %collective-permute-start.4) | collective-permute-done | bytes 262176 | tf_op jit(solution)/shard_map/ppermute | solution.py:42
  117.8 4.1 %collective-permute-done.5 = f32[64,8,128]{2,1,0:T(8,128)S(1)} collective-permute-done((f32[64,8,128]{2,1,0:T(8,128)S(1)}, f32[64,8,128]{2,1,0:T(8,128)S(1)}, u32[]{:S(2)}, u32[]{:S(2)}) %collective-permute-start.5) | collective-permute-done | bytes 262176 | tf_op jit(solution)/shard_map/ppermute | solution.py:43
  122.6 3.2 %gather_fusion.5 = f32[512,16,128]{2,1,0:T(8,128)} fusion(f32[64,16,128]{2,1,0:T(8,128)S(1)} %convolution_bitcast_fusion.3, s32[1024]{0:T(1024)S(1)} %get-tuple-element.50), kind=kCustom, calls=%fused_computation.5 | custom fusion | bytes 8390656 | tf_op jit(solution)/shard_map/gather | solution.py:75
  125.8 15.3 %fusion.24 = f32[64,16,128]{2,1,0:T(8,128)S(1)} fusion(f32[64,16,128]{2,1,0:T(8,128)S(1)} %get-tuple-element.43, f32[64,1024,128]{2,1,0:T(8,128)} %add_multiply_fusion, f32[64,8,2,8,128]{4,3,2,1,0:T(8,128)} %bitcast.146), kind=kOutput, calls=%fused_computation.33 | convolution fusion | flops 805437440 | bytes 38797312 | tf_op jit(solution)/shard_map/rkc,rdk->rdc/dot_general | solution.py:76
  141.1 3.1 %collective-permute-start.6 = (f32[64,8,128]{2,1,0:T(8,128)S(1)}, f32[64,8,128]{2,1,0:T(8,128)S(1)}, u32[]{:S(2)}, u32[]{:S(2)}) collective-permute-start(f32[64,8,128]{2,1,0:T(8,128)S(1)} %get-tuple-element.21), channel_id=1, source_target_pairs={{0,16},{16,32},{32,48},{48,112},{112,96},{96,80},{80,64},{64,1},{1... | collective-permute-start | bytes 786440 | tf_op jit(solution)/shard_map/ppermute | solution.py:42
  144.2 1.5 collective-permute-start.7
  145.7 3.5 %collective-permute-done.6 = f32[64,8,128]{2,1,0:T(8,128)S(1)} collective-permute-done((f32[64,8,128]{2,1,0:T(8,128)S(1)}, f32[64,8,128]{2,1,0:T(8,128)S(1)}, u32[]{:S(2)}, u32[]{:S(2)}) %collective-permute-start.6) | collective-permute-done | bytes 262176 | tf_op jit(solution)/shard_map/ppermute | solution.py:42
  149.2 4.1 %collective-permute-done.7 = f32[64,8,128]{2,1,0:T(8,128)S(1)} collective-permute-done((f32[64,8,128]{2,1,0:T(8,128)S(1)}, f32[64,8,128]{2,1,0:T(8,128)S(1)}, u32[]{:S(2)}, u32[]{:S(2)}) %collective-permute-start.7) | collective-permute-done | bytes 262176 | tf_op jit(solution)/shard_map/ppermute | solution.py:43
  154.0 3.2 %gather_fusion.6 = f32[512,16,128]{2,1,0:T(8,128)} fusion(f32[64,16,128]{2,1,0:T(8,128)S(1)} %convolution_bitcast_fusion.2, s32[1024]{0:T(1024)S(1)} %get-tuple-element.50), kind=kCustom, calls=%fused_computation.6 | custom fusion | bytes 8390656 | tf_op jit(solution)/shard_map/gather | solution.py:75
  157.2 15.3 %negate_multiply_fusion = (f32[64,16,128]{2,1,0:T(8,128)S(1)}, f32[64,16,128]{2,1,0:T(8,128)S(1)}, f32[64,16,128]{2,1,0:T(8,128)S(1)}, f32[64,16,128]{2,1,0:T(8,128)S(1)}) fusion(f32[64,16,128]{2,1,0:T(8,128)S(1)} %get-tuple-element.45, f32[64,1024,128]{2,1,0:T(8,128)} %add_multiply_fusion, f32[64,8,2,8,128]{4,3,2,1,0:T(8,128)} %bitcast.142), kind=kOutput, calls=%fused_computation.127 | convolution fusion | flops 805961728 | bytes 40370176 | tf_op jit(solution)/shard_map/rkc,rdk->rdc/dot_general | solution.py:76
  173.2 8.1 %shard_map.86.x_ref = f32[8,128]{1,0:T(8,128)} custom-call(f32[8,128]{1,0:T(8,128)} %pad.8.x_ref), custom_call_target="tpu_custom_call" | custom-call | tf_op jit(solution)/shard_map/pallas_call | solution.py:148
  181.3 11.0 %shard_map.87 = f32[8,128]{1,0:T(8,128)} custom-call(f32[8,128]{1,0:T(8,128)} %shard_map.86.x_ref), custom_call_target="tpu_custom_call" | custom-call | tf_op jit(solution)/shard_map/pallas_call | solution.py:148
  192.3 1.4 slice_reduce_fusion.3
  197.2 2.5 collective-permute-start.8
  199.7 1.3 collective-permute-start.9
  201.0 4.5 %collective-permute-done.8 = f32[64,8,128]{2,1,0:T(8,128)S(1)} collective-permute-done((f32[64,8,128]{2,1,0:T(8,128)S(1)}, f32[64,8,128]{2,1,0:T(8,128)S(1)}, u32[]{:S(2)}, u32[]{:S(2)}) %collective-permute-start.8) | collective-permute-done | bytes 262176 | tf_op jit(solution)/shard_map/ppermute | solution.py:42
  205.5 4.1 %collective-permute-done.9 = f32[64,8,128]{2,1,0:T(8,128)S(1)} collective-permute-done((f32[64,8,128]{2,1,0:T(8,128)S(1)}, f32[64,8,128]{2,1,0:T(8,128)S(1)}, u32[]{:S(2)}, u32[]{:S(2)}) %collective-permute-start.9) | collective-permute-done | bytes 262176 | tf_op jit(solution)/shard_map/ppermute | solution.py:43
  210.3 3.2 %gather_fusion.7 = f32[512,16,128]{2,1,0:T(8,128)} fusion(f32[64,16,128]{2,1,0:T(8,128)S(1)} %convolution_bitcast_fusion.1, s32[1024]{0:T(1024)S(1)} %get-tuple-element.50), kind=kCustom, calls=%fused_computation.7 | custom fusion | bytes 8390656 | tf_op jit(solution)/shard_map/gather | solution.py:75
  213.5 15.3 %fusion.30 = f32[64,16,128]{2,1,0:T(8,128)S(1)} fusion(f32[64,16,128]{2,1,0:T(8,128)S(1)} %get-tuple-element.43, f32[64,1024,128]{2,1,0:T(8,128)} %add_multiply_fusion, f32[64,8,2,8,128]{4,3,2,1,0:T(8,128)} %bitcast.147), kind=kOutput, calls=%fused_computation.35 | convolution fusion | flops 805437440 | bytes 38797312 | tf_op jit(solution)/shard_map/rkc,rdk->rdc/dot_general | solution.py:76
  228.8 3.1 %collective-permute-start.10 = (f32[64,8,128]{2,1,0:T(8,128)S(1)}, f32[64,8,128]{2,1,0:T(8,128)S(1)}, u32[]{:S(2)}, u32[]{:S(2)}) collective-permute-start(f32[64,8,128]{2,1,0:T(8,128)S(1)} %get-tuple-element.17), channel_id=1, source_target_pairs={{0,16},{16,32},{32,48},{48,112},{112,96},{96,80},{80,64},{64,1},{1... | collective-permute-start | bytes 786440 | tf_op jit(solution)/shard_map/ppermute | solution.py:42
  231.9 1.6 collective-permute-start.11
  233.5 3.1 %collective-permute-done.10 = f32[64,8,128]{2,1,0:T(8,128)S(1)} collective-permute-done((f32[64,8,128]{2,1,0:T(8,128)S(1)}, f32[64,8,128]{2,1,0:T(8,128)S(1)}, u32[]{:S(2)}, u32[]{:S(2)}) %collective-permute-start.10) | collective-permute-done | bytes 262176 | tf_op jit(solution)/shard_map/ppermute | solution.py:42
  236.6 4.1 %collective-permute-done.11 = f32[64,8,128]{2,1,0:T(8,128)S(1)} collective-permute-done((f32[64,8,128]{2,1,0:T(8,128)S(1)}, f32[64,8,128]{2,1,0:T(8,128)S(1)}, u32[]{:S(2)}, u32[]{:S(2)}) %collective-permute-start.11) | collective-permute-done | bytes 262176 | tf_op jit(solution)/shard_map/ppermute | solution.py:43
  241.4 3.2 %gather_fusion.8 = f32[512,16,128]{2,1,0:T(8,128)} fusion(f32[64,16,128]{2,1,0:T(8,128)S(1)} %convolution_bitcast_fusion, s32[1024]{0:T(1024)S(1)} %get-tuple-element.50), kind=kCustom, calls=%fused_computation.8 | custom fusion | bytes 8390656 | tf_op jit(solution)/shard_map/gather | solution.py:75
  244.6 15.3 %multiply_reduce_fusion = (f32[128]{0:T(128)S(1)}, f32[64,16,128]{2,1,0:T(8,128)S(1)}) fusion(f32[64,16,128]{2,1,0:T(8,128)S(1)} %multiply_add_fusion.1, f32[64,1024,128]{2,1,0:T(8,128)} %add_multiply_fusion, f32[64,8,2,8,128]{4,3,2,1,0:T(8,128)} %bitcast.143), kind=kOutput, calls=%fused_computation.95 | convolution fusion | flops 805699456 | bytes 38797824 | tf_op jit(solution)/shard_map/rkc,rdk->rdc/dot_general | solution.py:76
  260.5 8.3 %shard_map.88.x_ref = f32[8,128]{1,0:T(8,128)} custom-call(f32[8,128]{1,0:T(8,128)} %pad.9.x_ref), custom_call_target="tpu_custom_call" | custom-call | tf_op jit(solution)/shard_map/pallas_call | solution.py:148
  268.8 10.4 %shard_map.89 = f32[8,128]{1,0:T(8,128)} custom-call(f32[8,128]{1,0:T(8,128)} %shard_map.88.x_ref), custom_call_target="tpu_custom_call" | custom-call | tf_op jit(solution)/shard_map/pallas_call | solution.py:148
  279.2 1.3 slice_reduce_fusion.2
  281.9 19.5 %all_to_all.10 = f32[8,2,16,1024]{3,2,1,0:T(8,128)S(1)} all-to-all(f32[8,2,16,1024]{3,2,1,0:T(8,128)S(1)} %reshape.122), channel_id=1, replica_groups=mesh['space'=8,'tm'=16] {'space'}, dimensions={0} | all-to-all | bytes 2097152 | tf_op jit(solution)/shard_map/all_to_all | solution.py:99
  (51 shorter events, 13.9 us)
Async XLA Ops:
  0.6 12.6 %copy-start.1 = (f32[128,1024]{1,0:T(8,128)S(1)}, f32[128,1024]{1,0:T(8,128)}, u32[]{:S(2)}) copy-start(f32[128,1024]{1,0:T(8,128)} %param.7) | copy-start | bytes 1572868
  1.5 11.8 %collective-permute-start = (f32[8,1024]{1,0:T(8,128)S(1)}, f32[8,1024]{1,0:T(8,128)S(1)}, u32[]{:S(2)}, u32[]{:S(2)}) collective-permute-start(f32[8,1024]{1,0:T(8,128)S(1)} %get-tuple-element.29), channel_id=1, source_target_pairs={{0,1},{1,2},{2,3},{3,4},{4,5},{5,6},{6,7},{7,8},{8,9},{9,10},{10,1... | collective-permute-start | bytes 98312 | tf_op jit(solution)/shard_map/ppermute | solution.py:51
  2.8 10.6 %collective-permute-start.1 = (f32[8,1024]{1,0:T(8,128)S(1)}, f32[8,1024]{1,0:T(8,128)S(1)}, u32[]{:S(2)}, u32[]{:S(2)}) collective-permute-start(f32[8,1024]{1,0:T(8,128)S(1)} %get-tuple-element.30), channel_id=1, source_target_pairs={{1,0},{2,1},{3,2},{4,3},{5,4},{6,5},{7,6},{8,7},{9,8},{10,9},{11,1... | collective-permute-start | bytes 98312 | tf_op jit(solution)/shard_map/ppermute | solution.py:52
  21.8 33.7 %all-to-all-start = ((f32[8,3,16,1024]{3,2,1,0:T(8,128)}), f32[8,3,16,1024]{3,2,1,0:T(8,128)S(1)}, u32[]{:S(2)}, u32[]{:S(2)}) async-start(f32[8,3,16,1024]{3,2,1,0:T(8,128)} %gather_fusion), calls=%async_computation | async-start | bytes 3145728 | tf_op jit(solution)/shard_map/all_to_all | solution.py:88
  74.7 5.4 %copy-start = (f32[9]{0:T(128)S(1)}, f32[9]{0:T(128)}, u32[]{:S(2)}) copy-start(f32[9]{0:T(128)} %param.11) | copy-start | bytes 112
  74.7 9.6 %collective-permute-start.2 = (f32[64,8,128]{2,1,0:T(8,128)S(1)}, f32[64,8,128]{2,1,0:T(8,128)S(1)}, u32[]{:S(2)}, u32[]{:S(2)}) collective-permute-start(f32[64,8,128]{2,1,0:T(8,128)S(1)} %get-tuple-element.25), channel_id=1, source_target_pairs={{0,16},{16,32},{32,48},{48,112},{112,96},{96,80},{80,64},{64,1},{1... | collective-permute-start | bytes 786440 | tf_op jit(solution)/shard_map/ppermute | solution.py:42
  78.6 10.5 %collective-permute-start.3 = (f32[64,8,128]{2,1,0:T(8,128)S(1)}, f32[64,8,128]{2,1,0:T(8,128)S(1)}, u32[]{:S(2)}, u32[]{:S(2)}) collective-permute-start(f32[64,8,128]{2,1,0:T(8,128)S(1)} %get-tuple-element.26), channel_id=1, source_target_pairs={{16,0},{32,16},{48,32},{112,48},{96,112},{80,96},{64,80},{1,64},{1... | collective-permute-start | bytes 786440 | tf_op jit(solution)/shard_map/ppermute | solution.py:43
  108.3 9.5 %collective-permute-start.4 = (f32[64,8,128]{2,1,0:T(8,128)S(1)}, f32[64,8,128]{2,1,0:T(8,128)S(1)}, u32[]{:S(2)}, u32[]{:S(2)}) collective-permute-start(f32[64,8,128]{2,1,0:T(8,128)S(1)} %get-tuple-element.23), channel_id=1, source_target_pairs={{0,16},{16,32},{32,48},{48,112},{112,96},{96,80},{80,64},{64,1},{1... | collective-permute-start | bytes 786440 | tf_op jit(solution)/shard_map/ppermute | solution.py:42
  111.7 10.2 %collective-permute-start.5 = (f32[64,8,128]{2,1,0:T(8,128)S(1)}, f32[64,8,128]{2,1,0:T(8,128)S(1)}, u32[]{:S(2)}, u32[]{:S(2)}) collective-permute-start(f32[64,8,128]{2,1,0:T(8,128)S(1)} %get-tuple-element.24), channel_id=1, source_target_pairs={{16,0},{32,16},{48,32},{112,48},{96,112},{80,96},{64,80},{1,64},{1... | collective-permute-start | bytes 786440 | tf_op jit(solution)/shard_map/ppermute | solution.py:43
  141.1 8.1 %collective-permute-start.6 = (f32[64,8,128]{2,1,0:T(8,128)S(1)}, f32[64,8,128]{2,1,0:T(8,128)S(1)}, u32[]{:S(2)}, u32[]{:S(2)}) collective-permute-start(f32[64,8,128]{2,1,0:T(8,128)S(1)} %get-tuple-element.21), channel_id=1, source_target_pairs={{0,16},{16,32},{32,48},{48,112},{112,96},{96,80},{80,64},{64,1},{1... | collective-permute-start | bytes 786440 | tf_op jit(solution)/shard_map/ppermute | solution.py:42
  144.2 9.1 %collective-permute-start.7 = (f32[64,8,128]{2,1,0:T(8,128)S(1)}, f32[64,8,128]{2,1,0:T(8,128)S(1)}, u32[]{:S(2)}, u32[]{:S(2)}) collective-permute-start(f32[64,8,128]{2,1,0:T(8,128)S(1)} %get-tuple-element.22), channel_id=1, source_target_pairs={{16,0},{32,16},{48,32},{112,48},{96,112},{80,96},{64,80},{1,64},{1... | collective-permute-start | bytes 786440 | tf_op jit(solution)/shard_map/ppermute | solution.py:43
  197.2 8.3 %collective-permute-start.8 = (f32[64,8,128]{2,1,0:T(8,128)S(1)}, f32[64,8,128]{2,1,0:T(8,128)S(1)}, u32[]{:S(2)}, u32[]{:S(2)}) collective-permute-start(f32[64,8,128]{2,1,0:T(8,128)S(1)} %get-tuple-element.19), channel_id=1, source_target_pairs={{0,16},{16,32},{32,48},{48,112},{112,96},{96,80},{80,64},{64,1},{1... | collective-permute-start | bytes 786440 | tf_op jit(solution)/shard_map/ppermute | solution.py:42
  199.7 9.9 %collective-permute-start.9 = (f32[64,8,128]{2,1,0:T(8,128)S(1)}, f32[64,8,128]{2,1,0:T(8,128)S(1)}, u32[]{:S(2)}, u32[]{:S(2)}) collective-permute-start(f32[64,8,128]{2,1,0:T(8,128)S(1)} %get-tuple-element.20), channel_id=1, source_target_pairs={{16,0},{32,16},{48,32},{112,48},{96,112},{80,96},{64,80},{1,64},{1... | collective-permute-start | bytes 786440 | tf_op jit(solution)/shard_map/ppermute | solution.py:43
  228.8 7.8 %collective-permute-start.10 = (f32[64,8,128]{2,1,0:T(8,128)S(1)}, f32[64,8,128]{2,1,0:T(8,128)S(1)}, u32[]{:S(2)}, u32[]{:S(2)}) collective-permute-start(f32[64,8,128]{2,1,0:T(8,128)S(1)} %get-tuple-element.17), channel_id=1, source_target_pairs={{0,16},{16,32},{32,48},{48,112},{112,96},{96,80},{80,64},{64,1},{1... | collective-permute-start | bytes 786440 | tf_op jit(solution)/shard_map/ppermute | solution.py:42
  231.9 8.8 %collective-permute-start.11 = (f32[64,8,128]{2,1,0:T(8,128)S(1)}, f32[64,8,128]{2,1,0:T(8,128)S(1)}, u32[]{:S(2)}, u32[]{:S(2)}) collective-permute-start(f32[64,8,128]{2,1,0:T(8,128)S(1)} %get-tuple-element.18), channel_id=1, source_target_pairs={{16,0},{32,16},{48,32},{112,48},{96,112},{80,96},{64,80},{1,64},{1... | collective-permute-start | bytes 786440 | tf_op jit(solution)/shard_map/ppermute | solution.py:43

commit v8 on v7

--- a/solution.py
+++ b/solution.py
@@ -60,13 +60,10 @@
     def days(start):
         return lax.slice_in_dim(padded, start, start + length, axis=axis)
 
-    if axis == 0:
-        summed = temporal_taps[0] * field
-        for offset in range(1, BW + 1):
-            summed = summed + temporal_taps[offset] * (days(BW - offset) + days(BW + offset))
-        return summed
     lag = jnp.arange(length + 2 * BW)[None, :] - jnp.arange(length)[:, None] - BW
     band = jnp.where(jnp.abs(lag) <= BW, temporal_taps[jnp.clip(jnp.abs(lag), 0, BW)], 0.0)
+    if axis == 0:
+        return jnp.einsum("de,ec->dc", band, padded, precision=lax.Precision.HIGHEST)
     return jnp.einsum("de,rec->rdc", band, padded, precision=lax.Precision.HIGHEST)
 
 

time: 304 us -> 304 us (level)
  other arithmetic: 39 us -> 32.6 us
  matrix products: 95.2 us -> 101 us
    add x1 -> x0, other arithmetic: 6.44 us -> none  [band_product(): summed + temporal_taps[offset] * (days(BW - offset) + days(BW + offset))]
    dot_general x0 -> x1, matrix products: none -> 6.27 us  [band_product(): jnp.einsum('de,ec->dc', band, padded, precision=lax.Precision.HIGHEST)]
where the time goes in v8:
time: 304 us; the launch traced here: 303 us
  matrix products  101 us (33%)
  waiting for transfers between devices  37.8 us (12%)
  Pallas kernels  37.8 us (12%)
  local copies, waits for them, and re-layouts  36.1 us (12%)
  other arithmetic  32.6 us (11%)
  starting transfers between devices  32.5 us (11%)
  blocking collectives  19.5 us (6%)
  between operations  4.87 us (2%)
    dot_general x6, matrix products, block_product(): jnp.einsum('rkc,rdk->rdc', weights, picked, precision=lax.Precision.HIGH)  91.7 us
    pallas_call x4, Pallas kernels, group_sum(): pl.pallas_call(functools.partial(group_sum_kernel, axis), out_shape=jax.S...  37.8 us
    mul x1, other arithmetic, wendland(): return amplitude * remain ** 4 * (1.0 + 4.0 * scaled)  26.8 us
    ppermute x5, waiting for transfers between devices, day_order_halo(): high = lax.ppermute(field[:, :BW], axes, backward)  21.2 us
    all_to_all x1, blocking collectives, to_cells(): lax.all_to_all(chunked, 'space', split_axis=0, concat_axis=0, tiled=True)  19.5 us
    gather x6, local copies, waits for them, and re-layouts, block_product(): field[pattern].transpose(0, 2, 1, 3)  19.1 us
    ppermute x5, waiting for transfers between devices, day_order_halo(): low = lax.ppermute(field[:, field.shape[1] - BW:], axes, forward)  16.7 us
    ppermute x5, starting transfers between devices, day_order_halo(): low = lax.ppermute(field[:, field.shape[1] - BW:], axes, forward)  15.9 us
  transfers between devices with their start and end apart: 13, of which 10 were waited for; matrix products, arithmetic and copies ran while one was open for 13% of the time, Pallas kernels for 0%

profile of v8, /device:TPU:0, one launch (start us, length us, event | category | flops | bytes accessed | tf_op | source)
XLA Modules:
  0.0 302.6 jit_solution(1838435622938962406)
XLA Ops:
  1.5 1.3 collective-permute-start
  2.8 1.3 collective-permute-start.1
  4.8 1.6 fusion.155
  7.6 2.3 gather_fusion.2
  9.9 1.4 slice_reduce_fusion.1
  13.1 6.3 %fusion.61 = f32[128,1024]{1,0:T(8,128)S(1)} fusion(f32[8,1024]{1,0:T(8,128)S(1)} %collective-permute-done.1, f32[128,1024]{1,0:T(8,128)S(1)} %copy-done.1, f32[8,1024]{1,0:T(8,128)S(1)} %collective-permute-done, f32[]{:T(128)} %bitcast.6, f32[]{:T(128)} %bitcast.7, f32[]{:T(128)} %bitcast.8, f32[]{:T(128)} %bitcast.9, f32[]{:T(128)} %bitcast.10, ...), kind=kOutput, calls=%fused_computation.69 | convolution fusion | flops 227303424 | bytes 1114148 | tf_op jit(solution)/shard_map/de,ec->dc/dot_general | solution.py:66
  19.6 1.8 gather_fusion
  21.4 6.9 %all-to-all-start = ((f32[8,3,16,1024]{3,2,1,0:T(8,128)}), f32[8,3,16,1024]{3,2,1,0:T(8,128)S(1)}, u32[]{:S(2)}, u32[]{:S(2)}) async-start(f32[8,3,16,1024]{3,2,1,0:T(8,128)} %gather_fusion), calls=%async_computation | async-start | bytes 3145728 | tf_op jit(solution)/shard_map/all_to_all | solution.py:85
  28.3 26.8 %add_multiply_fusion = f32[64,1024,128]{2,1,0:T(8,128)} fusion(f32[64,1024]{1,0:T(8,128)S(1)} %get-tuple-element.47, f32[64,128]{1,0:T(8,128)S(1)} %bitcast.184, f32[64,1024]{1,0:T(8,128)S(1)} %get-tuple-element.48, f32[64,128]{1,0:T(8,128)S(1)} %bitcast.183), kind=kLoop, calls=%fused_computation.10 | loop fusion | flops 117440512 | bytes 34144256 | tf_op jit(solution)/shard_map/mul | solution.py:21
  55.8 3.2 %gather_fusion.1 = f32[512,16,128]{2,1,0:T(8,128)} fusion(f32[64,16,128]{2,1,0:T(8,128)S(1)} %bitcast.157, s32[1024]{0:T(1024)S(1)} %pad_clamp_fusion.1), kind=kCustom, calls=%fused_computation.1 | custom fusion | bytes 8390656 | tf_op jit(solution)/shard_map/gather | solution.py:72
  59.0 15.3 %bitcast_subtract_fusion = (f32[64,16,128]{2,1,0:T(8,128)S(1)}, f32[64,16,128]{2,1,0:T(8,128)S(1)}) fusion(f32[1,8,8,16,128]{4,3,2,1,0:T(8,128)S(1)} %get-tuple-element.7, f32[64,1024,128]{2,1,0:T(8,128)} %add_multiply_fusion, f32[64,8,2,8,128]{4,3,2,1,0:T(8,128)} %bitcast.161), kind=kOutput, calls=%fused_computation.75 | convolution fusion | flops 805437440 | bytes 39321600 | tf_op jit(solution)/shard_map/rkc,rdk->rdc/dot_general | solution.py:73
  74.4 3.8 %collective-permute-start.2 = (f32[64,8,128]{2,1,0:T(8,128)S(1)}, f32[64,8,128]{2,1,0:T(8,128)S(1)}, u32[]{:S(2)}, u32[]{:S(2)}) collective-permute-start(f32[64,8,128]{2,1,0:T(8,128)S(1)} %get-tuple-element.25), channel_id=1, source_target_pairs={{0,16},{16,32},{32,48},{48,112},{112,96},{96,80},{80,64},{64,1},{1... | collective-permute-start | bytes 786440 | tf_op jit(solution)/shard_map/ppermute | solution.py:42
  78.2 1.5 collective-permute-start.3
  79.8 3.3 %gather_fusion.3 = f32[512]{0:T(512)S(1)} fusion(f32[9]{0:T(128)S(1)} %copy-done, s32[1024]{0:T(1024)S(1)} %pad_clamp_fusion), kind=kCustom, calls=%fused_computation.3 | custom fusion | bytes 6144 | tf_op jit(solution)/shard_map/gather | solution.py:64
  84.0 4.7 %collective-permute-done.3 = f32[64,8,128]{2,1,0:T(8,128)S(1)} collective-permute-done((f32[64,8,128]{2,1,0:T(8,128)S(1)}, f32[64,8,128]{2,1,0:T(8,128)S(1)}, u32[]{:S(2)}, u32[]{:S(2)}) %collective-permute-start.3) | collective-permute-done | bytes 262176 | tf_op jit(solution)/shard_map/ppermute | solution.py:43
  89.4 3.2 %gather_fusion.4 = f32[512,16,128]{2,1,0:T(8,128)} fusion(f32[64,16,128]{2,1,0:T(8,128)S(1)} %convolution_bitcast_fusion.4, s32[1024]{0:T(1024)S(1)} %pad_clamp_fusion.1), kind=kCustom, calls=%fused_computation.4 | custom fusion | bytes 8390656 | tf_op jit(solution)/shard_map/gather | solution.py:72
  92.6 15.3 %fusion.156 = (f32[64,16,128]{2,1,0:T(8,128)S(1)}, f32[64,16,128]{2,1,0:T(8,128)S(1)}) fusion(f32[64,16,128]{2,1,0:T(8,128)S(1)} %bitcast.172, f32[64,1024,128]{2,1,0:T(8,128)} %add_multiply_fusion, f32[64,8,2,8,128]{4,3,2,1,0:T(8,128)} %bitcast.159), kind=kOutput, calls=%fused_computation.174 | convolution fusion | flops 805568512 | bytes 39321600 | tf_op jit(solution)/shard_map/rkc,rdk->rdc/dot_general | solution.py:73
  108.0 3.4 %collective-permute-start.4 = (f32[64,8,128]{2,1,0:T(8,128)S(1)}, f32[64,8,128]{2,1,0:T(8,128)S(1)}, u32[]{:S(2)}, u32[]{:S(2)}) collective-permute-start(f32[64,8,128]{2,1,0:T(8,128)S(1)} %get-tuple-element.23), channel_id=1, source_target_pairs={{0,16},{16,32},{32,48},{48,112},{112,96},{96,80},{80,64},{64,1},{1... | collective-permute-start | bytes 786440 | tf_op jit(solution)/shard_map/ppermute | solution.py:42
  111.3 1.3 collective-permute-start.5
  112.6 4.8 %collective-permute-done.4 = f32[64,8,128]{2,1,0:T(8,128)S(1)} collective-permute-done((f32[64,8,128]{2,1,0:T(8,128)S(1)}, f32[64,8,128]{2,1,0:T(8,128)S(1)}, u32[]{:S(2)}, u32[]{:S(2)}) %collective-permute-start.4) | collective-permute-done | bytes 262176 | tf_op jit(solution)/shard_map/ppermute | solution.py:42
  117.5 4.1 %collective-permute-done.5 = f32[64,8,128]{2,1,0:T(8,128)S(1)} collective-permute-done((f32[64,8,128]{2,1,0:T(8,128)S(1)}, f32[64,8,128]{2,1,0:T(8,128)S(1)}, u32[]{:S(2)}, u32[]{:S(2)}) %collective-permute-start.5) | collective-permute-done | bytes 262176 | tf_op jit(solution)/shard_map/ppermute | solution.py:43
  122.3 3.2 %gather_fusion.5 = f32[512,16,128]{2,1,0:T(8,128)} fusion(f32[64,16,128]{2,1,0:T(8,128)S(1)} %convolution_bitcast_fusion.3, s32[1024]{0:T(1024)S(1)} %pad_clamp_fusion.1), kind=kCustom, calls=%fused_computation.5 | custom fusion | bytes 8390656 | tf_op jit(solution)/shard_map/gather | solution.py:72
  125.5 15.3 %fusion.24 = f32[64,16,128]{2,1,0:T(8,128)S(1)} fusion(f32[64,16,128]{2,1,0:T(8,128)S(1)} %get-tuple-element.41, f32[64,1024,128]{2,1,0:T(8,128)} %add_multiply_fusion, f32[64,8,2,8,128]{4,3,2,1,0:T(8,128)} %bitcast.162), kind=kOutput, calls=%fused_computation.34 | convolution fusion | flops 805437440 | bytes 38797312 | tf_op jit(solution)/shard_map/rkc,rdk->rdc/dot_general | solution.py:73
  140.8 3.1 %collective-permute-start.6 = (f32[64,8,128]{2,1,0:T(8,128)S(1)}, f32[64,8,128]{2,1,0:T(8,128)S(1)}, u32[]{:S(2)}, u32[]{:S(2)}) collective-permute-start(f32[64,8,128]{2,1,0:T(8,128)S(1)} %get-tuple-element.21), channel_id=1, source_target_pairs={{0,16},{16,32},{32,48},{48,112},{112,96},{96,80},{80,64},{64,1},{1... | collective-permute-start | bytes 786440 | tf_op jit(solution)/shard_map/ppermute | solution.py:42
  143.9 1.5 collective-permute-start.7
  145.4 3.5 %collective-permute-done.6 = f32[64,8,128]{2,1,0:T(8,128)S(1)} collective-permute-done((f32[64,8,128]{2,1,0:T(8,128)S(1)}, f32[64,8,128]{2,1,0:T(8,128)S(1)}, u32[]{:S(2)}, u32[]{:S(2)}) %collective-permute-start.6) | collective-permute-done | bytes 262176 | tf_op jit(solution)/shard_map/ppermute | solution.py:42
  148.9 4.1 %collective-permute-done.7 = f32[64,8,128]{2,1,0:T(8,128)S(1)} collective-permute-done((f32[64,8,128]{2,1,0:T(8,128)S(1)}, f32[64,8,128]{2,1,0:T(8,128)S(1)}, u32[]{:S(2)}, u32[]{:S(2)}) %collective-permute-start.7) | collective-permute-done | bytes 262176 | tf_op jit(solution)/shard_map/ppermute | solution.py:43
  153.7 3.2 %gather_fusion.6 = f32[512,16,128]{2,1,0:T(8,128)} fusion(f32[64,16,128]{2,1,0:T(8,128)S(1)} %convolution_bitcast_fusion.2, s32[1024]{0:T(1024)S(1)} %pad_clamp_fusion.1), kind=kCustom, calls=%fused_computation.6 | custom fusion | bytes 8390656 | tf_op jit(solution)/shard_map/gather | solution.py:72
  156.9 15.3 %negate_multiply_fusion = (f32[64,16,128]{2,1,0:T(8,128)S(1)}, f32[64,16,128]{2,1,0:T(8,128)S(1)}, f32[64,16,128]{2,1,0:T(8,128)S(1)}, f32[64,16,128]{2,1,0:T(8,128)S(1)}) fusion(f32[64,16,128]{2,1,0:T(8,128)S(1)} %get-tuple-element.43, f32[64,1024,128]{2,1,0:T(8,128)} %add_multiply_fusion, f32[64,8,2,8,128]{4,3,2,1,0:T(8,128)} %bitcast.158), kind=kOutput, calls=%fused_computation.163 | convolution fusion | flops 805961728 | bytes 40370176 | tf_op jit(solution)/shard_map/rkc,rdk->rdc/dot_general | solution.py:73
  172.9 8.1 %shard_map.86.x_ref = f32[8,128]{1,0:T(8,128)} custom-call(f32[8,128]{1,0:T(8,128)} %pad.8.x_ref), custom_call_target="tpu_custom_call" | custom-call | tf_op jit(solution)/shard_map/pallas_call | solution.py:145
  181.0 11.0 %shard_map.87 = f32[8,128]{1,0:T(8,128)} custom-call(f32[8,128]{1,0:T(8,128)} %shard_map.86.x_ref), custom_call_target="tpu_custom_call" | custom-call | tf_op jit(solution)/shard_map/pallas_call | solution.py:145
  192.0 1.4 slice_reduce_fusion.3
  196.7 2.5 collective-permute-start.8
  199.2 1.3 collective-permute-start.9
  200.5 4.5 %collective-permute-done.8 = f32[64,8,128]{2,1,0:T(8,128)S(1)} collective-permute-done((f32[64,8,128]{2,1,0:T(8,128)S(1)}, f32[64,8,128]{2,1,0:T(8,128)S(1)}, u32[]{:S(2)}, u32[]{:S(2)}) %collective-permute-start.8) | collective-permute-done | bytes 262176 | tf_op jit(solution)/shard_map/ppermute | solution.py:42
  205.0 4.1 %collective-permute-done.9 = f32[64,8,128]{2,1,0:T(8,128)S(1)} collective-permute-done((f32[64,8,128]{2,1,0:T(8,128)S(1)}, f32[64,8,128]{2,1,0:T(8,128)S(1)}, u32[]{:S(2)}, u32[]{:S(2)}) %collective-permute-start.9) | collective-permute-done | bytes 262176 | tf_op jit(solution)/shard_map/ppermute | solution.py:43
  209.8 3.2 %gather_fusion.7 = f32[512,16,128]{2,1,0:T(8,128)} fusion(f32[64,16,128]{2,1,0:T(8,128)S(1)} %convolution_bitcast_fusion.1, s32[1024]{0:T(1024)S(1)} %pad_clamp_fusion.1), kind=kCustom, calls=%fused_computation.7 | custom fusion | bytes 8390656 | tf_op jit(solution)/shard_map/gather | solution.py:72
  213.0 15.3 %fusion.30 = f32[64,16,128]{2,1,0:T(8,128)S(1)} fusion(f32[64,16,128]{2,1,0:T(8,128)S(1)} %get-tuple-element.41, f32[64,1024,128]{2,1,0:T(8,128)} %add_multiply_fusion, f32[64,8,2,8,128]{4,3,2,1,0:T(8,128)} %bitcast.163), kind=kOutput, calls=%fused_computation.36 | convolution fusion | flops 805437440 | bytes 38797312 | tf_op jit(solution)/shard_map/rkc,rdk->rdc/dot_general | solution.py:73
  228.3 3.1 %collective-permute-start.10 = (f32[64,8,128]{2,1,0:T(8,128)S(1)}, f32[64,8,128]{2,1,0:T(8,128)S(1)}, u32[]{:S(2)}, u32[]{:S(2)}) collective-permute-start(f32[64,8,128]{2,1,0:T(8,128)S(1)} %get-tuple-element.17), channel_id=1, source_target_pairs={{0,16},{16,32},{32,48},{48,112},{112,96},{96,80},{80,64},{64,1},{1... | collective-permute-start | bytes 786440 | tf_op jit(solution)/shard_map/ppermute | solution.py:42
  231.4 1.6 collective-permute-start.11
  233.0 3.1 %collective-permute-done.10 = f32[64,8,128]{2,1,0:T(8,128)S(1)} collective-permute-done((f32[64,8,128]{2,1,0:T(8,128)S(1)}, f32[64,8,128]{2,1,0:T(8,128)S(1)}, u32[]{:S(2)}, u32[]{:S(2)}) %collective-permute-start.10) | collective-permute-done | bytes 262176 | tf_op jit(solution)/shard_map/ppermute | solution.py:42
  236.1 4.1 %collective-permute-done.11 = f32[64,8,128]{2,1,0:T(8,128)S(1)} collective-permute-done((f32[64,8,128]{2,1,0:T(8,128)S(1)}, f32[64,8,128]{2,1,0:T(8,128)S(1)}, u32[]{:S(2)}, u32[]{:S(2)}) %collective-permute-start.11) | collective-permute-done | bytes 262176 | tf_op jit(solution)/shard_map/ppermute | solution.py:43
  240.9 3.2 %gather_fusion.8 = f32[512,16,128]{2,1,0:T(8,128)} fusion(f32[64,16,128]{2,1,0:T(8,128)S(1)} %convolution_bitcast_fusion, s32[1024]{0:T(1024)S(1)} %pad_clamp_fusion.1), kind=kCustom, calls=%fused_computation.8 | custom fusion | bytes 8390656 | tf_op jit(solution)/shard_map/gather | solution.py:72
  244.1 15.3 %multiply_reduce_fusion = (f32[128]{0:T(128)S(1)}, f32[64,16,128]{2,1,0:T(8,128)S(1)}) fusion(f32[64,16,128]{2,1,0:T(8,128)S(1)} %multiply_add_fusion.1, f32[64,1024,128]{2,1,0:T(8,128)} %add_multiply_fusion, f32[64,8,2,8,128]{4,3,2,1,0:T(8,128)} %bitcast.160), kind=kOutput, calls=%fused_computation.78 | convolution fusion | flops 805699456 | bytes 38797824 | tf_op jit(solution)/shard_map/rkc,rdk->rdc/dot_general | solution.py:73
  260.0 8.3 %shard_map.88.x_ref = f32[8,128]{1,0:T(8,128)} custom-call(f32[8,128]{1,0:T(8,128)} %pad.9.x_ref), custom_call_target="tpu_custom_call" | custom-call | tf_op jit(solution)/shard_map/pallas_call | solution.py:145
  268.3 10.4 %shard_map.89 = f32[8,128]{1,0:T(8,128)} custom-call(f32[8,128]{1,0:T(8,128)} %shard_map.88.x_ref), custom_call_target="tpu_custom_call" | custom-call | tf_op jit(solution)/shard_map/pallas_call | solution.py:145
  278.7 1.3 slice_reduce_fusion.2
  281.5 19.5 %all_to_all.10 = f32[8,2,16,1024]{3,2,1,0:T(8,128)S(1)} all-to-all(f32[8,2,16,1024]{3,2,1,0:T(8,128)S(1)} %reshape.156), channel_id=1, replica_groups=mesh['space'=8,'tm'=16] {'space'}, dimensions={0} | all-to-all | bytes 2097152 | tf_op jit(solution)/shard_map/all_to_all | solution.py:96
  (46 shorter events, 13.8 us)
Async XLA Ops:
  0.6 12.5 %copy-start.1 = (f32[128,1024]{1,0:T(8,128)S(1)}, f32[128,1024]{1,0:T(8,128)}, u32[]{:S(2)}) copy-start(f32[128,1024]{1,0:T(8,128)} %param.7) | copy-start | bytes 1572868
  1.5 11.6 %collective-permute-start = (f32[8,1024]{1,0:T(8,128)S(1)}, f32[8,1024]{1,0:T(8,128)S(1)}, u32[]{:S(2)}, u32[]{:S(2)}) collective-permute-start(f32[8,1024]{1,0:T(8,128)S(1)} %get-tuple-element.27), channel_id=1, source_target_pairs={{0,1},{1,2},{2,3},{3,4},{4,5},{5,6},{6,7},{7,8},{8,9},{9,10},{10,1... | collective-permute-start | bytes 98312 | tf_op jit(solution)/shard_map/ppermute | solution.py:51
  2.8 10.4 %collective-permute-start.1 = (f32[8,1024]{1,0:T(8,128)S(1)}, f32[8,1024]{1,0:T(8,128)S(1)}, u32[]{:S(2)}, u32[]{:S(2)}) collective-permute-start(f32[8,1024]{1,0:T(8,128)S(1)} %get-tuple-element.28), channel_id=1, source_target_pairs={{1,0},{2,1},{3,2},{4,3},{5,4},{6,5},{7,6},{8,7},{9,8},{10,9},{11,1... | collective-permute-start | bytes 98312 | tf_op jit(solution)/shard_map/ppermute | solution.py:52
  21.4 33.7 %all-to-all-start = ((f32[8,3,16,1024]{3,2,1,0:T(8,128)}), f32[8,3,16,1024]{3,2,1,0:T(8,128)S(1)}, u32[]{:S(2)}, u32[]{:S(2)}) async-start(f32[8,3,16,1024]{3,2,1,0:T(8,128)} %gather_fusion), calls=%async_computation | async-start | bytes 3145728 | tf_op jit(solution)/shard_map/all_to_all | solution.py:85
  74.3 5.5 %copy-start = (f32[9]{0:T(128)S(1)}, f32[9]{0:T(128)}, u32[]{:S(2)}) copy-start(f32[9]{0:T(128)} %param.11) | copy-start | bytes 112
  74.4 9.6 %collective-permute-start.2 = (f32[64,8,128]{2,1,0:T(8,128)S(1)}, f32[64,8,128]{2,1,0:T(8,128)S(1)}, u32[]{:S(2)}, u32[]{:S(2)}) collective-permute-start(f32[64,8,128]{2,1,0:T(8,128)S(1)} %get-tuple-element.25), channel_id=1, source_target_pairs={{0,16},{16,32},{32,48},{48,112},{112,96},{96,80},{80,64},{64,1},{1... | collective-permute-start | bytes 786440 | tf_op jit(solution)/shard_map/ppermute | solution.py:42
  78.2 10.5 %collective-permute-start.3 = (f32[64,8,128]{2,1,0:T(8,128)S(1)}, f32[64,8,128]{2,1,0:T(8,128)S(1)}, u32[]{:S(2)}, u32[]{:S(2)}) collective-permute-start(f32[64,8,128]{2,1,0:T(8,128)S(1)} %get-tuple-element.26), channel_id=1, source_target_pairs={{16,0},{32,16},{48,32},{112,48},{96,112},{80,96},{64,80},{1,64},{1... | collective-permute-start | bytes 786440 | tf_op jit(solution)/shard_map/ppermute | solution.py:43
  108.0 9.5 %collective-permute-start.4 = (f32[64,8,128]{2,1,0:T(8,128)S(1)}, f32[64,8,128]{2,1,0:T(8,128)S(1)}, u32[]{:S(2)}, u32[]{:S(2)}) collective-permute-start(f32[64,8,128]{2,1,0:T(8,128)S(1)} %get-tuple-element.23), channel_id=1, source_target_pairs={{0,16},{16,32},{32,48},{48,112},{112,96},{96,80},{80,64},{64,1},{1... | collective-permute-start | bytes 786440 | tf_op jit(solution)/shard_map/ppermute | solution.py:42
  111.3 10.2 %collective-permute-start.5 = (f32[64,8,128]{2,1,0:T(8,128)S(1)}, f32[64,8,128]{2,1,0:T(8,128)S(1)}, u32[]{:S(2)}, u32[]{:S(2)}) collective-permute-start(f32[64,8,128]{2,1,0:T(8,128)S(1)} %get-tuple-element.24), channel_id=1, source_target_pairs={{16,0},{32,16},{48,32},{112,48},{96,112},{80,96},{64,80},{1,64},{1... | collective-permute-start | bytes 786440 | tf_op jit(solution)/shard_map/ppermute | solution.py:43
  140.8 8.1 %collective-permute-start.6 = (f32[64,8,128]{2,1,0:T(8,128)S(1)}, f32[64,8,128]{2,1,0:T(8,128)S(1)}, u32[]{:S(2)}, u32[]{:S(2)}) collective-permute-start(f32[64,8,128]{2,1,0:T(8,128)S(1)} %get-tuple-element.21), channel_id=1, source_target_pairs={{0,16},{16,32},{32,48},{48,112},{112,96},{96,80},{80,64},{64,1},{1... | collective-permute-start | bytes 786440 | tf_op jit(solution)/shard_map/ppermute | solution.py:42
  143.9 9.1 %collective-permute-start.7 = (f32[64,8,128]{2,1,0:T(8,128)S(1)}, f32[64,8,128]{2,1,0:T(8,128)S(1)}, u32[]{:S(2)}, u32[]{:S(2)}) collective-permute-start(f32[64,8,128]{2,1,0:T(8,128)S(1)} %get-tuple-element.22), channel_id=1, source_target_pairs={{16,0},{32,16},{48,32},{112,48},{96,112},{80,96},{64,80},{1,64},{1... | collective-permute-start | bytes 786440 | tf_op jit(solution)/shard_map/ppermute | solution.py:43
  196.7 8.3 %collective-permute-start.8 = (f32[64,8,128]{2,1,0:T(8,128)S(1)}, f32[64,8,128]{2,1,0:T(8,128)S(1)}, u32[]{:S(2)}, u32[]{:S(2)}) collective-permute-start(f32[64,8,128]{2,1,0:T(8,128)S(1)} %get-tuple-element.19), channel_id=1, source_target_pairs={{0,16},{16,32},{32,48},{48,112},{112,96},{96,80},{80,64},{64,1},{1... | collective-permute-start | bytes 786440 | tf_op jit(solution)/shard_map/ppermute | solution.py:42
  199.2 9.9 %collective-permute-start.9 = (f32[64,8,128]{2,1,0:T(8,128)S(1)}, f32[64,8,128]{2,1,0:T(8,128)S(1)}, u32[]{:S(2)}, u32[]{:S(2)}) collective-permute-start(f32[64,8,128]{2,1,0:T(8,128)S(1)} %get-tuple-element.20), channel_id=1, source_target_pairs={{16,0},{32,16},{48,32},{112,48},{96,112},{80,96},{64,80},{1,64},{1... | collective-permute-start | bytes 786440 | tf_op jit(solution)/shard_map/ppermute | solution.py:43
  228.3 7.8 %collective-permute-start.10 = (f32[64,8,128]{2,1,0:T(8,128)S(1)}, f32[64,8,128]{2,1,0:T(8,128)S(1)}, u32[]{:S(2)}, u32[]{:S(2)}) collective-permute-start(f32[64,8,128]{2,1,0:T(8,128)S(1)} %get-tuple-element.17), channel_id=1, source_target_pairs={{0,16},{16,32},{32,48},{48,112},{112,96},{96,80},{80,64},{64,1},{1... | collective-permute-start | bytes 786440 | tf_op jit(solution)/shard_map/ppermute | solution.py:42
  231.4 8.8 %collective-permute-start.11 = (f32[64,8,128]{2,1,0:T(8,128)S(1)}, f32[64,8,128]{2,1,0:T(8,128)S(1)}, u32[]{:S(2)}, u32[]{:S(2)}) collective-permute-start(f32[64,8,128]{2,1,0:T(8,128)S(1)} %get-tuple-element.18), channel_id=1, source_target_pairs={{16,0},{32,16},{48,32},{112,48},{96,112},{80,96},{64,80},{1,64},{1... | collective-permute-start | bytes 786440 | tf_op jit(solution)/shard_map/ppermute | solution.py:43
